TPU v7x, 32 devices: a whole 2x2x4 slice. The times are simulated.
32 devices in a mesh: blk: 8 (over y, x, core), chan: 4 (over z).
Axes of the slice: x: 2, y: 2, z: 4, core: 2. Of those that a mesh axis runs over, the one named last changes fastest.
Arguments:
- positions: float32 [3, 1024], P(None, 'blk'), may hold values from 0 to 48, as said below
- species: int32 [1024], P('blk'), may hold values from 0 to 1
- node_features: float32 [64, 1024], P('chan', 'blk'), may hold values from -6 to 6
- block_mask: int32 [8, 7], P('blk'), may hold values from 0 to 1, as said below
- radial_weight: float32 [8, 64], P(None, 'chan'), may hold values from -2 to 2
- species_embed: float32 [64, 2], P('chan'), may hold values from 0.25 to 1.75
- center_embed: float32 [64, 2], P('chan'), may hold values from 0.25 to 1.75
- mix_weight: float32 [3, 64, 64], replicated, may hold values from -0.75 to 0.75
Outputs:
- descriptors: float32 [3, 64, 1024], P(None, 'chan', 'blk')
Inputs may be any that keep to these rules, and one draw needn't show every extreme that they name: `positions`: atom g lies in slab s = g // 128: its first coordinate in [s * 5 / 3, (s + 1) * 5 / 3), the other two in [0, 48). An arbitrary set of kept slab pairs, symmetric between the two slabs of a pair: block_mask[i, 3 + k] equals block_mask[(i + k) mod 8, 3 - k]; the middle column is 1.
All inputs are finite; a program needn't handle non-finite values.
Results may differ from a plain program's by a relative error of at most 0.0035.
Values sent between devices are 32-bit elements; how exact they have to be, the bound alone decides.
No kernel may reach another device: no remote copies, remote signals or barrier semaphores. Data moves between devices by JAX's collectives and lax.ppermute only.
A program may use at most 64 MiB of HBM per device.

v0:
```python
import math

import jax
import jax.numpy as jnp
from jax import lax
from jax.experimental import pallas as pl
from jax.experimental.pallas import tpu as pltpu
from jax.sharding import PartitionSpec as P

slab_width = 5.0 / 3.0
cross_width = 48.0
cut_radius = 5.0
soften = 0.25
components = 9
orders = ((0, 1), (1, 4), (4, 9))
lanes = 128
tile = 16

cos_terms = (
    -0.6056998671923182,
    -0.8837930130905377,
    0.5945743675766054,
    -0.11556393696983189,
    0.011100594647768918,
    -0.0006430391121701238,
    2.490485442655993e-05,
)
sinc_terms = (
    0.22505602342469963,
    -0.30281424022132397,
    0.08828480791644601,
    -0.011306965460218523,
    0.0008171987621448651,
    -3.805921488925154e-05,
    1.2352514278347018e-06,
)


def horner(terms, v):
    value = jnp.full_like(v, terms[-1])
    for term in terms[-2::-1]:
        value = value * v + term
    return value


def pair_rows(own, other, box_x, count, apart):
    shift = []
    for axis, length in enumerate((box_x, cross_width, cross_width)):
        r = other[axis] - own[axis]
        shift.append(r - length * jnp.floor(r * (1.0 / length) + 0.5))
    x, y, z = shift
    xx, yy, zz = x * x, y * y, z * z
    s = xx + yy + zz + soften
    inverse = lax.rsqrt(s)
    d = s * inverse
    scaled = d * (1.0 / cut_radius)
    square = s * (1.0 / cut_radius**2)
    sixth = square * square * square
    envelope = 1.0 + sixth * (scaled * 48.0 - 28.0 - 21.0 * square)
    keep = s < cut_radius**2
    if apart is not None:
        keep = jnp.logical_and(keep, apart)
    v = s * (2.0 / cut_radius**2) - 1.0
    first = jnp.where(keep, envelope * math.sqrt(2.0 / cut_radius), 0.0) * horner(sinc_terms, v)
    twice = 2.0 * horner(cos_terms, v)
    radial = [first, twice * first]
    while len(radial) < count:
        radial.append(twice * radial[-1] - radial[-2])
    root3, root15 = math.sqrt(3.0), math.sqrt(15.0)
    over = inverse * inverse
    s15 = root15 * over
    over3 = root3 * inverse
    harmonics = [
        None,
        x * over3,
        y * over3,
        z * over3,
        x * y * s15,
        y * z * s15,
        (2.0 * zz - xx - yy) * (0.5 * math.sqrt(5.0) * over),
        x * z * s15,
        (xx - yy) * (0.5 * s15),
    ]
    return [[r if h is None else r * h for h in harmonics] for r in radial[:count]]


def pair_kernel(slabs, data_count, own_slab, first, last, box_x, count, *refs):
    refs = list(refs)
    pos_ref, act_ref, par_ref = refs[:3]
    data = refs[3 : 3 + data_count]
    rest = refs[3 + data_count :]
    if not first:
        acc_ref = rest.pop(0)
    if last:
        mix_ref = rest.pop(0)
    out_ref, table_ref, weight_ref, sum_ref = rest
    channels = par_ref.shape[0]
    own = [jnp.broadcast_to(pos_ref[axis : axis + 1, :], (tile, lanes)) for axis in range(3)]
    for place, (which, base, index) in enumerate(slabs):
        ref = data[which]
        feats = ref[base : base + channels, :] * act_ref[index : index + 1, :]
        columns = ref[base + channels : base + channels + 8, :].T
        for n in range(count):
            weight_ref[:, n * lanes : (n + 1) * lanes] = (par_ref[:, n : n + 1] * feats).astype(
                jnp.bfloat16
            )
        for step in range(lanes // tile):
            rows = slice(step * tile, (step + 1) * tile)
            other = [
                jnp.broadcast_to(columns[rows, axis : axis + 1], (tile, lanes)) for axis in range(3)
            ]
            apart = None
            if index == own_slab:
                apart = (
                    lax.broadcasted_iota(jnp.int32, (tile, lanes), 0) + step * tile
                ) != lax.broadcasted_iota(jnp.int32, (tile, lanes), 1)
            table = pair_rows(own, other, box_x, count, apart)
            for n in range(count):
                for m in range(components):
                    table_ref[
                        n * lanes + step * tile : n * lanes + (step + 1) * tile,
                        m * lanes : (m + 1) * lanes,
                    ] = table[n][m].astype(jnp.bfloat16)
        part = jnp.dot(weight_ref[...], table_ref[...], preferred_element_type=jnp.float32)
        target = out_ref if not last else sum_ref
        if place == 0:
            target[...] = part if first else acc_ref[...] + part
        else:
            target[...] += part
    if not last:
        return
    kinds = par_ref.shape[1] - count
    centre = jnp.zeros((channels, lanes), jnp.float32)
    for kind in range(kinds):
        here = pos_ref[3:4, :] == float(kind)
        centre = jnp.where(here, par_ref[:, count + kind : count + kind + 1], centre)
    for order, (start, stop) in enumerate(orders):
        mix = mix_ref[order]
        mix_high = mix.astype(jnp.bfloat16)
        mix_low = (mix - mix_high.astype(jnp.float32)).astype(jnp.bfloat16)
        total = None
        for m in range(start, stop):
            features = sum_ref[:, m * lanes : (m + 1) * lanes] * centre
            high = features.astype(jnp.bfloat16)
            low = (features - high.astype(jnp.float32)).astype(jnp.bfloat16)
            mixed = (
                jnp.dot(mix_high, high, preferred_element_type=jnp.float32)
                + jnp.dot(mix_high, low, preferred_element_type=jnp.float32)
                + jnp.dot(mix_low, high, preferred_element_type=jnp.float32)
            )
            total = mixed * mixed if total is None else total + mixed * mixed
        out_ref[order] = jnp.log1p(total)


def accumulate(name, pos, act, par, data, slabs, own_slab, box_x, count, acc=None, mix=None):
    channels, atoms = par.shape[0], pos.shape[1]
    operands = [pos, act, par, *data]
    if acc is not None:
        operands.append(acc)
    if mix is not None:
        operands.append(mix)
    wide = (channels, components * atoms)
    shape = wide if mix is None else (mix.shape[0], mix.shape[1], atoms)
    flops = 2 * channels * count * components * atoms * atoms * len(slabs)

    def body(*refs):
        pair_kernel(
            slabs, len(data), own_slab, acc is None, mix is not None, box_x, count, *refs
        )

    return pl.pallas_call(
        body,
        out_shape=jax.ShapeDtypeStruct(shape, jnp.float32),
        in_specs=[pl.BlockSpec(memory_space=pltpu.VMEM)] * len(operands),
        out_specs=pl.BlockSpec(memory_space=pltpu.VMEM),
        scratch_shapes=[
            pltpu.VMEM((count * atoms, components * atoms), jnp.bfloat16),
            pltpu.VMEM((channels, count * atoms), jnp.bfloat16),
            pltpu.VMEM(wide if mix is not None else (8, lanes), jnp.float32),
        ],
        cost_estimate=pl.CostEstimate(flops=flops, bytes_accessed=1 << 20, transcendentals=0),
        name=name,
    )(*operands)


def moved(value, axis, target):
    size = lax.axis_size(axis)
    return lax.ppermute(value, axis, [(i, target(i, size)) for i in range(size)])


def flipped(value, axis, bit):
    return moved(value, axis, lambda i, size: i ^ bit)


def shards(
    positions,
    species,
    node_features,
    block_mask,
    radial_weight,
    species_embed,
    center_embed,
    mix_weight,
):
    slab_count = lax.axis_size("blk")
    owner_count = lax.axis_size("chan")
    box_x = float(slab_count) * slab_width
    reach = (block_mask.shape[1] - 1) // 2
    count = radial_weight.shape[0]
    kinds = species_embed.shape[1]
    held, atoms = node_features.shape
    me = lax.axis_index("blk")
    owner = lax.axis_index("chan")

    embedded = jnp.zeros((held, atoms), jnp.float32)
    for kind in range(kinds):
        embedded = jnp.where(species[None, :] == kind, species_embed[:, kind : kind + 1], embedded)
    rows = jnp.concatenate([radial_weight, center_embed.T], axis=0)
    rows = jnp.pad(rows, ((0, tile - count - kinds), (0, atoms - held)))
    owned = jnp.concatenate([node_features * embedded, rows], axis=0)[None]
    bit = owner_count // 2
    flips = [0]
    while bit:
        owned = jnp.concatenate([owned, flipped(owned, "chan", bit)], axis=0)
        flips = flips + [f ^ bit for f in flips]
        bit //= 2
    channels = held * owner_count
    feats = owned[:, :held].reshape(channels, atoms)
    par = owned[:, held : held + count + kinds, :held].transpose(0, 2, 1)
    par = par.reshape(channels, count + kinds)
    mine = lax.dynamic_slice_in_dim(mix_weight, owner * held, held, 1)
    mix = jnp.concatenate(
        [lax.dynamic_slice_in_dim(mine, (owner ^ f) * held, held, 2) for f in flips], axis=2
    )

    pos = jnp.concatenate(
        [positions, species[None].astype(jnp.float32), jnp.zeros((4, atoms), jnp.float32)], axis=0
    )
    bundle = jnp.concatenate([feats, pos], axis=0)
    depth = bundle.shape[0]

    def activity(places):
        offset = jnp.stack([lax.rem(p - me + reach + slab_count, slab_count) for p in places])
        at = offset[:, None] == jnp.arange(2 * reach + 1, dtype=jnp.int32)[None, :]
        value = jnp.sum(jnp.where(at, block_mask, 0), axis=1).astype(jnp.float32)
        return jnp.broadcast_to(value[:, None], (len(places), atoms))

    call = lambda name, act, data, slabs, acc=None, mix=None: accumulate(
        name, pos, act, par, data, slabs, 0, box_x, count, acc, mix
    )
    if slab_count == 2 * (reach + 1) == 8:
        act = activity([me ^ j for j in range(slab_count)])
        two = flipped(bundle, "blk", 2)
        pair = jnp.concatenate([bundle, two], axis=0)
        four = flipped(pair, "blk", 4)
        acc = call("near", act, [bundle, two], [(0, 0, 0), (1, 0, 2)])
        quad = jnp.concatenate([pair, four], axis=0)
        one = flipped(quad, "blk", 1)
        acc = call("middle", act, [four], [(0, depth, 6)], acc)
        return call("far", act, [one], [(0, j // 2 * depth, j) for j in (1, 3, 5, 7)], acc, mix)
    places = [0] + [k for h in range(1, reach + 1) for k in (h, -h)]
    act = activity([lax.rem(me + k + slab_count, slab_count) for k in places])
    act = jnp.pad(act, ((0, 8 - len(places)), (0, 0)))
    data = [bundle] + [
        moved(bundle, "blk", lambda i, size, k=k: (i - k) % size) for k in places[1:]
    ]
    return call("all", act, data, [(j, 0, j) for j in range(len(places))], None, mix)


def solution(mesh):
    return jax.shard_map(
        shards,
        mesh=mesh,
        in_specs=(
            P(None, "blk"),
            P("blk"),
            P("chan", "blk"),
            P("blk", None),
            P(None, "chan"),
            P("chan", None),
            P("chan", None),
            P(),
        ),
        out_specs=P(None, "chan", "blk"),
        check_vma=False,
    )
```

profile of v0, /device:TPU:0, one launch (start us, length us, event | category | flops | bytes accessed | tf_op | source)
XLA Modules:
  0.0 34.8 jit_solution(6955820647319321024)
XLA Ops:
  0.0 0.0 copy-start.7
  0.0 0.0 copy-start.5
  0.0 0.0 copy-start.2
  0.0 0.8 %slice_bitcast_fusion.2 = (f32[16]{0:T(128)S(1)}, f32[16]{0:T(128)S(1)}) fusion(f32[16,2]{0,1:T(2,128)} %param.13), kind=kLoop, calls=%fused_computation.18 | loop fusion | bytes 256 | tf_op jit(solution)/shard_map/jit(_where)/broadcast_in_dim | solution.py:217
  0.8 0.0 copy-done.7
  0.8 0.0 copy-done.5
  0.8 0.8 %select_maximum_fusion = (f32[16,128]{1,0:T(8,128)S(1)}, f32[16,128]{1,0:T(8,128)S(1)}) fusion(f32[2,16]{1,0:T(2,128)} %bitcast.27, f32[8,16]{1,0:T(8,128)} %param.12, f32[16,128]{1,0:T(8,128)S(1)} %copy-done.5, f32[16]{0:T(128)S(1)} %get-tuple-element.10, pred[128]{0:T(512)(128)(4,1)S(1)} %get-tuple-element.12, f32[16]{0:T(128)S(1)} %get-tuple-element.9, ...), kind=kLoop, calls=%fused_computation.6 | loop fusion | flops 22528 | bytes 25600 | tf_op jit(solution)/shard_map/concatenate | solution.py:218
  1.6 4.1 %collective-permute-start = (f32[1,32,128]{2,1,0:T(8,128)S(1)}, f32[1,32,128]{2,1,0:T(8,128)S(1)}, u32[]{:S(2)}, u32[]{:S(2)}) collective-permute-start(f32[1,32,128]{2,1,0:T(8,128)S(1)} %maximum_bitcast_fusion), channel_id=1, source_target_pairs={{0,2},{1,3},{2,0},{3,1},{4,6},{5,7},{6,4},{7,5},{8,10},{9,11},{10,... | collective-permute-start | bytes 49160 | tf_op jit(solution)/shard_map/ppermute | solution.py:188
  5.7 0.0 copy-done.2
  5.7 0.1 constant_dynamic-slice_fusion.2
  5.9 0.1 stack.31
  5.9 1.5 %collective-permute-done = f32[1,32,128]{2,1,0:T(8,128)S(1)} collective-permute-done((f32[1,32,128]{2,1,0:T(8,128)S(1)}, f32[1,32,128]{2,1,0:T(8,128)S(1)}, u32[]{:S(2)}, u32[]{:S(2)}) %collective-permute-start) | collective-permute-done | bytes 16416 | tf_op jit(solution)/shard_map/ppermute | solution.py:188
  7.4 0.0 copy-start.8
  7.4 1.9 %collective-permute-start.1 = (f32[2,32,128]{2,1,0:T(8,128)S(1)}, f32[2,32,128]{2,1,0:T(8,128)S(1)}, u32[]{:S(2)}, u32[]{:S(2)}) collective-permute-start(f32[2,32,128]{2,1,0:T(8,128)S(1)} %pad_maximum_fusion.2), channel_id=1, source_target_pairs={{0,1},{1,0},{2,3},{3,2},{4,5},{5,4},{6,7},{7,6},{8,9},{9,8},{10,11... | collective-permute-start | bytes 98312 | tf_op jit(solution)/shard_map/ppermute | solution.py:188
  9.3 0.0 copy-done.8
  9.3 0.2 select_reduce_fusion
  9.5 1.8 %collective-permute-done.1 = f32[2,32,128]{2,1,0:T(8,128)S(1)} collective-permute-done((f32[2,32,128]{2,1,0:T(8,128)S(1)}, f32[2,32,128]{2,1,0:T(8,128)S(1)}, u32[]{:S(2)}, u32[]{:S(2)}) %collective-permute-start.1) | collective-permute-done | bytes 32800 | tf_op jit(solution)/shard_map/ppermute | solution.py:188
  11.3 0.0 copy-start.4
  11.3 0.7 %copy-done.4 = f32[3,128]{1,0:T(4,128)S(1)} copy-done((f32[3,128]{1,0:T(4,128)S(1)}, f32[3,128]{1,0:T(4,128)}, u32[]{:S(2)}) %copy-start.4) | copy-done | bytes 1560
  12.0 0.0 copy-start.3
  12.0 1.9 %collective-permute-start.2 = (f32[72,128]{1,0:T(8,128)S(1)}, f32[72,128]{1,0:T(8,128)S(1)}, u32[]{:S(2)}, u32[]{:S(2)}) collective-permute-start(f32[72,128]{1,0:T(8,128)S(1)} %pad_maximum_fusion.1.refs_3_), channel_id=1, source_target_pairs={{0,8},{4,12},{8,0},{12,4},{16,24},{20,28},{24,16},{28,20},{1,9},{5... | collective-permute-start | bytes 110600 | tf_op jit(solution)/shard_map/ppermute | solution.py:188
  14.0 0.7 %pad_maximum_fusion.3.refs_5_ = f32[3,16,64]{2,1,0:T(8,128)} fusion(f32[3,16,16]{2,1,0:T(8,128)S(1)} %get-tuple-element.7, f32[3,16,16]{2,1,0:T(8,128)S(1)} %get-tuple-element.8, f32[3,16,16]{2,1,0:T(8,128)S(1)} %get-tuple-element.6, f32[3,16,16]{2,1,0:T(8,128)S(1)} %get-tuple-element.5), kind=kLoop, calls=%fused_computation.4 | loop fusion | flops 9216 | bytes 24576 | tf_op jit(solution)/shard_map/concatenate | solution.py:232
  14.7 0.0 copy-done.3
  14.7 1.4 %collective-permute-done.2.refs_4_ = f32[72,128]{1,0:T(8,128)S(1)} collective-permute-done((f32[72,128]{1,0:T(8,128)S(1)}, f32[72,128]{1,0:T(8,128)S(1)}, u32[]{:S(2)}, u32[]{:S(2)}) %collective-permute-start.2) | collective-permute-done | bytes 36896 | tf_op jit(solution)/shard_map/ppermute | solution.py:188
  16.1 0.0 copy-start.1
  16.1 2.0 %collective-permute-start.3 = (f32[144,128]{1,0:T(8,128)S(1)}, f32[144,128]{1,0:T(8,128)S(1)}, u32[]{:S(2)}, u32[]{:S(2)}) collective-permute-start(f32[144,128]{1,0:T(8,128)S(1)} %concatenate.37), channel_id=1, source_target_pairs={{0,16},{4,20},{8,24},{12,28},{16,0},{20,4},{24,8},{28,12},{1,17},{... | collective-permute-start | bytes 221192 | tf_op jit(solution)/shard_map/ppermute | solution.py:188
  18.0 0.6 %pad_maximum_fusion.4.refs_0_ = f32[8,128]{1,0:T(8,128)} fusion(f32[4,128]{1,0:T(4,128)S(1)} %broadcast_in_dim.64, f32[1,128]{1,0:T(1,128)S(1)} %convert_bitcast_fusion, f32[3,128]{1,0:T(4,128)S(1)} %copy-done.4), kind=kLoop, calls=%fused_computation.10 | loop fusion | flops 2048 | bytes 8192 | tf_op jit(solution)/shard_map/concatenate | solution.py:236
  18.6 1.9 %collective-permute-done.3.refs_3_ = f32[144,128]{1,0:T(8,128)S(1)} collective-permute-done((f32[144,128]{1,0:T(8,128)S(1)}, f32[144,128]{1,0:T(8,128)S(1)}, u32[]{:S(2)}, u32[]{:S(2)}) %collective-permute-start.3) | collective-permute-done | bytes 73760 | tf_op jit(solution)/shard_map/ppermute | solution.py:188
  20.5 0.0 copy-done.1
  20.5 0.0 copy-start
  20.5 0.6 %copy-done = f32[144,128]{1,0:T(8,128)} copy-done((f32[144,128]{1,0:T(8,128)}, f32[144,128]{1,0:T(8,128)S(1)}, u32[]{:S(2)}) %copy-start) | copy-done | bytes 73752
  21.1 0.0 collective-permute-start.4
  21.1 0.7 %copy.10 = f32[4,16,10]{2,1,0:T(8,128)} copy(f32[4,16,10]{1,2,0:T(8,128)S(1)} %slice_bitcast_fusion) | data formatting | bytes 5120 | tf_op jit(solution)/shard_map/transpose | solution.py:229
  21.9 0.7 %broadcast_in_dim.68.refs_1_ = f32[8,128]{1,0:T(8,128)} broadcast(f32[8]{0:T(128)S(1)} %convert_element_type.17), dimensions={0} | broadcast | bytes 4128 | tf_op jit(solution)/shard_map/broadcast_in_dim | solution.py:246
  22.5 3.5 %near.1.refs_4_ = f32[64,1152]{1,0:T(8,128)} custom-call(f32[8,128]{1,0:T(8,128)} %pad_maximum_fusion.4.refs_0_, f32[8,128]{1,0:T(8,128)} %broadcast_in_dim.68.refs_1_, f32[64,10]{1,0:T(8,128)} %bitcast.24, f32[72,128]{1,0:T(8,128)} %copy-done.3, f32[72,128]{1,0:T(8,128)} %copy-done.1), custom_call_target="tpu_custom_call" | custom-call | flops 301989888 | bytes 1048576 | tf_op jit(solution)/shard_map/near/pallas_call | solution.py:171
  26.1 2.9 %middle.1.refs_4_ = f32[64,1152]{1,0:T(8,128)} custom-call(f32[8,128]{1,0:T(8,128)} %pad_maximum_fusion.4.refs_0_, f32[8,128]{1,0:T(8,128)} %broadcast_in_dim.68.refs_1_, f32[64,10]{1,0:T(8,128)} %bitcast.25, f32[144,128]{1,0:T(8,128)} %copy-done, f32[64,1152]{1,0:T(8,128)} %near.1.refs_4_), custom_call_target="tpu_custom_call" | custom-call | flops 150994944 | bytes 1048576 | tf_op jit(solution)/shard_map/middle/pallas_call | solution.py:171
  28.9 0.0 collective-permute-done.4.refs_3_
  28.9 0.0 copy-start.6
  28.9 0.7 %copy-done.6 = f32[288,128]{1,0:T(8,128)} copy-done((f32[288,128]{1,0:T(8,128)}, f32[288,128]{1,0:T(8,128)S(1)}, u32[]{:S(2)}) %copy-start.6) | copy-done | bytes 147480
  29.6 5.3 %far.1 = f32[3,16,128]{2,1,0:T(8,128)} custom-call(f32[8,128]{1,0:T(8,128)} %pad_maximum_fusion.4.refs_0_, f32[8,128]{1,0:T(8,128)} %broadcast_in_dim.68.refs_1_, f32[64,10]{1,0:T(8,128)} %bitcast.26, f32[288,128]{1,0:T(8,128)} %copy-done.6, f32[64,1152]{1,0:T(8,128)} %middle.1.refs_4_, f32[3,16,64]{2,1,0:T(8,128)} %pad_maximum_fusion.3.refs_5_), custom_call_target="tpu_custom_call" | custom-call | flops 603979776 | bytes 1048576 | tf_op jit(solution)/shard_map/far/pallas_call | solution.py:171
  (12 shorter events, 0.1 us)
Async XLA Ops:
  0.0 0.8 %copy-start.7 = (s32[128]{0:T(128)S(1)}, s32[128]{0:T(128)}, u32[]{:S(2)}) copy-start(s32[128]{0:T(128)} %param.9) | copy-start | bytes 1540
  0.0 0.8 %copy-start.5 = (f32[16,128]{1,0:T(8,128)S(1)}, f32[16,128]{1,0:T(8,128)}, u32[]{:S(2)}) copy-start(f32[16,128]{1,0:T(8,128)} %param.10) | copy-start | bytes 24580
  0.0 5.7 %copy-start.2 = (f32[3,64,64]{2,1,0:T(8,128)S(1)}, f32[3,64,64]{2,1,0:T(8,128)}, u32[]{:S(2)}) copy-start(f32[3,64,64]{2,1,0:T(8,128)} %param.15) | copy-start | bytes 147460
  1.6 5.8 %collective-permute-start = (f32[1,32,128]{2,1,0:T(8,128)S(1)}, f32[1,32,128]{2,1,0:T(8,128)S(1)}, u32[]{:S(2)}, u32[]{:S(2)}) collective-permute-start(f32[1,32,128]{2,1,0:T(8,128)S(1)} %maximum_bitcast_fusion), channel_id=1, source_target_pairs={{0,2},{1,3},{2,0},{3,1},{4,6},{5,7},{6,4},{7,5},{8,10},{9,11},{10,... | collective-permute-start | bytes 49160 | tf_op jit(solution)/shard_map/ppermute | solution.py:188
  7.4 1.9 %copy-start.8 = (s32[1,7]{1,0:T(1,128)S(1)}, s32[1,7]{1,0:T(1,128)}, u32[]{:S(2)}) copy-start(s32[1,7]{1,0:T(1,128)} %param.11) | copy-start | bytes 88
  7.4 3.9 %collective-permute-start.1 = (f32[2,32,128]{2,1,0:T(8,128)S(1)}, f32[2,32,128]{2,1,0:T(8,128)S(1)}, u32[]{:S(2)}, u32[]{:S(2)}) collective-permute-start(f32[2,32,128]{2,1,0:T(8,128)S(1)} %pad_maximum_fusion.2), channel_id=1, source_target_pairs={{0,1},{1,0},{2,3},{3,2},{4,5},{5,4},{6,7},{7,6},{8,9},{9,8},{10,11... | collective-permute-start | bytes 98312 | tf_op jit(solution)/shard_map/ppermute | solution.py:188
  11.3 0.7 %copy-start.4 = (f32[3,128]{1,0:T(4,128)S(1)}, f32[3,128]{1,0:T(4,128)}, u32[]{:S(2)}) copy-start(f32[3,128]{1,0:T(4,128)} %param.8) | copy-start | bytes 4612
  12.0 2.6 %copy-start.3 = (f32[72,128]{1,0:T(8,128)}, f32[72,128]{1,0:T(8,128)S(1)}, u32[]{:S(2)}) copy-start(f32[72,128]{1,0:T(8,128)S(1)} %pad_maximum_fusion.1.refs_3_) | copy-start | bytes 110596
  12.0 4.0 %collective-permute-start.2 = (f32[72,128]{1,0:T(8,128)S(1)}, f32[72,128]{1,0:T(8,128)S(1)}, u32[]{:S(2)}, u32[]{:S(2)}) collective-permute-start(f32[72,128]{1,0:T(8,128)S(1)} %pad_maximum_fusion.1.refs_3_), channel_id=1, source_target_pairs={{0,8},{4,12},{8,0},{12,4},{16,24},{20,28},{24,16},{28,20},{1,9},{5... | collective-permute-start | bytes 110600 | tf_op jit(solution)/shard_map/ppermute | solution.py:188
  16.1 4.4 %copy-start.1 = (f32[72,128]{1,0:T(8,128)}, f32[72,128]{1,0:T(8,128)S(1)}, u32[]{:S(2)}) copy-start(f32[72,128]{1,0:T(8,128)S(1)} %collective-permute-done.2.refs_4_) | copy-start | bytes 110596
  16.1 4.4 %collective-permute-start.3 = (f32[144,128]{1,0:T(8,128)S(1)}, f32[144,128]{1,0:T(8,128)S(1)}, u32[]{:S(2)}, u32[]{:S(2)}) collective-permute-start(f32[144,128]{1,0:T(8,128)S(1)} %concatenate.37), channel_id=1, source_target_pairs={{0,16},{4,20},{8,24},{12,28},{16,0},{20,4},{24,8},{28,12},{1,17},{... | collective-permute-start | bytes 221192 | tf_op jit(solution)/shard_map/ppermute | solution.py:188
  20.5 0.6 %copy-start = (f32[144,128]{1,0:T(8,128)}, f32[144,128]{1,0:T(8,128)S(1)}, u32[]{:S(2)}) copy-start(f32[144,128]{1,0:T(8,128)S(1)} %collective-permute-done.3.refs_3_) | copy-start | bytes 221188
  21.1 7.8 %collective-permute-start.4 = (f32[288,128]{1,0:T(8,128)S(1)}, f32[288,128]{1,0:T(8,128)S(1)}, u32[]{:S(2)}, u32[]{:S(2)}) collective-permute-start(f32[288,128]{1,0:T(8,128)S(1)} %concatenate.38), channel_id=1, source_target_pairs={{0,4},{4,0},{8,12},{12,8},{16,20},{20,16},{24,28},{28,24},{1,5},{5... | collective-permute-start | bytes 442376 | tf_op jit(solution)/shard_map/ppermute | solution.py:188
  28.9 0.7 %copy-start.6 = (f32[288,128]{1,0:T(8,128)}, f32[288,128]{1,0:T(8,128)S(1)}, u32[]{:S(2)}) copy-start(f32[288,128]{1,0:T(8,128)S(1)} %collective-permute-done.4.refs_3_) | copy-start | bytes 442372
where the time goes:
time: 35.2 us; the launch traced here: 34.8 us
  Pallas kernels  11.7 us (33%)
  starting transfers between devices  9.91 us (28%)
  waiting for transfers between devices  6.52 us (19%)
  local copies, waits for them, and re-layouts  4.32 us (12%)
  other arithmetic  2.28 us (6%)
    pallas_call x3, Pallas kernels, accumulate(): pl.pallas_call(body, out_shape=jax.ShapeDtypeStruct(shape, jnp.float32),...  11.7 us
    ppermute x5, starting transfers between devices, moved(): lax.ppermute(value, axis, [(i, target(i, size)) for i in range(size)])  9.91 us
    ppermute x5, waiting for transfers between devices, moved(): lax.ppermute(value, axis, [(i, target(i, size)) for i in range(size)])  6.52 us
    unnamed x18, local copies, waits for them, and re-layouts  1.95 us
    concatenate x1, other arithmetic, shards(): rows = jnp.concatenate([radial_weight, center_embed.T], axis=0)  0.78 us
    broadcast_in_dim x1, local copies, waits for them, and re-layouts, shards(): jnp.where(species[None, :] == kind, species_embed[:, kind:kind + 1], embe...  0.76 us
    transpose x2, local copies, waits for them, and re-layouts, shards(): par = owned[:, held:held + count + kinds, :held].transpose(0, 2, 1)  0.72 us
  transfers between devices with their start and end apart: 5, of which 4 were waited for; matrix products, arithmetic and copies ran while one was open for 9% of the time, Pallas kernels for 18%

commit v1 on v0

--- a/solution.py
+++ b/solution.py
@@ -179,7 +179,62 @@
             pltpu.VMEM(wide if mix is not None else (8, lanes), jnp.float32),
         ],
         cost_estimate=pl.CostEstimate(flops=flops, bytes_accessed=1 << 20, transcendentals=0),
+        compiler_params=pltpu.CompilerParams(vmem_limit_bytes=16 << 20),
         name=name,
+    )(*operands)
+
+
+def pack_kernel(*refs):
+    sources, (out_ref, own_ref), held_refs = refs[:6], refs[6:8], refs[8:14]
+    tile_ref, sems = refs[14:]
+    copies = [
+        pltpu.make_async_copy(source, held_ref, sems.at[i])
+        for i, (source, held_ref) in enumerate(zip(sources, held_refs))
+    ]
+    for copy in copies:
+        copy.start()
+    feats_ref, species_ref, pos_ref, embed_ref, radial_ref, center_ref = held_refs
+    held = feats_ref.shape[0]
+    kinds, count = embed_ref.shape[0], radial_ref.shape[0]
+    tile_ref[...] = jnp.zeros_like(tile_ref)
+    out_ref[held:, :] = jnp.zeros((tile, lanes), jnp.float32)
+    own_ref[...] = jnp.zeros_like(own_ref)
+    for copy in copies:
+        copy.wait()
+    tile_ref[0:kinds, 0:held] = embed_ref[...]
+    columns = tile_ref[...].T
+    embedded = jnp.zeros(feats_ref.shape, jnp.float32)
+    for kind in range(kinds):
+        embedded = jnp.where(species_ref[...] == kind, columns[:held, kind : kind + 1], embedded)
+    out_ref[0:held, :] = feats_ref[...] * embedded
+    out_ref[held : held + count, 0:held] = radial_ref[...]
+    out_ref[held + count : held + count + kinds, 0:held] = center_ref[...]
+    own_ref[0:3, :] = pos_ref[...]
+    own_ref[3:4, :] = species_ref[...].astype(jnp.float32)
+
+
+def pack(node_features, species, positions, species_embed, radial_weight, center_embed):
+    held, atoms = node_features.shape
+    operands = (
+        node_features,
+        species[None],
+        positions,
+        species_embed.T,
+        radial_weight,
+        center_embed.T,
+    )
+    return pl.pallas_call(
+        pack_kernel,
+        out_shape=(
+            jax.ShapeDtypeStruct((held + tile, atoms), jnp.float32),
+            jax.ShapeDtypeStruct((8, atoms), jnp.float32),
+        ),
+        in_specs=[pl.BlockSpec(memory_space=pltpu.HBM)] * len(operands),
+        out_specs=[pl.BlockSpec(memory_space=pltpu.VMEM)] * 2,
+        scratch_shapes=[pltpu.VMEM(x.shape, x.dtype) for x in operands]
+        + [pltpu.VMEM((8, lanes), jnp.float32), pltpu.SemaphoreType.DMA((len(operands),))],
+        compiler_params=pltpu.CompilerParams(vmem_limit_bytes=1 << 20),
+        name="pack",
     )(*operands)
 
 
@@ -212,12 +267,10 @@
     me = lax.axis_index("blk")
     owner = lax.axis_index("chan")
 
-    embedded = jnp.zeros((held, atoms), jnp.float32)
-    for kind in range(kinds):
-        embedded = jnp.where(species[None, :] == kind, species_embed[:, kind : kind + 1], embedded)
-    rows = jnp.concatenate([radial_weight, center_embed.T], axis=0)
-    rows = jnp.pad(rows, ((0, tile - count - kinds), (0, atoms - held)))
-    owned = jnp.concatenate([node_features * embedded, rows], axis=0)[None]
+    owned, pos = pack(
+        node_features, species, positions, species_embed, radial_weight, center_embed
+    )
+    owned = owned[None]
     bit = owner_count // 2
     flips = [0]
     while bit:
@@ -233,9 +286,6 @@
         [lax.dynamic_slice_in_dim(mine, (owner ^ f) * held, held, 2) for f in flips], axis=2
     )
 
-    pos = jnp.concatenate(
-        [positions, species[None].astype(jnp.float32), jnp.zeros((4, atoms), jnp.float32)], axis=0
-    )
     bundle = jnp.concatenate([feats, pos], axis=0)
     depth = bundle.shape[0]
 
@@ -251,13 +301,20 @@
     if slab_count == 2 * (reach + 1) == 8:
         act = activity([me ^ j for j in range(slab_count)])
         two = flipped(bundle, "blk", 2)
+        acc = call("own", act, [bundle], [(0, 0, 0)])
+        two, acc = lax.optimization_barrier((two, acc))
         pair = jnp.concatenate([bundle, two], axis=0)
         four = flipped(pair, "blk", 4)
-        acc = call("near", act, [bundle, two], [(0, 0, 0), (1, 0, 2)])
-        quad = jnp.concatenate([pair, four], axis=0)
-        one = flipped(quad, "blk", 1)
-        acc = call("middle", act, [four], [(0, depth, 6)], acc)
-        return call("far", act, [one], [(0, j // 2 * depth, j) for j in (1, 3, 5, 7)], acc, mix)
+        one = flipped(pair, "blk", 1)
+        acc = call("two", act, [two], [(0, 0, 2)], acc)
+        acc = call("one", act, [one], [(0, 0, 1)], acc)
+        four, acc = lax.optimization_barrier((four, acc))
+        five = flipped(four, "blk", 1)
+        acc = call("three", act, [one], [(0, depth, 3)], acc)
+        five, acc = lax.optimization_barrier((five, acc))
+        return call(
+            "far", act, [four, five], [(0, depth, 6), (1, 0, 5), (1, depth, 7)], acc, mix
+        )
     places = [0] + [k for h in range(1, reach + 1) for k in (h, -h)]
     act = activity([lax.rem(me + k + slab_count, slab_count) for k in places])
     act = jnp.pad(act, ((0, 8 - len(places)), (0, 0)))

time: 35.2 us -> 26.7 us (0.76)
  Pallas kernels: 11.7 us -> 8.22 us
  other arithmetic: 2.28 us -> 0.29 us
  waiting for transfers between devices: 6.52 us -> 4.71 us
  local copies, waits for them, and re-layouts: 4.32 us -> 3.12 us
    pallas_call x3 -> x5, Pallas kernels: 11.7 us -> 8 us  [accumulate(): pl.pallas_call(body, out_shape=jax.ShapeDtypeStruct(shape, jnp.float32),...]
    ppermute x5 -> x6, waiting for transfers between devices: 6.52 us -> 4.71 us  [moved(): lax.ppermute(value, axis, [(i, target(i, size)) for i in range(size)])]
    concatenate x2 -> x1, other arithmetic: 1.38 us -> 0.01 us  [shards(): pair = jnp.concatenate([bundle, two], axis=0)]
    unnamed x18 -> x16, local copies, waits for them, and re-layouts: 1.95 us -> 2.76 us
    broadcast_in_dim x2 -> x0, local copies, waits for them, and re-layouts: 0.76 us -> none  [the longest x1 0.76 us: shards(): jnp.where(species[None, :] == kind, species_embed[:, kind:kind + 1], embe...]
    transpose x2, local copies, waits for them, and re-layouts: 0.72 us -> 0.1 us  [shards(): par = owned[:, held:held + count + kinds, :held].transpose(0, 2, 1)]
    concatenate x1, other arithmetic: 0.69 us -> 0.08 us  [shards(): jnp.concatenate([lax.dynamic_slice_in_dim(mine, (owner ^ f) * held, held,...]
    broadcast_in_dim x1, local copies, waits for them, and re-layouts: 0.66 us -> 0.07 us  [activity(): return jnp.broadcast_to(value[:, None], (len(places), atoms))]
  transfers between devices with their start and end apart: 5 -> 6, of which waited for: 4 -> 4; matrix products, arithmetic and copies ran while one was open for 9% -> 2% of each run, Pallas kernels for 18% -> 17%
where the time goes in v1:
time: 26.7 us; the launch traced here: 26.4 us
  starting transfers between devices  9.95 us (37%)
  Pallas kernels  8.22 us (31%)
  waiting for transfers between devices  4.71 us (18%)
  local copies, waits for them, and re-layouts  3.12 us (12%)
  other arithmetic  0.29 us (1%)
    ppermute x6, starting transfers between devices, moved(): lax.ppermute(value, axis, [(i, target(i, size)) for i in range(size)])  9.95 us
    pallas_call x5, Pallas kernels, accumulate(): pl.pallas_call(body, out_shape=jax.ShapeDtypeStruct(shape, jnp.float32),...  8 us
    ppermute x6, waiting for transfers between devices, moved(): lax.ppermute(value, axis, [(i, target(i, size)) for i in range(size)])  4.71 us
    unnamed x16, local copies, waits for them, and re-layouts  2.76 us
  transfers between devices with their start and end apart: 6, of which 4 were waited for; matrix products, arithmetic and copies ran while one was open for 2% of the time, Pallas kernels for 17%

profile of v1, /device:TPU:0, one launch (start us, length us, event | category | flops | bytes accessed | tf_op | source)
XLA Modules:
  0.0 26.4 jit_solution(4266653735223005125)
XLA Ops:
  0.0 0.0 copy-start.1
  0.0 0.0 copy-start.3
  0.0 0.0 copy-start.5
  0.0 0.7 %copy-done.1 = f32[8,16]{1,0:T(8,128)S(1)} copy-done((f32[8,16]{1,0:T(8,128)S(1)}, f32[8,16]{1,0:T(8,128)}, u32[]{:S(2)}) %copy-start.1) | copy-done | bytes 536
  0.7 0.0 copy-done.3
  0.7 0.0 copy-done.5
  0.7 0.0 copy-start
  0.7 0.7 %copy-done = f32[16,128]{1,0:T(8,128)S(1)} copy-done((f32[16,128]{1,0:T(8,128)S(1)}, f32[16,128]{1,0:T(8,128)}, u32[]{:S(2)}) %copy-start) | copy-done | bytes 8216
  1.4 0.0 copy-start.2
  1.4 0.7 %copy-done.2 = f32[3,128]{1,0:T(4,128)S(1)} copy-done((f32[3,128]{1,0:T(4,128)S(1)}, f32[3,128]{1,0:T(4,128)}, u32[]{:S(2)}) %copy-start.2) | copy-done | bytes 1560
  2.1 0.0 copy-start.4
  2.1 0.7 %copy-done.4 = f32[16,2]{0,1:T(2,128)S(1)} copy-done((f32[16,2]{0,1:T(2,128)S(1)}, f32[16,2]{0,1:T(2,128)}, u32[]{:S(2)}) %copy-start.4) | copy-done | bytes 152
  2.8 0.2 pack.1
  3.0 4.1 %collective-permute-start = (f32[1,32,128]{2,1,0:T(8,128)S(1)}, f32[1,32,128]{2,1,0:T(8,128)S(1)}, u32[]{:S(2)}, u32[]{:S(2)}) collective-permute-start(f32[1,32,128]{2,1,0:T(8,128)S(1)} %bitcast.21), channel_id=1, source_target_pairs={{0,2},{1,3},{2,0},{3,1},{4,6},{5,7},{6,4},{7,5},{8,10},{9,11},{10,... | collective-permute-start | bytes 49160 | tf_op jit(solution)/shard_map/ppermute | solution.py:243
  7.1 0.1 stack.31
  7.2 1.6 %collective-permute-done = f32[1,32,128]{2,1,0:T(8,128)S(1)} collective-permute-done((f32[1,32,128]{2,1,0:T(8,128)S(1)}, f32[1,32,128]{2,1,0:T(8,128)S(1)}, u32[]{:S(2)}, u32[]{:S(2)}) %collective-permute-start) | collective-permute-done | bytes 16416 | tf_op jit(solution)/shard_map/ppermute | solution.py:243
  8.8 0.0 copy-start.7
  8.8 1.9 %collective-permute-start.1 = (f32[2,32,128]{2,1,0:T(8,128)S(1)}, f32[2,32,128]{2,1,0:T(8,128)S(1)}, u32[]{:S(2)}, u32[]{:S(2)}) collective-permute-start(f32[2,32,128]{2,1,0:T(8,128)S(1)} %pad_maximum_fusion.3), channel_id=1, source_target_pairs={{0,1},{1,0},{2,3},{3,2},{4,5},{5,4},{6,7},{7,6},{8,9},{9,8},{10,11... | collective-permute-start | bytes 98312 | tf_op jit(solution)/shard_map/ppermute | solution.py:243
  10.7 0.0 copy-done.7
  10.8 0.2 select_reduce_fusion
  11.0 1.8 %collective-permute-done.1 = f32[2,32,128]{2,1,0:T(8,128)S(1)} collective-permute-done((f32[2,32,128]{2,1,0:T(8,128)S(1)}, f32[2,32,128]{2,1,0:T(8,128)S(1)}, u32[]{:S(2)}, u32[]{:S(2)}) %collective-permute-start.1) | collective-permute-done | bytes 32800 | tf_op jit(solution)/shard_map/ppermute | solution.py:243
  12.8 1.9 %collective-permute-start.2 = (f32[72,128]{1,0:T(8,128)S(1)}, f32[72,128]{1,0:T(8,128)S(1)}, u32[]{:S(2)}, u32[]{:S(2)}) collective-permute-start(f32[72,128]{1,0:T(8,128)S(1)} %pad_maximum_fusion.2.refs_3_), channel_id=1, source_target_pairs={{0,8},{4,12},{8,0},{12,4},{16,24},{20,28},{24,16},{28,20},{1,9},{5... | collective-permute-start | bytes 110600 | tf_op jit(solution)/shard_map/ppermute | solution.py:243
  14.7 0.1 copy.10
  14.8 0.1 broadcast_in_dim.32.refs_1_
  14.9 1.1 %own.1.refs_4_ = f32[64,1152]{1,0:T(8,128)S(1)} custom-call(f32[8,128]{1,0:T(8,128)S(1)} %get-tuple-element.13.refs_0_, f32[8,128]{1,0:T(8,128)S(1)} %broadcast_in_dim.32.refs_1_, f32[64,10]{1,0:T(8,128)S(1)} %bitcast.16, f32[72,128]{1,0:T(8,128)S(1)} %pad_maximum_fusion.2.refs_3_), custom_call_target="tpu_custom_call" | custom-call | flops 150994944 | bytes 1048576 | tf_op jit(solution)/shard_map/own/pallas_call | solution.py:171
  16.0 0.0 copy-start.6
  16.0 0.8 %collective-permute-done.2.refs_3_ = f32[72,128]{1,0:T(8,128)S(1)} collective-permute-done((f32[72,128]{1,0:T(8,128)S(1)}, f32[72,128]{1,0:T(8,128)S(1)}, u32[]{:S(2)}, u32[]{:S(2)}) %collective-permute-start.2) | collective-permute-done | bytes 36896 | tf_op jit(solution)/shard_map/ppermute | solution.py:243
  16.8 0.0 collective-permute-start.4
  16.8 2.0 %collective-permute-start.3 = (f32[144,128]{1,0:T(8,128)S(1)}, f32[144,128]{1,0:T(8,128)S(1)}, u32[]{:S(2)}, u32[]{:S(2)}) collective-permute-start(f32[144,128]{1,0:T(8,128)S(1)} %pad_maximum_fusion), channel_id=1, source_target_pairs={{0,16},{4,20},{8,24},{12,28},{16,0},{20,4},{24,8},{28,12},{1,17},{... | collective-permute-start | bytes 221192 | tf_op jit(solution)/shard_map/ppermute | solution.py:243
  18.8 0.0 copy-done.6
  18.8 0.1 constant_dynamic-slice_fusion.2
  18.9 1.1 %two.1.refs_4_ = f32[64,1152]{1,0:T(8,128)S(1)} custom-call(f32[8,128]{1,0:T(8,128)S(1)} %get-tuple-element.13.refs_0_, f32[8,128]{1,0:T(8,128)S(1)} %broadcast_in_dim.32.refs_1_, f32[64,10]{1,0:T(8,128)S(1)} %bitcast.17, f32[72,128]{1,0:T(8,128)S(1)} %collective-permute-done.2.refs_3_, f32[64,1152]{1,0:T(8,128)S(1)} %own.1.refs_4_), custom_call_target="tpu_custom_call" | custom-call | flops 150994944 | bytes 1048576 | tf_op jit(solution)/shard_map/two/pallas_call | solution.py:171
  20.0 0.0 collective-permute-done.4.refs_3_
  20.0 1.1 %one.1.refs_4_ = f32[64,1152]{1,0:T(8,128)S(1)} custom-call(f32[8,128]{1,0:T(8,128)S(1)} %get-tuple-element.13.refs_0_, f32[8,128]{1,0:T(8,128)S(1)} %broadcast_in_dim.32.refs_1_, f32[64,10]{1,0:T(8,128)S(1)} %bitcast.18, f32[144,128]{1,0:T(8,128)S(1)} %collective-permute-done.4.refs_3_, f32[64,1152]{1,0:T(8,128)S(1)} %two.1.refs_4_), custom_call_target="tpu_custom_call" | custom-call | flops 150994944 | bytes 1048576 | tf_op jit(solution)/shard_map/one/pallas_call | solution.py:171
  21.2 0.5 %collective-permute-done.3.refs_3_ = f32[144,128]{1,0:T(8,128)S(1)} collective-permute-done((f32[144,128]{1,0:T(8,128)S(1)}, f32[144,128]{1,0:T(8,128)S(1)}, u32[]{:S(2)}, u32[]{:S(2)}) %collective-permute-start.3) | collective-permute-done | bytes 73760 | tf_op jit(solution)/shard_map/ppermute | solution.py:243
  21.7 0.0 collective-permute-start.5
  21.7 0.1 pad_maximum_fusion.4.refs_6_
  21.8 1.1 %three.1.refs_5_ = f32[64,1152]{1,0:T(8,128)S(1)} custom-call(f32[8,128]{1,0:T(8,128)S(1)} %get-tuple-element.13.refs_0_, f32[8,128]{1,0:T(8,128)S(1)} %broadcast_in_dim.32.refs_1_, f32[64,10]{1,0:T(8,128)S(1)} %bitcast.19, f32[144,128]{1,0:T(8,128)S(1)} %collective-permute-done.4.refs_3_, f32[64,1152]{1,0:T(8,128)S(1)} %one.1.refs_4_), custom_call_target="tpu_custom_call" | custom-call | flops 150994944 | bytes 1048576 | tf_op jit(solution)/shard_map/three/pallas_call | solution.py:171
  22.9 0.0 collective-permute-done.5.refs_4_
  22.9 3.5 %far.1 = f32[3,16,128]{2,1,0:T(8,128)} custom-call(f32[8,128]{1,0:T(8,128)S(1)} %get-tuple-element.13.refs_0_, f32[8,128]{1,0:T(8,128)S(1)} %broadcast_in_dim.32.refs_1_, f32[64,10]{1,0:T(8,128)S(1)} %bitcast.20, f32[144,128]{1,0:T(8,128)S(1)} %collective-permute-done.3.refs_3_, f32[144,128]{1,0:T(8,128)S(1)} %collective-permute-done.5.refs_4_, ...), custom_call_target="tpu_custom_call" | custom-call | flops 452984832 | bytes 1048576 | tf_op jit(solution)/shard_map/far/pallas_call | solution.py:171
  (7 shorter events, 0.0 us)
Async XLA Ops:
  0.0 0.7 %copy-start.1 = (f32[8,16]{1,0:T(8,128)S(1)}, f32[8,16]{1,0:T(8,128)}, u32[]{:S(2)}) copy-start(f32[8,16]{1,0:T(8,128)} %refs_4_.1) | copy-start | bytes 1540
  0.0 0.7 %copy-start.3 = (f32[16,2]{0,1:T(2,128)S(1)}, f32[16,2]{0,1:T(2,128)}, u32[]{:S(2)}) copy-start(f32[16,2]{0,1:T(2,128)} %param.13) | copy-start | bytes 388
  0.0 0.7 %copy-start.5 = (s32[128]{0:T(128)S(1)}, s32[128]{0:T(128)}, u32[]{:S(2)}) copy-start(s32[128]{0:T(128)} %param.9) | copy-start | bytes 1540
  0.7 0.7 %copy-start = (f32[16,128]{1,0:T(8,128)S(1)}, f32[16,128]{1,0:T(8,128)}, u32[]{:S(2)}) copy-start(f32[16,128]{1,0:T(8,128)} %refs_0_.1) | copy-start | bytes 24580
  1.4 0.7 %copy-start.2 = (f32[3,128]{1,0:T(4,128)S(1)}, f32[3,128]{1,0:T(4,128)}, u32[]{:S(2)}) copy-start(f32[3,128]{1,0:T(4,128)} %refs_2_.1) | copy-start | bytes 4612
  2.1 0.7 %copy-start.4 = (f32[16,2]{0,1:T(2,128)S(1)}, f32[16,2]{0,1:T(2,128)}, u32[]{:S(2)}) copy-start(f32[16,2]{0,1:T(2,128)} %param.14) | copy-start | bytes 388
  3.0 5.8 %collective-permute-start = (f32[1,32,128]{2,1,0:T(8,128)S(1)}, f32[1,32,128]{2,1,0:T(8,128)S(1)}, u32[]{:S(2)}, u32[]{:S(2)}) collective-permute-start(f32[1,32,128]{2,1,0:T(8,128)S(1)} %bitcast.21), channel_id=1, source_target_pairs={{0,2},{1,3},{2,0},{3,1},{4,6},{5,7},{6,4},{7,5},{8,10},{9,11},{10,... | collective-permute-start | bytes 49160 | tf_op jit(solution)/shard_map/ppermute | solution.py:243
  8.8 1.9 %copy-start.7 = (s32[1,7]{1,0:T(1,128)S(1)}, s32[1,7]{1,0:T(1,128)}, u32[]{:S(2)}) copy-start(s32[1,7]{1,0:T(1,128)} %param.11) | copy-start | bytes 88
  8.8 3.9 %collective-permute-start.1 = (f32[2,32,128]{2,1,0:T(8,128)S(1)}, f32[2,32,128]{2,1,0:T(8,128)S(1)}, u32[]{:S(2)}, u32[]{:S(2)}) collective-permute-start(f32[2,32,128]{2,1,0:T(8,128)S(1)} %pad_maximum_fusion.3), channel_id=1, source_target_pairs={{0,1},{1,0},{2,3},{3,2},{4,5},{5,4},{6,7},{7,6},{8,9},{9,8},{10,11... | collective-permute-start | bytes 98312 | tf_op jit(solution)/shard_map/ppermute | solution.py:243
  12.8 4.0 %collective-permute-start.2 = (f32[72,128]{1,0:T(8,128)S(1)}, f32[72,128]{1,0:T(8,128)S(1)}, u32[]{:S(2)}, u32[]{:S(2)}) collective-permute-start(f32[72,128]{1,0:T(8,128)S(1)} %pad_maximum_fusion.2.refs_3_), channel_id=1, source_target_pairs={{0,8},{4,12},{8,0},{12,4},{16,24},{20,28},{24,16},{28,20},{1,9},{5... | collective-permute-start | bytes 110600 | tf_op jit(solution)/shard_map/ppermute | solution.py:243
  16.0 2.8 %copy-start.6 = (f32[3,64,64]{2,1,0:T(8,128)S(1)}, f32[3,64,64]{2,1,0:T(8,128)}, u32[]{:S(2)}) copy-start(f32[3,64,64]{2,1,0:T(8,128)} %param.15) | copy-start | bytes 147460
  16.8 3.2 %collective-permute-start.4 = (f32[144,128]{1,0:T(8,128)S(1)}, f32[144,128]{1,0:T(8,128)S(1)}, u32[]{:S(2)}, u32[]{:S(2)}) collective-permute-start(f32[144,128]{1,0:T(8,128)S(1)} %pad_maximum_fusion), channel_id=1, source_target_pairs={{0,4},{4,0},{8,12},{12,8},{16,20},{20,16},{24,28},{28,24},{1,5},{5... | collective-permute-start | bytes 221192 | tf_op jit(solution)/shard_map/ppermute | solution.py:243
  16.8 4.8 %collective-permute-start.3 = (f32[144,128]{1,0:T(8,128)S(1)}, f32[144,128]{1,0:T(8,128)S(1)}, u32[]{:S(2)}, u32[]{:S(2)}) collective-permute-start(f32[144,128]{1,0:T(8,128)S(1)} %pad_maximum_fusion), channel_id=1, source_target_pairs={{0,16},{4,20},{8,24},{12,28},{16,0},{20,4},{24,8},{28,12},{1,17},{... | collective-permute-start | bytes 221192 | tf_op jit(solution)/shard_map/ppermute | solution.py:243
  21.7 1.3 %collective-permute-start.5 = (f32[144,128]{1,0:T(8,128)S(1)}, f32[144,128]{1,0:T(8,128)S(1)}, u32[]{:S(2)}, u32[]{:S(2)}) collective-permute-start(f32[144,128]{1,0:T(8,128)S(1)} %collective-permute-done.3.refs_3_), channel_id=1, source_target_pairs={{0,4},{4,0},{8,12},{12,8},{16,20},{20,16},{24,28},{28,24},{1,5},{5... | collective-permute-start | bytes 221192 | tf_op jit(solution)/shard_map/ppermute | solution.py:243

commit v2 on v1

--- a/solution.py
+++ b/solution.py
@@ -223,6 +223,7 @@
         radial_weight,
         center_embed.T,
     )
+    operands = [pltpu.with_memory_space_constraint(x, pltpu.HBM) for x in operands]
     return pl.pallas_call(
         pack_kernel,
         out_shape=(
@@ -300,21 +301,19 @@
     )
     if slab_count == 2 * (reach + 1) == 8:
         act = activity([me ^ j for j in range(slab_count)])
-        two = flipped(bundle, "blk", 2)
+        three = flipped(bundle, "blk", 3)
         acc = call("own", act, [bundle], [(0, 0, 0)])
-        two, acc = lax.optimization_barrier((two, acc))
-        pair = jnp.concatenate([bundle, two], axis=0)
-        four = flipped(pair, "blk", 4)
+        three, acc = lax.optimization_barrier((three, acc))
+        pair = jnp.concatenate([bundle, three], axis=0)
+        five = flipped(pair, "blk", 5)
         one = flipped(pair, "blk", 1)
-        acc = call("two", act, [two], [(0, 0, 2)], acc)
-        acc = call("one", act, [one], [(0, 0, 1)], acc)
-        four, acc = lax.optimization_barrier((four, acc))
-        five = flipped(four, "blk", 1)
-        acc = call("three", act, [one], [(0, depth, 3)], acc)
+        acc = call("near", act, [three], [(0, 0, 3)], acc)
+        acc = call("middle", act, [one], [(0, 0, 1), (0, depth, 2)], acc)
         five, acc = lax.optimization_barrier((five, acc))
-        return call(
-            "far", act, [four, five], [(0, depth, 6), (1, 0, 5), (1, depth, 7)], acc, mix
-        )
+        seven = flipped(five[depth:], "blk", 1)
+        acc = call("next", act, [five], [(0, 0, 5)], acc)
+        seven, acc = lax.optimization_barrier((seven, acc))
+        return call("far", act, [five, seven], [(0, depth, 6), (1, 0, 7)], acc, mix)
     places = [0] + [k for h in range(1, reach + 1) for k in (h, -h)]
     act = activity([lax.rem(me + k + slab_count, slab_count) for k in places])
     act = jnp.pad(act, ((0, 8 - len(places)), (0, 0)))

time: 26.7 us -> 24.3 us (0.910)
  local copies, waits for them, and re-layouts: 3.12 us -> 0.37 us
  starting transfers between devices: 9.95 us -> 8.65 us
  Pallas kernels: 8.22 us -> 9.16 us
  waiting for transfers between devices: 4.71 us -> 5.47 us
    unnamed x16 -> x4, local copies, waits for them, and re-layouts: 2.76 us -> 0.01 us
    ppermute x6, starting transfers between devices: 9.95 us -> 8.65 us  [moved(): lax.ppermute(value, axis, [(i, target(i, size)) for i in range(size)])]
    ppermute x6, waiting for transfers between devices: 4.71 us -> 5.47 us  [moved(): lax.ppermute(value, axis, [(i, target(i, size)) for i in range(size)])]
    pallas_call x1, Pallas kernels: 0.22 us -> 0.96 us  [pack(): pl.pallas_call(pack_kernel, out_shape=(jax.ShapeDtypeStruct((held + tile,...]
  transfers between devices with their start and end apart: 6 -> 6, of which waited for: 4 -> 3; matrix products, arithmetic and copies ran while one was open for 2% -> 3% of each run, Pallas kernels for 17% -> 22%
where the time goes in v2:
time: 24.3 us; the launch traced here: 24.1 us
  Pallas kernels  9.16 us (38%)
  starting transfers between devices  8.65 us (36%)
  waiting for transfers between devices  5.47 us (23%)
  local copies, waits for them, and re-layouts  0.37 us (2%)
  other arithmetic  0.29 us (1%)
    ppermute x6, starting transfers between devices, moved(): lax.ppermute(value, axis, [(i, target(i, size)) for i in range(size)])  8.65 us
    pallas_call x5, Pallas kernels, accumulate(): pl.pallas_call(body, out_shape=jax.ShapeDtypeStruct(shape, jnp.float32),...  8.2 us
    ppermute x6, waiting for transfers between devices, moved(): lax.ppermute(value, axis, [(i, target(i, size)) for i in range(size)])  5.47 us
    pallas_call x1, Pallas kernels, pack(): pl.pallas_call(pack_kernel, out_shape=(jax.ShapeDtypeStruct((held + tile,...  0.96 us
  transfers between devices with their start and end apart: 6, of which 3 were waited for; matrix products, arithmetic and copies ran while one was open for 3% of the time, Pallas kernels for 22%

profile of v2, /device:TPU:0, one launch (start us, length us, event | category | flops | bytes accessed | tf_op | source)
XLA Modules:
  0.0 24.1 jit_solution(16378494542748442577)
XLA Ops:
  0.0 1.0 %pack.1 = (f32[32,128]{1,0:T(8,128)S(1)}, f32[8,128]{1,0:T(8,128)S(1)}) custom-call(f32[16,128]{1,0:T(8,128)} %refs_0_.1, s32[1,128]{1,0:T(1,128)} %bitcast.28, f32[3,128]{1,0:T(4,128)} %refs_2_.1, f32[2,16]{1,0:T(2,128)} %bitcast.26, f32[8,16]{1,0:T(8,128)} %refs_4_.1, f32[2,16]{1,0:T(2,128)} %bitcast.27), custom_call_target="tpu_custom_call" | custom-call | tf_op jit(solution)/shard_map/pack/pallas_call | solution.py:227
  1.0 4.1 %collective-permute-start = (f32[1,32,128]{2,1,0:T(8,128)S(1)}, f32[1,32,128]{2,1,0:T(8,128)S(1)}, u32[]{:S(2)}, u32[]{:S(2)}) collective-permute-start(f32[1,32,128]{2,1,0:T(8,128)S(1)} %bitcast.21), channel_id=1, source_target_pairs={{0,2},{1,3},{2,0},{3,1},{4,6},{5,7},{6,4},{7,5},{8,10},{9,11},{10,... | collective-permute-start | bytes 49160 | tf_op jit(solution)/shard_map/ppermute | solution.py:244
  5.1 0.1 stack.31
  5.2 1.6 %collective-permute-done = f32[1,32,128]{2,1,0:T(8,128)S(1)} collective-permute-done((f32[1,32,128]{2,1,0:T(8,128)S(1)}, f32[1,32,128]{2,1,0:T(8,128)S(1)}, u32[]{:S(2)}, u32[]{:S(2)}) %collective-permute-start) | collective-permute-done | bytes 16416 | tf_op jit(solution)/shard_map/ppermute | solution.py:244
  6.8 0.0 copy-start.1
  6.8 1.9 %collective-permute-start.1 = (f32[2,32,128]{2,1,0:T(8,128)S(1)}, f32[2,32,128]{2,1,0:T(8,128)S(1)}, u32[]{:S(2)}, u32[]{:S(2)}) collective-permute-start(f32[2,32,128]{2,1,0:T(8,128)S(1)} %pad_maximum_fusion.3), channel_id=1, source_target_pairs={{0,1},{1,0},{2,3},{3,2},{4,5},{5,4},{6,7},{7,6},{8,9},{9,8},{10,11... | collective-permute-start | bytes 98312 | tf_op jit(solution)/shard_map/ppermute | solution.py:244
  8.7 0.0 copy-done.1
  8.7 0.2 select_reduce_fusion
  9.0 1.8 %collective-permute-done.1 = f32[2,32,128]{2,1,0:T(8,128)S(1)} collective-permute-done((f32[2,32,128]{2,1,0:T(8,128)S(1)}, f32[2,32,128]{2,1,0:T(8,128)S(1)}, u32[]{:S(2)}, u32[]{:S(2)}) %collective-permute-start.1) | collective-permute-done | bytes 32800 | tf_op jit(solution)/shard_map/ppermute | solution.py:244
  10.8 0.1 collective-permute-start.2
  10.9 0.1 copy.10
  11.0 0.1 broadcast_in_dim.32.refs_1_
  11.0 1.1 %own.1.refs_4_ = f32[64,1152]{1,0:T(8,128)S(1)} custom-call(f32[8,128]{1,0:T(8,128)S(1)} %get-tuple-element.13.refs_0_, f32[8,128]{1,0:T(8,128)S(1)} %broadcast_in_dim.32.refs_1_, f32[64,10]{1,0:T(8,128)S(1)} %bitcast.16, f32[72,128]{1,0:T(8,128)S(1)} %pad_maximum_fusion.2.refs_3_), custom_call_target="tpu_custom_call" | custom-call | flops 150994944 | bytes 1048576 | tf_op jit(solution)/shard_map/own/pallas_call | solution.py:171
  12.1 0.0 copy-start
  12.2 2.1 %collective-permute-done.2.refs_3_ = f32[72,128]{1,0:T(8,128)S(1)} collective-permute-done((f32[72,128]{1,0:T(8,128)S(1)}, f32[72,128]{1,0:T(8,128)S(1)}, u32[]{:S(2)}, u32[]{:S(2)}) %collective-permute-start.2) | collective-permute-done | bytes 36896 | tf_op jit(solution)/shard_map/ppermute | solution.py:244
  14.2 0.2 %collective-permute-start.4 = (f32[144,128]{1,0:T(8,128)S(1)}, f32[144,128]{1,0:T(8,128)S(1)}, u32[]{:S(2)}, u32[]{:S(2)}) collective-permute-start(f32[144,128]{1,0:T(8,128)S(1)} %pad_maximum_fusion), channel_id=1, source_target_pairs={{0,4},{4,0},{8,12},{12,8},{16,20},{20,16},{24,28},{28,24},{1,5},{5... | collective-permute-start | bytes 221192 | tf_op jit(solution)/shard_map/ppermute | solution.py:244
  14.5 2.1 %collective-permute-start.3 = (f32[144,128]{1,0:T(8,128)S(1)}, f32[144,128]{1,0:T(8,128)S(1)}, u32[]{:S(2)}, u32[]{:S(2)}) collective-permute-start(f32[144,128]{1,0:T(8,128)S(1)} %pad_maximum_fusion), channel_id=1, source_target_pairs={{0,20},{4,16},{8,28},{12,24},{16,4},{20,0},{24,12},{28,8},{1,21},{... | collective-permute-start | bytes 221192 | tf_op jit(solution)/shard_map/ppermute | solution.py:244
  16.6 0.0 copy-done
  16.6 0.1 constant_dynamic-slice_fusion.2
  16.7 1.1 %near.1.refs_4_ = f32[64,1152]{1,0:T(8,128)S(1)} custom-call(f32[8,128]{1,0:T(8,128)S(1)} %get-tuple-element.13.refs_0_, f32[8,128]{1,0:T(8,128)S(1)} %broadcast_in_dim.32.refs_1_, f32[64,10]{1,0:T(8,128)S(1)} %bitcast.17, f32[72,128]{1,0:T(8,128)S(1)} %collective-permute-done.2.refs_3_, f32[64,1152]{1,0:T(8,128)S(1)} %own.1.refs_4_), custom_call_target="tpu_custom_call" | custom-call | flops 150994944 | bytes 1048576 | tf_op jit(solution)/shard_map/near/pallas_call | solution.py:171
  17.8 0.0 collective-permute-done.4.refs_3_
  17.8 2.0 %middle.1.refs_4_ = f32[64,1152]{1,0:T(8,128)S(1)} custom-call(f32[8,128]{1,0:T(8,128)S(1)} %get-tuple-element.13.refs_0_, f32[8,128]{1,0:T(8,128)S(1)} %broadcast_in_dim.32.refs_1_, f32[64,10]{1,0:T(8,128)S(1)} %bitcast.18, f32[144,128]{1,0:T(8,128)S(1)} %collective-permute-done.4.refs_3_, f32[64,1152]{1,0:T(8,128)S(1)} %near.1.refs_4_), custom_call_target="tpu_custom_call" | custom-call | flops 301989888 | bytes 1048576 | tf_op jit(solution)/shard_map/middle/pallas_call | solution.py:171
  19.9 0.0 collective-permute-done.3.refs_3_
  19.9 0.2 collective-permute-start.5
  20.1 0.1 pad_maximum_fusion.4.refs_6_
  20.2 1.1 %next.1.refs_5_ = f32[64,1152]{1,0:T(8,128)S(1)} custom-call(f32[8,128]{1,0:T(8,128)S(1)} %get-tuple-element.13.refs_0_, f32[8,128]{1,0:T(8,128)S(1)} %broadcast_in_dim.32.refs_1_, f32[64,10]{1,0:T(8,128)S(1)} %bitcast.19, f32[144,128]{1,0:T(8,128)S(1)} %collective-permute-done.3.refs_3_, f32[64,1152]{1,0:T(8,128)S(1)} %middle.1.refs_4_), custom_call_target="tpu_custom_call" | custom-call | flops 150994944 | bytes 1048576 | tf_op jit(solution)/shard_map/next/pallas_call | solution.py:171
  21.3 0.0 collective-permute-done.5.refs_4_
  21.3 2.8 %far.1 = f32[3,16,128]{2,1,0:T(8,128)} custom-call(f32[8,128]{1,0:T(8,128)S(1)} %get-tuple-element.13.refs_0_, f32[8,128]{1,0:T(8,128)S(1)} %broadcast_in_dim.32.refs_1_, f32[64,10]{1,0:T(8,128)S(1)} %bitcast.20, f32[144,128]{1,0:T(8,128)S(1)} %collective-permute-done.3.refs_3_, f32[72,128]{1,0:T(8,128)S(1)} %collective-permute-done.5.refs_4_, ...), custom_call_target="tpu_custom_call" | custom-call | flops 301989888 | bytes 1048576 | tf_op jit(solution)/shard_map/far/pallas_call | solution.py:171
  (8 shorter events, 0.0 us)
Async XLA Ops:
  1.0 5.8 %collective-permute-start = (f32[1,32,128]{2,1,0:T(8,128)S(1)}, f32[1,32,128]{2,1,0:T(8,128)S(1)}, u32[]{:S(2)}, u32[]{:S(2)}) collective-permute-start(f32[1,32,128]{2,1,0:T(8,128)S(1)} %bitcast.21), channel_id=1, source_target_pairs={{0,2},{1,3},{2,0},{3,1},{4,6},{5,7},{6,4},{7,5},{8,10},{9,11},{10,... | collective-permute-start | bytes 49160 | tf_op jit(solution)/shard_map/ppermute | solution.py:244
  6.8 1.9 %copy-start.1 = (s32[1,7]{1,0:T(1,128)S(1)}, s32[1,7]{1,0:T(1,128)}, u32[]{:S(2)}) copy-start(s32[1,7]{1,0:T(1,128)} %param.11) | copy-start | bytes 88
  6.8 3.9 %collective-permute-start.1 = (f32[2,32,128]{2,1,0:T(8,128)S(1)}, f32[2,32,128]{2,1,0:T(8,128)S(1)}, u32[]{:S(2)}, u32[]{:S(2)}) collective-permute-start(f32[2,32,128]{2,1,0:T(8,128)S(1)} %pad_maximum_fusion.3), channel_id=1, source_target_pairs={{0,1},{1,0},{2,3},{3,2},{4,5},{5,4},{6,7},{7,6},{8,9},{9,8},{10,11... | collective-permute-start | bytes 98312 | tf_op jit(solution)/shard_map/ppermute | solution.py:244
  10.8 3.4 %collective-permute-start.2 = (f32[72,128]{1,0:T(8,128)S(1)}, f32[72,128]{1,0:T(8,128)S(1)}, u32[]{:S(2)}, u32[]{:S(2)}) collective-permute-start(f32[72,128]{1,0:T(8,128)S(1)} %pad_maximum_fusion.2.refs_3_), channel_id=1, source_target_pairs={{0,12},{4,8},{8,4},{12,0},{16,28},{20,24},{24,20},{28,16},{1,13},{... | collective-permute-start | bytes 110600 | tf_op jit(solution)/shard_map/ppermute | solution.py:244
  12.1 4.4 %copy-start = (f32[3,64,64]{2,1,0:T(8,128)S(1)}, f32[3,64,64]{2,1,0:T(8,128)}, u32[]{:S(2)}) copy-start(f32[3,64,64]{2,1,0:T(8,128)} %param.15) | copy-start | bytes 147460
  14.2 3.6 %collective-permute-start.4 = (f32[144,128]{1,0:T(8,128)S(1)}, f32[144,128]{1,0:T(8,128)S(1)}, u32[]{:S(2)}, u32[]{:S(2)}) collective-permute-start(f32[144,128]{1,0:T(8,128)S(1)} %pad_maximum_fusion), channel_id=1, source_target_pairs={{0,4},{4,0},{8,12},{12,8},{16,20},{20,16},{24,28},{28,24},{1,5},{5... | collective-permute-start | bytes 221192 | tf_op jit(solution)/shard_map/ppermute | solution.py:244
  14.5 5.4 %collective-permute-start.3 = (f32[144,128]{1,0:T(8,128)S(1)}, f32[144,128]{1,0:T(8,128)S(1)}, u32[]{:S(2)}, u32[]{:S(2)}) collective-permute-start(f32[144,128]{1,0:T(8,128)S(1)} %pad_maximum_fusion), channel_id=1, source_target_pairs={{0,20},{4,16},{8,28},{12,24},{16,4},{20,0},{24,12},{28,8},{1,21},{... | collective-permute-start | bytes 221192 | tf_op jit(solution)/shard_map/ppermute | solution.py:244
  19.9 1.4 %collective-permute-start.5 = (f32[72,128]{1,0:T(8,128)S(1)}, f32[72,128]{1,0:T(8,128)S(1)}, u32[]{:S(2)}, u32[]{:S(2)}) collective-permute-start(f32[72,128]{1,0:T(8,128)S(1)} %slice.11), channel_id=1, source_target_pairs={{0,4},{4,0},{8,12},{12,8},{16,20},{20,16},{24,28},{28,24},{1,5},{5... | collective-permute-start | bytes 110600 | tf_op jit(solution)/shard_map/ppermute | solution.py:244

commit v3 on v2

--- a/solution.py
+++ b/solution.py
@@ -47,7 +47,7 @@
     shift = []
     for axis, length in enumerate((box_x, cross_width, cross_width)):
         r = other[axis] - own[axis]
-        shift.append(r - length * jnp.floor(r * (1.0 / length) + 0.5))
+        shift.append(length * (r - jnp.round(r)))
     x, y, z = shift
     xx, yy, zz = x * x, y * y, z * z
     s = xx + yy + zz + soften
@@ -81,7 +81,9 @@
         x * z * s15,
         (xx - yy) * (0.5 * s15),
     ]
-    return [[r if h is None else r * h for h in harmonics] for r in radial[:count]]
+    radial = [r.astype(jnp.bfloat16) for r in radial[:count]]
+    harmonics = [None if h is None else h.astype(jnp.bfloat16) for h in harmonics]
+    return [[r if h is None else r * h for h in harmonics] for r in radial]
 
 
 def pair_kernel(slabs, data_count, own_slab, first, last, box_x, count, *refs):
@@ -93,35 +95,44 @@
         acc_ref = rest.pop(0)
     if last:
         mix_ref = rest.pop(0)
-    out_ref, table_ref, weight_ref, sum_ref = rest
+    out_ref, sum_ref = rest
     channels = par_ref.shape[0]
-    own = [jnp.broadcast_to(pos_ref[axis : axis + 1, :], (tile, lanes)) for axis in range(3)]
+    scale = [1.0 / box_x, 1.0 / cross_width, 1.0 / cross_width]
+    own = [
+        jnp.broadcast_to(pos_ref[axis : axis + 1, :] * scale[axis], (tile, lanes))
+        for axis in range(3)
+    ]
+    lane = lax.broadcasted_iota(jnp.int32, (channels, lanes), 1)
+    group, within = lane // tile, lax.rem(lane, tile)
+    spread = jnp.broadcast_to(par_ref[:, 0:1], (channels, lanes))
+    for n in range(1, count):
+        spread = jnp.where(group == n, par_ref[:, n : n + 1], spread)
     for place, (which, base, index) in enumerate(slabs):
         ref = data[which]
         feats = ref[base : base + channels, :] * act_ref[index : index + 1, :]
         columns = ref[base + channels : base + channels + 8, :].T
-        for n in range(count):
-            weight_ref[:, n * lanes : (n + 1) * lanes] = (par_ref[:, n : n + 1] * feats).astype(
-                jnp.bfloat16
+        part = None
+        for pair in range(lanes // (2 * tile)):
+            weights, tables = [], []
+            for step in (2 * pair, 2 * pair + 1):
+                picked = jnp.take_along_axis(feats, within + step * tile, axis=1)
+                weights.append((spread * picked).astype(jnp.bfloat16))
+                rows = slice(step * tile, (step + 1) * tile)
+                other = [
+                    jnp.broadcast_to(columns[rows, axis : axis + 1] * scale[axis], (tile, lanes))
+                    for axis in range(3)
+                ]
+                apart = None
+                if index == own_slab:
+                    apart = (
+                        lax.broadcasted_iota(jnp.int32, (tile, lanes), 0) + step * tile
+                    ) != lax.broadcasted_iota(jnp.int32, (tile, lanes), 1)
+                tables += pair_rows(own, other, box_x, count, apart)
+            stacked = jnp.concatenate([jnp.concatenate(row, axis=1) for row in tables], axis=0)
+            product = jnp.dot(
+                jnp.concatenate(weights, axis=1), stacked, preferred_element_type=jnp.float32
             )
-        for step in range(lanes // tile):
-            rows = slice(step * tile, (step + 1) * tile)
-            other = [
-                jnp.broadcast_to(columns[rows, axis : axis + 1], (tile, lanes)) for axis in range(3)
-            ]
-            apart = None
-            if index == own_slab:
-                apart = (
-                    lax.broadcasted_iota(jnp.int32, (tile, lanes), 0) + step * tile
-                ) != lax.broadcasted_iota(jnp.int32, (tile, lanes), 1)
-            table = pair_rows(own, other, box_x, count, apart)
-            for n in range(count):
-                for m in range(components):
-                    table_ref[
-                        n * lanes + step * tile : n * lanes + (step + 1) * tile,
-                        m * lanes : (m + 1) * lanes,
-                    ] = table[n][m].astype(jnp.bfloat16)
-        part = jnp.dot(weight_ref[...], table_ref[...], preferred_element_type=jnp.float32)
+            part = product if part is None else part + product
         target = out_ref if not last else sum_ref
         if place == 0:
             target[...] = part if first else acc_ref[...] + part
@@ -174,8 +185,6 @@
         in_specs=[pl.BlockSpec(memory_space=pltpu.VMEM)] * len(operands),
         out_specs=pl.BlockSpec(memory_space=pltpu.VMEM),
         scratch_shapes=[
-            pltpu.VMEM((count * atoms, components * atoms), jnp.bfloat16),
-            pltpu.VMEM((channels, count * atoms), jnp.bfloat16),
             pltpu.VMEM(wide if mix is not None else (8, lanes), jnp.float32),
         ],
         cost_estimate=pl.CostEstimate(flops=flops, bytes_accessed=1 << 20, transcendentals=0),

time: 24.3 us -> 22.8 us (0.938)
  Pallas kernels: 9.16 us -> 7.09 us
  waiting for transfers between devices: 5.47 us -> 6.08 us
    pallas_call x5, Pallas kernels: 8.2 us -> 6.13 us  [accumulate(): pl.pallas_call(body, out_shape=jax.ShapeDtypeStruct(shape, jnp.float32),...]
    ppermute x6, waiting for transfers between devices: 5.47 us -> 6.08 us  [moved(): lax.ppermute(value, axis, [(i, target(i, size)) for i in range(size)])]
  transfers between devices with their start and end apart: 6 -> 6, of which waited for: 3 -> 5; matrix products, arithmetic and copies ran while one was open for 3% -> 3% of each run, Pallas kernels for 22% -> 17%
where the time goes in v3:
time: 22.8 us; the launch traced here: 22.6 us
  starting transfers between devices  8.59 us (38%)
  Pallas kernels  7.09 us (31%)
  waiting for transfers between devices  6.08 us (27%)
  local copies, waits for them, and re-layouts  0.37 us (2%)
  other arithmetic  0.29 us (1%)
    ppermute x6, starting transfers between devices, moved(): lax.ppermute(value, axis, [(i, target(i, size)) for i in range(size)])  8.59 us
    pallas_call x5, Pallas kernels, accumulate(): pl.pallas_call(body, out_shape=jax.ShapeDtypeStruct(shape, jnp.float32),...  6.13 us
    ppermute x6, waiting for transfers between devices, moved(): lax.ppermute(value, axis, [(i, target(i, size)) for i in range(size)])  6.08 us
    pallas_call x1, Pallas kernels, pack(): pl.pallas_call(pack_kernel, out_shape=(jax.ShapeDtypeStruct((held + tile,...  0.96 us
  transfers between devices with their start and end apart: 6, of which 5 were waited for; matrix products, arithmetic and copies ran while one was open for 3% of the time, Pallas kernels for 17%

profile of v3, /device:TPU:0, one launch (start us, length us, event | category | flops | bytes accessed | tf_op | source)
XLA Modules:
  0.0 22.6 jit_solution(8771778544573998559)
XLA Ops:
  0.0 1.0 %pack.1 = (f32[32,128]{1,0:T(8,128)S(1)}, f32[8,128]{1,0:T(8,128)S(1)}) custom-call(f32[16,128]{1,0:T(8,128)} %refs_0_.1, s32[1,128]{1,0:T(1,128)} %bitcast.28, f32[3,128]{1,0:T(4,128)} %refs_2_.1, f32[2,16]{1,0:T(2,128)} %bitcast.26, f32[8,16]{1,0:T(8,128)} %refs_4_.1, f32[2,16]{1,0:T(2,128)} %bitcast.27), custom_call_target="tpu_custom_call" | custom-call | tf_op jit(solution)/shard_map/pack/pallas_call | solution.py:236
  1.0 4.1 %collective-permute-start = (f32[1,32,128]{2,1,0:T(8,128)S(1)}, f32[1,32,128]{2,1,0:T(8,128)S(1)}, u32[]{:S(2)}, u32[]{:S(2)}) collective-permute-start(f32[1,32,128]{2,1,0:T(8,128)S(1)} %bitcast.21), channel_id=1, source_target_pairs={{0,2},{1,3},{2,0},{3,1},{4,6},{5,7},{6,4},{7,5},{8,10},{9,11},{10,... | collective-permute-start | bytes 49160 | tf_op jit(solution)/shard_map/ppermute | solution.py:253
  5.1 0.1 stack.31
  5.2 1.6 %collective-permute-done = f32[1,32,128]{2,1,0:T(8,128)S(1)} collective-permute-done((f32[1,32,128]{2,1,0:T(8,128)S(1)}, f32[1,32,128]{2,1,0:T(8,128)S(1)}, u32[]{:S(2)}, u32[]{:S(2)}) %collective-permute-start) | collective-permute-done | bytes 16416 | tf_op jit(solution)/shard_map/ppermute | solution.py:253
  6.8 0.0 copy-start.1
  6.8 1.9 %collective-permute-start.1 = (f32[2,32,128]{2,1,0:T(8,128)S(1)}, f32[2,32,128]{2,1,0:T(8,128)S(1)}, u32[]{:S(2)}, u32[]{:S(2)}) collective-permute-start(f32[2,32,128]{2,1,0:T(8,128)S(1)} %pad_maximum_fusion.3), channel_id=1, source_target_pairs={{0,1},{1,0},{2,3},{3,2},{4,5},{5,4},{6,7},{7,6},{8,9},{9,8},{10,11... | collective-permute-start | bytes 98312 | tf_op jit(solution)/shard_map/ppermute | solution.py:253
  8.7 0.0 copy-done.1
  8.7 0.2 select_reduce_fusion
  9.0 1.8 %collective-permute-done.1 = f32[2,32,128]{2,1,0:T(8,128)S(1)} collective-permute-done((f32[2,32,128]{2,1,0:T(8,128)S(1)}, f32[2,32,128]{2,1,0:T(8,128)S(1)}, u32[]{:S(2)}, u32[]{:S(2)}) %collective-permute-start.1) | collective-permute-done | bytes 32800 | tf_op jit(solution)/shard_map/ppermute | solution.py:253
  10.8 0.1 collective-permute-start.2
  10.9 0.1 copy.10
  11.0 0.1 broadcast_in_dim.32.refs_1_
  11.0 0.8 %own.1.refs_4_ = f32[64,1152]{1,0:T(8,128)S(1)} custom-call(f32[8,128]{1,0:T(8,128)S(1)} %get-tuple-element.13.refs_0_, f32[8,128]{1,0:T(8,128)S(1)} %broadcast_in_dim.32.refs_1_, f32[64,10]{1,0:T(8,128)S(1)} %bitcast.16, f32[72,128]{1,0:T(8,128)S(1)} %pad_maximum_fusion.2.refs_3_), custom_call_target="tpu_custom_call" | custom-call | flops 150994944 | bytes 1048576 | tf_op jit(solution)/shard_map/own/pallas_call | solution.py:182
  11.9 0.0 copy-start
  11.9 2.3 %collective-permute-done.2.refs_3_ = f32[72,128]{1,0:T(8,128)S(1)} collective-permute-done((f32[72,128]{1,0:T(8,128)S(1)}, f32[72,128]{1,0:T(8,128)S(1)}, u32[]{:S(2)}, u32[]{:S(2)}) %collective-permute-start.2) | collective-permute-done | bytes 36896 | tf_op jit(solution)/shard_map/ppermute | solution.py:253
  14.2 0.2 %collective-permute-start.4 = (f32[144,128]{1,0:T(8,128)S(1)}, f32[144,128]{1,0:T(8,128)S(1)}, u32[]{:S(2)}, u32[]{:S(2)}) collective-permute-start(f32[144,128]{1,0:T(8,128)S(1)} %pad_maximum_fusion), channel_id=1, source_target_pairs={{0,4},{4,0},{8,12},{12,8},{16,20},{20,16},{24,28},{28,24},{1,5},{5... | collective-permute-start | bytes 221192 | tf_op jit(solution)/shard_map/ppermute | solution.py:253
  14.5 2.1 %collective-permute-start.3 = (f32[144,128]{1,0:T(8,128)S(1)}, f32[144,128]{1,0:T(8,128)S(1)}, u32[]{:S(2)}, u32[]{:S(2)}) collective-permute-start(f32[144,128]{1,0:T(8,128)S(1)} %pad_maximum_fusion), channel_id=1, source_target_pairs={{0,20},{4,16},{8,28},{12,24},{16,4},{20,0},{24,12},{28,8},{1,21},{... | collective-permute-start | bytes 221192 | tf_op jit(solution)/shard_map/ppermute | solution.py:253
  16.6 0.0 copy-done
  16.6 0.1 constant_dynamic-slice_fusion.2
  16.7 0.8 %near.1.refs_4_ = f32[64,1152]{1,0:T(8,128)S(1)} custom-call(f32[8,128]{1,0:T(8,128)S(1)} %get-tuple-element.13.refs_0_, f32[8,128]{1,0:T(8,128)S(1)} %broadcast_in_dim.32.refs_1_, f32[64,10]{1,0:T(8,128)S(1)} %bitcast.17, f32[72,128]{1,0:T(8,128)S(1)} %collective-permute-done.2.refs_3_, f32[64,1152]{1,0:T(8,128)S(1)} %own.1.refs_4_), custom_call_target="tpu_custom_call" | custom-call | flops 150994944 | bytes 1048576 | tf_op jit(solution)/shard_map/near/pallas_call | solution.py:182
  17.5 0.0 collective-permute-done.4.refs_3_
  17.5 1.4 %middle.1.refs_4_ = f32[64,1152]{1,0:T(8,128)S(1)} custom-call(f32[8,128]{1,0:T(8,128)S(1)} %get-tuple-element.13.refs_0_, f32[8,128]{1,0:T(8,128)S(1)} %broadcast_in_dim.32.refs_1_, f32[64,10]{1,0:T(8,128)S(1)} %bitcast.18, f32[144,128]{1,0:T(8,128)S(1)} %collective-permute-done.4.refs_3_, f32[64,1152]{1,0:T(8,128)S(1)} %near.1.refs_4_), custom_call_target="tpu_custom_call" | custom-call | flops 301989888 | bytes 1048576 | tf_op jit(solution)/shard_map/middle/pallas_call | solution.py:182
  18.9 0.2 collective-permute-done.3.refs_3_
  19.1 0.1 collective-permute-start.5
  19.2 0.1 pad_maximum_fusion.4.refs_6_
  19.3 0.8 %next.1.refs_5_ = f32[64,1152]{1,0:T(8,128)S(1)} custom-call(f32[8,128]{1,0:T(8,128)S(1)} %get-tuple-element.13.refs_0_, f32[8,128]{1,0:T(8,128)S(1)} %broadcast_in_dim.32.refs_1_, f32[64,10]{1,0:T(8,128)S(1)} %bitcast.19, f32[144,128]{1,0:T(8,128)S(1)} %collective-permute-done.3.refs_3_, f32[64,1152]{1,0:T(8,128)S(1)} %middle.1.refs_4_), custom_call_target="tpu_custom_call" | custom-call | flops 150994944 | bytes 1048576 | tf_op jit(solution)/shard_map/next/pallas_call | solution.py:182
  20.2 0.2 collective-permute-done.5.refs_4_
  20.3 2.2 %far.1 = f32[3,16,128]{2,1,0:T(8,128)} custom-call(f32[8,128]{1,0:T(8,128)S(1)} %get-tuple-element.13.refs_0_, f32[8,128]{1,0:T(8,128)S(1)} %broadcast_in_dim.32.refs_1_, f32[64,10]{1,0:T(8,128)S(1)} %bitcast.20, f32[144,128]{1,0:T(8,128)S(1)} %collective-permute-done.3.refs_3_, f32[72,128]{1,0:T(8,128)S(1)} %collective-permute-done.5.refs_4_, ...), custom_call_target="tpu_custom_call" | custom-call | flops 301989888 | bytes 1048576 | tf_op jit(solution)/shard_map/far/pallas_call | solution.py:182
  (8 shorter events, 0.0 us)
Async XLA Ops:
  1.0 5.8 %collective-permute-start = (f32[1,32,128]{2,1,0:T(8,128)S(1)}, f32[1,32,128]{2,1,0:T(8,128)S(1)}, u32[]{:S(2)}, u32[]{:S(2)}) collective-permute-start(f32[1,32,128]{2,1,0:T(8,128)S(1)} %bitcast.21), channel_id=1, source_target_pairs={{0,2},{1,3},{2,0},{3,1},{4,6},{5,7},{6,4},{7,5},{8,10},{9,11},{10,... | collective-permute-start | bytes 49160 | tf_op jit(solution)/shard_map/ppermute | solution.py:253
  6.8 1.9 %copy-start.1 = (s32[1,7]{1,0:T(1,128)S(1)}, s32[1,7]{1,0:T(1,128)}, u32[]{:S(2)}) copy-start(s32[1,7]{1,0:T(1,128)} %param.11) | copy-start | bytes 88
  6.8 3.9 %collective-permute-start.1 = (f32[2,32,128]{2,1,0:T(8,128)S(1)}, f32[2,32,128]{2,1,0:T(8,128)S(1)}, u32[]{:S(2)}, u32[]{:S(2)}) collective-permute-start(f32[2,32,128]{2,1,0:T(8,128)S(1)} %pad_maximum_fusion.3), channel_id=1, source_target_pairs={{0,1},{1,0},{2,3},{3,2},{4,5},{5,4},{6,7},{7,6},{8,9},{9,8},{10,11... | collective-permute-start | bytes 98312 | tf_op jit(solution)/shard_map/ppermute | solution.py:253
  10.8 3.4 %collective-permute-start.2 = (f32[72,128]{1,0:T(8,128)S(1)}, f32[72,128]{1,0:T(8,128)S(1)}, u32[]{:S(2)}, u32[]{:S(2)}) collective-permute-start(f32[72,128]{1,0:T(8,128)S(1)} %pad_maximum_fusion.2.refs_3_), channel_id=1, source_target_pairs={{0,12},{4,8},{8,4},{12,0},{16,28},{20,24},{24,20},{28,16},{1,13},{... | collective-permute-start | bytes 110600 | tf_op jit(solution)/shard_map/ppermute | solution.py:253
  11.9 4.7 %copy-start = (f32[3,64,64]{2,1,0:T(8,128)S(1)}, f32[3,64,64]{2,1,0:T(8,128)}, u32[]{:S(2)}) copy-start(f32[3,64,64]{2,1,0:T(8,128)} %param.15) | copy-start | bytes 147460
  14.2 3.3 %collective-permute-start.4 = (f32[144,128]{1,0:T(8,128)S(1)}, f32[144,128]{1,0:T(8,128)S(1)}, u32[]{:S(2)}, u32[]{:S(2)}) collective-permute-start(f32[144,128]{1,0:T(8,128)S(1)} %pad_maximum_fusion), channel_id=1, source_target_pairs={{0,4},{4,0},{8,12},{12,8},{16,20},{20,16},{24,28},{28,24},{1,5},{5... | collective-permute-start | bytes 221192 | tf_op jit(solution)/shard_map/ppermute | solution.py:253
  14.5 4.6 %collective-permute-start.3 = (f32[144,128]{1,0:T(8,128)S(1)}, f32[144,128]{1,0:T(8,128)S(1)}, u32[]{:S(2)}, u32[]{:S(2)}) collective-permute-start(f32[144,128]{1,0:T(8,128)S(1)} %pad_maximum_fusion), channel_id=1, source_target_pairs={{0,20},{4,16},{8,28},{12,24},{16,4},{20,0},{24,12},{28,8},{1,21},{... | collective-permute-start | bytes 221192 | tf_op jit(solution)/shard_map/ppermute | solution.py:253
  19.1 1.2 %collective-permute-start.5 = (f32[72,128]{1,0:T(8,128)S(1)}, f32[72,128]{1,0:T(8,128)S(1)}, u32[]{:S(2)}, u32[]{:S(2)}) collective-permute-start(f32[72,128]{1,0:T(8,128)S(1)} %slice.11), channel_id=1, source_target_pairs={{0,4},{4,0},{8,12},{12,8},{16,20},{20,16},{24,28},{28,24},{1,5},{5... | collective-permute-start | bytes 110600 | tf_op jit(solution)/shard_map/ppermute | solution.py:253

commit v4 on v3

v4 whole, which is shorter than its diff:
```python
import functools
import math

import jax
import jax.numpy as jnp
from jax import lax
from jax.experimental import pallas as pl
from jax.experimental.pallas import tpu as pltpu
from jax.sharding import PartitionSpec as P


slab_width = 5.0 / 3.0
cross_width = 48.0
cut_radius = 5.0
soften = 0.25
components = 9
orders = ((0, 1), (1, 4), (4, 9))
lanes = 128
tile = 16

twice_cos_terms = (
    1.9999999781180455,
    -9.869602249726915,
    8.117389682486351,
    -2.670316860337427,
    0.4700596167989333,
    -0.05071796727719481,
    0.003187821366091919,
)
factors = (1.0, math.sqrt(3.0), math.sqrt(15.0))


def horner(terms, v):
    value = jnp.full_like(v, terms[-1])
    for term in terms[-2::-1]:
        value = value * v + term
    return value


def pair_rows(own, other, lengths, count, apart):
    shift = []
    for axis, length in enumerate(lengths):
        r = other[axis] - own[axis]
        shift.append(length * (r - jnp.round(r)))
    x, y, z = shift
    s = x * x + y * y + z * z + soften
    inverse = lax.rsqrt(s)
    square = s * (1.0 / cut_radius**2)
    sixth = square * square * square
    level = 0.5 * math.sqrt(2.0 / cut_radius)
    envelope = level + sixth * (
        square * (inverse * (48.0 * cut_radius * level) - 21.0 * level) - 28.0 * level
    )
    keep = square < 1.0
    if apart is not None:
        keep = jnp.logical_and(keep, apart)
    twice = horner(twice_cos_terms, square)
    rest = jnp.maximum(4.0 - twice * twice, 1e-12)
    sine = rest * lax.rsqrt(rest)
    first = jnp.where(keep, envelope, 0.0) * (sine * inverse)
    radial = [first, twice * first]
    while len(radial) < count:
        radial.append(twice * radial[-1] - radial[-2])
    x, y, z = x * inverse, y * inverse, z * inverse
    xx, yy = x * x, y * y
    harmonics = [
        None,
        x,
        y,
        z,
        x * y,
        y * z,
        z * z * (1.0 / math.sqrt(3.0)) - (xx + yy) * (0.5 / math.sqrt(3.0)),
        x * z,
        (xx - yy) * 0.5,
    ]
    radial = [r.astype(jnp.bfloat16) for r in radial[:count]]
    harmonics = [None if h is None else h.astype(jnp.bfloat16) for h in harmonics]
    return [[r if h is None else r * h for h in harmonics] for r in radial]


def pair_kernel(slabs, data_count, own_slab, first, last, box_x, count, *refs):
    refs = list(refs)
    pos_ref, act_ref = refs[:2]
    data = refs[2 : 2 + data_count]
    rest = refs[2 + data_count :]
    lengths = (box_x, cross_width, cross_width)
    own = [jnp.broadcast_to(pos_ref[axis : axis + 1, :], (tile, lanes)) for axis in range(3)]
    channels = rest[0].shape[0]
    lane = lax.broadcasted_iota(jnp.int32, (channels, lanes), 1)
    group, within = lane // tile, lax.rem(lane, tile)
    if first:
        par_ref = rest.pop(0)
        spread = jnp.broadcast_to(par_ref[:, 0:1], (channels, lanes))
        for n in range(1, count):
            spread = jnp.where(group == n, par_ref[:, n : n + 1], spread)
        centre = jnp.zeros((channels, lanes), jnp.float32)
        for kind in range(par_ref.shape[1] - count):
            here = pos_ref[3:4, :] == float(kind)
            centre = jnp.where(here, par_ref[:, count + kind : count + kind + 1], centre)
    else:
        acc_ref, spread_ref, centre_ref = rest.pop(0), rest.pop(0), rest.pop(0)
        spread = spread_ref[...]
    if last:
        mix_ref, out_ref, sum_ref = rest
    elif first:
        sum_ref, spread_ref, centre_ref = rest
        spread_ref[...] = spread
        centre_ref[...] = centre
    else:
        (sum_ref,) = rest
    part = None
    for which, base, index in slabs:
        ref = data[which]
        feats = ref[base : base + channels, :] * act_ref[index : index + 1, :]
        columns = ref[base + channels : base + channels + 8, :].T
        for pair in range(lanes // (2 * tile)):
            weights, tables = [], []
            for step in (2 * pair, 2 * pair + 1):
                picked = jnp.take_along_axis(feats, within + step * tile, axis=1)
                weights.append((spread * picked).astype(jnp.bfloat16))
                rows = slice(step * tile, (step + 1) * tile)
                other = [
                    jnp.broadcast_to(columns[rows, axis : axis + 1], (tile, lanes))
                    for axis in range(3)
                ]
                apart = None
                if index == own_slab:
                    apart = (
                        lax.broadcasted_iota(jnp.int32, (tile, lanes), 0) + step * tile
                    ) != lax.broadcasted_iota(jnp.int32, (tile, lanes), 1)
                tables += pair_rows(own, other, lengths, count, apart)
            stacked = jnp.concatenate([jnp.concatenate(row, axis=1) for row in tables], axis=0)
            product = jnp.dot(
                jnp.concatenate(weights, axis=1), stacked, preferred_element_type=jnp.float32
            )
            part = product if part is None else part + product
    sum_ref[...] = part if first else acc_ref[...] + part
    if not last:
        return
    if not first:
        centre = centre_ref[...]
    held = mix_ref.shape[1]
    for order, (start, stop) in enumerate(orders):
        mix = mix_ref[order] * factors[order]
        mix_high = mix.astype(jnp.bfloat16)
        mix_low = (mix - mix_high.astype(jnp.float32)).astype(jnp.bfloat16)
        features = [sum_ref[:, m * lanes : (m + 1) * lanes] * centre for m in range(start, stop)]
        features = features[0] if len(features) == 1 else jnp.concatenate(features, axis=1)
        high = features.astype(jnp.bfloat16)
        low = (features - high.astype(jnp.float32)).astype(jnp.bfloat16)
        both = jnp.dot(
            jnp.concatenate([mix_high, mix_low], axis=0), high, preferred_element_type=jnp.float32
        )
        mixed = both[:held] + both[held:]
        mixed = mixed + jnp.dot(mix_high, low, preferred_element_type=jnp.float32)
        total = None
        for m in range(stop - start):
            one = mixed[:, m * lanes : (m + 1) * lanes]
            total = one * one if total is None else total + one * one
        out_ref[order] = jnp.log1p(total)


def accumulate(pos, act, data, slabs, own_slab, box_x, count, start, mix=None):
    atoms = pos.shape[1]
    first, last = not isinstance(start, tuple), mix is not None
    channels = (start if first else start[1]).shape[0]
    operands = [pos, act, *data, *((start,) if first else start)]
    wide = jax.ShapeDtypeStruct((channels, components * atoms), jnp.float32)
    narrow = jax.ShapeDtypeStruct((channels, atoms), jnp.float32)
    if last:
        operands.append(mix)
        shapes = jax.ShapeDtypeStruct((len(orders), mix.shape[1], atoms), jnp.float32)
    else:
        shapes = [wide, narrow, narrow] if first else [wide]
    flops = 2 * channels * count * components * atoms * atoms * len(slabs)

    def body(*refs):
        pair_kernel(slabs, len(data), own_slab, first, last, box_x, count, *refs)

    whole = pl.BlockSpec(memory_space=pltpu.VMEM)
    result = pl.pallas_call(
        body,
        out_shape=shapes,
        in_specs=[whole] * len(operands),
        out_specs=whole if last else [whole] * len(shapes),
        scratch_shapes=[pltpu.VMEM(wide.shape, jnp.float32)] if last else [],
        cost_estimate=pl.CostEstimate(flops=flops, bytes_accessed=1 << 20, transcendentals=0),
        compiler_params=pltpu.CompilerParams(vmem_limit_bytes=16 << 20),
    )(*operands)
    return result if last else tuple(result) if first else (result[0], *start[1:])


def pack_kernel(box_x, *refs):
    sources, (out_ref, own_ref), held_refs = refs[:6], refs[6:8], refs[8:14]
    tile_ref, sems = refs[14:]
    copies = [
        pltpu.make_async_copy(source, held_ref, sems.at[i])
        for i, (source, held_ref) in enumerate(zip(sources, held_refs))
    ]
    for copy in copies:
        copy.start()
    feats_ref, species_ref, pos_ref, embed_ref, radial_ref, center_ref = held_refs
    held = feats_ref.shape[0]
    kinds, count = embed_ref.shape[0], radial_ref.shape[0]
    tile_ref[...] = jnp.zeros_like(tile_ref)
    out_ref[held:, :] = jnp.zeros((tile, lanes), jnp.float32)
    own_ref[...] = jnp.zeros_like(own_ref)
    for copy in copies:
        copy.wait()
    tile_ref[0:kinds, 0:held] = embed_ref[...]
    columns = tile_ref[...].T
    embedded = jnp.zeros(feats_ref.shape, jnp.float32)
    for kind in range(kinds):
        embedded = jnp.where(species_ref[...] == kind, columns[:held, kind : kind + 1], embedded)
    out_ref[0:held, :] = feats_ref[...] * embedded
    out_ref[held : held + count, 0:held] = radial_ref[...]
    out_ref[held + count : held + count + kinds, 0:held] = center_ref[...]
    for axis, length in enumerate((box_x, cross_width, cross_width)):
        own_ref[axis : axis + 1, :] = pos_ref[axis : axis + 1, :] * (1.0 / length)
    own_ref[3:4, :] = species_ref[...].astype(jnp.float32)


def pack(box_x, node_features, species, positions, species_embed, radial_weight, center_embed):
    held, atoms = node_features.shape
    operands = (
        node_features,
        species[None],
        positions,
        species_embed.T,
        radial_weight,
        center_embed.T,
    )
    operands = [pltpu.with_memory_space_constraint(x, pltpu.HBM) for x in operands]
    return pl.pallas_call(
        functools.partial(pack_kernel, box_x),
        out_shape=(
            jax.ShapeDtypeStruct((held + tile, atoms), jnp.float32),
            jax.ShapeDtypeStruct((8, atoms), jnp.float32),
        ),
        in_specs=[pl.BlockSpec(memory_space=pltpu.HBM)] * len(operands),
        out_specs=[pl.BlockSpec(memory_space=pltpu.VMEM)] * 2,
        scratch_shapes=[pltpu.VMEM(x.shape, x.dtype) for x in operands]
        + [pltpu.VMEM((8, lanes), jnp.float32), pltpu.SemaphoreType.DMA((len(operands),))],
        compiler_params=pltpu.CompilerParams(vmem_limit_bytes=1 << 20),
        name="pack",
    )(*operands)


def moved(value, axis, target):
    size = lax.axis_size(axis)
    return lax.ppermute(value, axis, [(i, target(i, size)) for i in range(size)])


def flipped(value, axis, bit):
    return moved(value, axis, lambda i, size: i ^ bit)


def shards(
    positions,
    species,
    node_features,
    block_mask,
    radial_weight,
    species_embed,
    center_embed,
    mix_weight,
):
    slab_count = lax.axis_size("blk")
    owner_count = lax.axis_size("chan")
    box_x = float(slab_count) * slab_width
    reach = (block_mask.shape[1] - 1) // 2
    count = radial_weight.shape[0]
    kinds = species_embed.shape[1]
    held, atoms = node_features.shape
    me = lax.axis_index("blk")
    owner = lax.axis_index("chan")

    owned, pos = pack(
        box_x, node_features, species, positions, species_embed, radial_weight, center_embed
    )
    owned = owned[None]
    bit = owner_count // 2
    flips = [0]
    while bit:
        owned = jnp.concatenate([owned, flipped(owned, "chan", bit)], axis=0)
        flips = flips + [f ^ bit for f in flips]
        bit //= 2
    channels = held * owner_count
    feats = owned[:, :held].reshape(channels, atoms)
    par = owned[:, held : held + count + kinds, :held].transpose(0, 2, 1)
    par = par.reshape(channels, count + kinds)
    mine = lax.dynamic_slice_in_dim(mix_weight, owner * held, held, 1)
    mix = jnp.concatenate(
        [lax.dynamic_slice_in_dim(mine, (owner ^ f) * held, held, 2) for f in flips], axis=2
    )

    bundle = jnp.concatenate([feats, pos], axis=0)
    depth = bundle.shape[0]

    def activity(places):
        offset = jnp.stack([lax.rem(p - me + reach + slab_count, slab_count) for p in places])
        at = offset[:, None] == jnp.arange(2 * reach + 1, dtype=jnp.int32)[None, :]
        value = jnp.sum(jnp.where(at, block_mask, 0), axis=1).astype(jnp.float32)
        return jnp.broadcast_to(value[:, None], (len(places), atoms))

    call = lambda act, data, slabs, start, mix=None: accumulate(
        pos, act, data, slabs, 0, box_x, count, start, mix
    )
    if slab_count == 2 * (reach + 1) == 8:
        act = activity([me ^ j for j in range(slab_count)])
        three = flipped(bundle, "blk", 3)
        acc = call(act, [bundle], [(0, 0, 0)], par)
        three, acc = lax.optimization_barrier((three, acc))
        pair = jnp.concatenate([bundle, three], axis=0)
        five = flipped(pair, "blk", 5)
        one = flipped(pair, "blk", 1)
        acc = call(act, [three], [(0, 0, 3)], acc)
        acc = call(act, [one], [(0, 0, 1), (0, depth, 2)], acc)
        five, acc = lax.optimization_barrier((five, acc))
        seven = flipped(five[depth:], "blk", 1)
        acc = call(act, [five], [(0, 0, 5)], acc)
        seven, acc = lax.optimization_barrier((seven, acc))
        return call(act, [five, seven], [(0, depth, 6), (1, 0, 7)], acc, mix)
    places = [0] + [k for h in range(1, reach + 1) for k in (h, -h)]
    act = activity([lax.rem(me + k + slab_count, slab_count) for k in places])
    act = jnp.pad(act, ((0, 8 - len(places)), (0, 0)))
    data = [bundle] + [
        moved(bundle, "blk", lambda i, size, k=k: (i - k) % size) for k in places[1:]
    ]
    return call(act, data, [(j, 0, j) for j in range(len(places))], par, mix)


def solution(mesh):
    return jax.shard_map(
        shards,
        mesh=mesh,
        in_specs=(
            P(None, "blk"),
            P("blk"),
            P("chan", "blk"),
            P("blk", None),
            P(None, "chan"),
            P("chan", None),
            P("chan", None),
            P(),
        ),
        out_specs=P(None, "chan", "blk"),
        check_vma=False,
    )
```

time: 22.8 us -> 22.5 us (0.987)
  Pallas kernels: 7.09 us -> 6.32 us
  waiting for transfers between devices: 6.08 us -> 6.56 us
    pallas_call x6, Pallas kernels: 7.09 us -> 6.32 us  [the longest x5 5.36 us: accumulate(): pl.pallas_call(body, out_shape=shapes, in_specs=[whole] * len(operands),...]
    ppermute x6, waiting for transfers between devices: 6.08 us -> 6.56 us  [moved(): lax.ppermute(value, axis, [(i, target(i, size)) for i in range(size)])]
  transfers between devices with their start and end apart: 6 -> 6, of which waited for: 5 -> 5; matrix products, arithmetic and copies ran while one was open for 3% -> 3% of each run, Pallas kernels for 17% -> 15%
where the time goes in v4:
time: 22.5 us; the launch traced here: 22.3 us
  starting transfers between devices  8.59 us (38%)
  waiting for transfers between devices  6.56 us (29%)
  Pallas kernels  6.32 us (28%)
  local copies, waits for them, and re-layouts  0.37 us (2%)
  other arithmetic  0.29 us (1%)
    ppermute x6, starting transfers between devices, moved(): lax.ppermute(value, axis, [(i, target(i, size)) for i in range(size)])  8.59 us
    ppermute x6, waiting for transfers between devices, moved(): lax.ppermute(value, axis, [(i, target(i, size)) for i in range(size)])  6.56 us
    pallas_call x5, Pallas kernels, accumulate(): pl.pallas_call(body, out_shape=shapes, in_specs=[whole] * len(operands),...  5.36 us
    pallas_call x1, Pallas kernels, pack(): pl.pallas_call(functools.partial(pack_kernel, box_x), out_shape=(jax.Shap...  0.96 us
  transfers between devices with their start and end apart: 6, of which 5 were waited for; matrix products, arithmetic and copies ran while one was open for 3% of the time, Pallas kernels for 15%

profile of v4, /device:TPU:0, one launch (start us, length us, event | category | flops | bytes accessed | tf_op | source)
XLA Modules:
  0.0 22.3 jit_solution(633315532516295103)
XLA Ops:
  0.0 1.0 %pack.1 = (f32[32,128]{1,0:T(8,128)S(1)}, f32[8,128]{1,0:T(8,128)S(1)}) custom-call(f32[16,128]{1,0:T(8,128)} %refs_0_.1, s32[1,128]{1,0:T(1,128)} %bitcast.24, f32[3,128]{1,0:T(4,128)} %refs_2_.1, f32[2,16]{1,0:T(2,128)} %bitcast.22, f32[8,16]{1,0:T(8,128)} %refs_4_.1, f32[2,16]{1,0:T(2,128)} %bitcast.23), custom_call_target="tpu_custom_call" | custom-call | tf_op jit(solution)/shard_map/pack/pallas_call | solution.py:235
  1.0 4.1 %collective-permute-start = (f32[1,32,128]{2,1,0:T(8,128)S(1)}, f32[1,32,128]{2,1,0:T(8,128)S(1)}, u32[]{:S(2)}, u32[]{:S(2)}) collective-permute-start(f32[1,32,128]{2,1,0:T(8,128)S(1)} %bitcast.16), channel_id=1, source_target_pairs={{0,2},{1,3},{2,0},{3,1},{4,6},{5,7},{6,4},{7,5},{8,10},{9,11},{10,... | collective-permute-start | bytes 49160 | tf_op jit(solution)/shard_map/ppermute | solution.py:252
  5.1 0.1 stack.31
  5.2 1.6 %collective-permute-done = f32[1,32,128]{2,1,0:T(8,128)S(1)} collective-permute-done((f32[1,32,128]{2,1,0:T(8,128)S(1)}, f32[1,32,128]{2,1,0:T(8,128)S(1)}, u32[]{:S(2)}, u32[]{:S(2)}) %collective-permute-start) | collective-permute-done | bytes 16416 | tf_op jit(solution)/shard_map/ppermute | solution.py:252
  6.8 0.0 copy-start.1
  6.8 1.9 %collective-permute-start.1 = (f32[2,32,128]{2,1,0:T(8,128)S(1)}, f32[2,32,128]{2,1,0:T(8,128)S(1)}, u32[]{:S(2)}, u32[]{:S(2)}) collective-permute-start(f32[2,32,128]{2,1,0:T(8,128)S(1)} %pad_maximum_fusion.3), channel_id=1, source_target_pairs={{0,1},{1,0},{2,3},{3,2},{4,5},{5,4},{6,7},{7,6},{8,9},{9,8},{10,11... | collective-permute-start | bytes 98312 | tf_op jit(solution)/shard_map/ppermute | solution.py:252
  8.7 0.0 copy-done.1
  8.7 0.2 select_reduce_fusion
  9.0 1.8 %collective-permute-done.1 = f32[2,32,128]{2,1,0:T(8,128)S(1)} collective-permute-done((f32[2,32,128]{2,1,0:T(8,128)S(1)}, f32[2,32,128]{2,1,0:T(8,128)S(1)}, u32[]{:S(2)}, u32[]{:S(2)}) %collective-permute-start.1) | collective-permute-done | bytes 32800 | tf_op jit(solution)/shard_map/ppermute | solution.py:252
  10.8 0.1 collective-permute-start.2
  10.9 0.1 copy.10
  11.0 0.1 broadcast_in_dim.32.refs_1_
  11.0 0.8 %shard_map.82 = (f32[64,1152]{1,0:T(8,128)S(1)}, f32[64,128]{1,0:T(8,128)S(1)}, f32[64,128]{1,0:T(8,128)S(1)}) custom-call(f32[8,128]{1,0:T(8,128)S(1)} %get-tuple-element.22.refs_0_, f32[8,128]{1,0:T(8,128)S(1)} %broadcast_in_dim.32.refs_1_, f32[72,128]{1,0:T(8,128)S(1)} %pad_maximum_fusion.2.refs_2_, f32[64,10]{1,0:T(8,128)S(1)} %bitcast.19), custom_call_target="tpu_custom_call" | custom-call | flops 150994944 | bytes 1048576 | tf_op jit(solution)/shard_map/pallas_call | solution.py:182
  11.8 0.0 copy-start
  11.8 2.4 %collective-permute-done.2.refs_2_ = f32[72,128]{1,0:T(8,128)S(1)} collective-permute-done((f32[72,128]{1,0:T(8,128)S(1)}, f32[72,128]{1,0:T(8,128)S(1)}, u32[]{:S(2)}, u32[]{:S(2)}) %collective-permute-start.2) | collective-permute-done | bytes 36896 | tf_op jit(solution)/shard_map/ppermute | solution.py:252
  14.2 0.2 %collective-permute-start.4 = (f32[144,128]{1,0:T(8,128)S(1)}, f32[144,128]{1,0:T(8,128)S(1)}, u32[]{:S(2)}, u32[]{:S(2)}) collective-permute-start(f32[144,128]{1,0:T(8,128)S(1)} %pad_maximum_fusion), channel_id=1, source_target_pairs={{0,4},{4,0},{8,12},{12,8},{16,20},{20,16},{24,28},{28,24},{1,5},{5... | collective-permute-start | bytes 221192 | tf_op jit(solution)/shard_map/ppermute | solution.py:252
  14.5 2.1 %collective-permute-start.3 = (f32[144,128]{1,0:T(8,128)S(1)}, f32[144,128]{1,0:T(8,128)S(1)}, u32[]{:S(2)}, u32[]{:S(2)}) collective-permute-start(f32[144,128]{1,0:T(8,128)S(1)} %pad_maximum_fusion), channel_id=1, source_target_pairs={{0,20},{4,16},{8,28},{12,24},{16,4},{20,0},{24,12},{28,8},{1,21},{... | collective-permute-start | bytes 221192 | tf_op jit(solution)/shard_map/ppermute | solution.py:252
  16.6 0.0 copy-done
  16.6 0.1 constant_dynamic-slice_fusion.2
  16.7 0.7 %shard_map.83.refs_3_ = f32[64,1152]{1,0:T(8,128)S(1)} custom-call(f32[8,128]{1,0:T(8,128)S(1)} %get-tuple-element.22.refs_0_, f32[8,128]{1,0:T(8,128)S(1)} %broadcast_in_dim.32.refs_1_, f32[72,128]{1,0:T(8,128)S(1)} %collective-permute-done.2.refs_2_, f32[64,1152]{1,0:T(8,128)S(1)} %get-tuple-element.28.refs_3_, ...), custom_call_target="tpu_custom_call" | custom-call | flops 150994944 | bytes 1048576 | tf_op jit(solution)/shard_map/pallas_call | solution.py:182
  17.4 0.0 collective-permute-done.4.refs_2_
  17.4 1.2 %shard_map.84.refs_3_ = f32[64,1152]{1,0:T(8,128)S(1)} custom-call(f32[8,128]{1,0:T(8,128)S(1)} %get-tuple-element.22.refs_0_, f32[8,128]{1,0:T(8,128)S(1)} %broadcast_in_dim.32.refs_1_, f32[144,128]{1,0:T(8,128)S(1)} %collective-permute-done.4.refs_2_, f32[64,1152]{1,0:T(8,128)S(1)} %shard_map.83.refs_3_, f32[64,128]{1,0:T(8,128)S(1)} %get-tuple-element.37.refs_4_.refs_5_, ...), custom_call_target="tpu_custom_call" | custom-call | flops 301989888 | bytes 1048576 | tf_op jit(solution)/shard_map/pallas_call | solution.py:182
  18.6 0.5 %collective-permute-done.3.refs_2_ = f32[144,128]{1,0:T(8,128)S(1)} collective-permute-done((f32[144,128]{1,0:T(8,128)S(1)}, f32[144,128]{1,0:T(8,128)S(1)}, u32[]{:S(2)}, u32[]{:S(2)}) %collective-permute-start.3) | collective-permute-done | bytes 73760 | tf_op jit(solution)/shard_map/ppermute | solution.py:252
  19.1 0.1 collective-permute-start.5
  19.2 0.1 pad_maximum_fusion.4.refs_7_
  19.3 0.7 %shard_map.85.refs_4_ = f32[64,1152]{1,0:T(8,128)S(1)} custom-call(f32[8,128]{1,0:T(8,128)S(1)} %get-tuple-element.22.refs_0_, f32[8,128]{1,0:T(8,128)S(1)} %broadcast_in_dim.32.refs_1_, f32[144,128]{1,0:T(8,128)S(1)} %collective-permute-done.3.refs_2_, f32[64,1152]{1,0:T(8,128)S(1)} %shard_map.84.refs_3_, f32[64,128]{1,0:T(8,128)S(1)} %get-tuple-element.37.refs_4_.refs_5_, ...), custom_call_target="tpu_custom_call" | custom-call | flops 150994944 | bytes 1048576 | tf_op jit(solution)/shard_map/pallas_call | solution.py:182
  20.0 0.3 %collective-permute-done.5.refs_3_ = f32[72,128]{1,0:T(8,128)S(1)} collective-permute-done((f32[72,128]{1,0:T(8,128)S(1)}, f32[72,128]{1,0:T(8,128)S(1)}, u32[]{:S(2)}, u32[]{:S(2)}) %collective-permute-start.5) | collective-permute-done | bytes 36896 | tf_op jit(solution)/shard_map/ppermute | solution.py:252
  20.3 1.9 %shard_map.86 = f32[3,16,128]{2,1,0:T(8,128)} custom-call(f32[8,128]{1,0:T(8,128)S(1)} %get-tuple-element.22.refs_0_, f32[8,128]{1,0:T(8,128)S(1)} %broadcast_in_dim.32.refs_1_, f32[144,128]{1,0:T(8,128)S(1)} %collective-permute-done.3.refs_2_, f32[72,128]{1,0:T(8,128)S(1)} %collective-permute-done.5.refs_3_, f32[64,1152]{1,0:T(8,128)S(1)} %shard_map.85.refs_4_, ...), custom_call_target="tpu_custom_call" | custom-call | flops 301989888 | bytes 1048576 | tf_op jit(solution)/shard_map/pallas_call | solution.py:182
  (8 shorter events, 0.0 us)
Async XLA Ops:
  1.0 5.8 %collective-permute-start = (f32[1,32,128]{2,1,0:T(8,128)S(1)}, f32[1,32,128]{2,1,0:T(8,128)S(1)}, u32[]{:S(2)}, u32[]{:S(2)}) collective-permute-start(f32[1,32,128]{2,1,0:T(8,128)S(1)} %bitcast.16), channel_id=1, source_target_pairs={{0,2},{1,3},{2,0},{3,1},{4,6},{5,7},{6,4},{7,5},{8,10},{9,11},{10,... | collective-permute-start | bytes 49160 | tf_op jit(solution)/shard_map/ppermute | solution.py:252
  6.8 1.9 %copy-start.1 = (s32[1,7]{1,0:T(1,128)S(1)}, s32[1,7]{1,0:T(1,128)}, u32[]{:S(2)}) copy-start(s32[1,7]{1,0:T(1,128)} %param.11) | copy-start | bytes 88
  6.8 3.9 %collective-permute-start.1 = (f32[2,32,128]{2,1,0:T(8,128)S(1)}, f32[2,32,128]{2,1,0:T(8,128)S(1)}, u32[]{:S(2)}, u32[]{:S(2)}) collective-permute-start(f32[2,32,128]{2,1,0:T(8,128)S(1)} %pad_maximum_fusion.3), channel_id=1, source_target_pairs={{0,1},{1,0},{2,3},{3,2},{4,5},{5,4},{6,7},{7,6},{8,9},{9,8},{10,11... | collective-permute-start | bytes 98312 | tf_op jit(solution)/shard_map/ppermute | solution.py:252
  10.8 3.4 %collective-permute-start.2 = (f32[72,128]{1,0:T(8,128)S(1)}, f32[72,128]{1,0:T(8,128)S(1)}, u32[]{:S(2)}, u32[]{:S(2)}) collective-permute-start(f32[72,128]{1,0:T(8,128)S(1)} %pad_maximum_fusion.2.refs_2_), channel_id=1, source_target_pairs={{0,12},{4,8},{8,4},{12,0},{16,28},{20,24},{24,20},{28,16},{1,13},{... | collective-permute-start | bytes 110600 | tf_op jit(solution)/shard_map/ppermute | solution.py:252
  11.8 4.8 %copy-start = (f32[3,64,64]{2,1,0:T(8,128)S(1)}, f32[3,64,64]{2,1,0:T(8,128)}, u32[]{:S(2)}) copy-start(f32[3,64,64]{2,1,0:T(8,128)} %param.15) | copy-start | bytes 147460
  14.2 3.2 %collective-permute-start.4 = (f32[144,128]{1,0:T(8,128)S(1)}, f32[144,128]{1,0:T(8,128)S(1)}, u32[]{:S(2)}, u32[]{:S(2)}) collective-permute-start(f32[144,128]{1,0:T(8,128)S(1)} %pad_maximum_fusion), channel_id=1, source_target_pairs={{0,4},{4,0},{8,12},{12,8},{16,20},{20,16},{24,28},{28,24},{1,5},{5... | collective-permute-start | bytes 221192 | tf_op jit(solution)/shard_map/ppermute | solution.py:252
  14.5 4.6 %collective-permute-start.3 = (f32[144,128]{1,0:T(8,128)S(1)}, f32[144,128]{1,0:T(8,128)S(1)}, u32[]{:S(2)}, u32[]{:S(2)}) collective-permute-start(f32[144,128]{1,0:T(8,128)S(1)} %pad_maximum_fusion), channel_id=1, source_target_pairs={{0,20},{4,16},{8,28},{12,24},{16,4},{20,0},{24,12},{28,8},{1,21},{... | collective-permute-start | bytes 221192 | tf_op jit(solution)/shard_map/ppermute | solution.py:252
  19.1 1.2 %collective-permute-start.5 = (f32[72,128]{1,0:T(8,128)S(1)}, f32[72,128]{1,0:T(8,128)S(1)}, u32[]{:S(2)}, u32[]{:S(2)}) collective-permute-start(f32[72,128]{1,0:T(8,128)S(1)} %slice.11), channel_id=1, source_target_pairs={{0,4},{4,0},{8,12},{12,8},{16,20},{20,16},{24,28},{28,24},{1,5},{5... | collective-permute-start | bytes 110600 | tf_op jit(solution)/shard_map/ppermute | solution.py:252

commit v5 on v4

--- a/solution.py
+++ b/solution.py
@@ -110,10 +110,11 @@
     else:
         (sum_ref,) = rest
     part = None
-    for which, base, index in slabs:
-        ref = data[which]
-        feats = ref[base : base + channels, :] * act_ref[index : index + 1, :]
-        columns = ref[base + channels : base + channels + 8, :].T
+    for pieces, (where, base), index in slabs:
+        feats = [data[which][at : at + channels // len(pieces), :] for which, at in pieces]
+        feats = feats[0] if len(feats) == 1 else jnp.concatenate(feats, axis=0)
+        feats = feats * act_ref[index : index + 1, :]
+        columns = data[where][base : base + 8, :].T
         for pair in range(lanes // (2 * tile)):
             weights, tables = [], []
             for step in (2 * pair, 2 * pair + 1):
@@ -256,6 +257,14 @@
     return moved(value, axis, lambda i, size: i ^ bit)
 
 
+def crossed(value, bit):
+    blocks, owners = lax.axis_size("blk"), lax.axis_size("chan")
+    pairs = [
+        (b * owners + c, (b ^ 1) * owners + (c ^ bit)) for b in range(blocks) for c in range(owners)
+    ]
+    return lax.ppermute(value, ("blk", "chan"), pairs)
+
+
 def shards(
     positions,
     species,
@@ -279,24 +288,25 @@
     owned, pos = pack(
         box_x, node_features, species, positions, species_embed, radial_weight, center_embed
     )
-    owned = owned[None]
-    bit = owner_count // 2
-    flips = [0]
-    while bit:
-        owned = jnp.concatenate([owned, flipped(owned, "chan", bit)], axis=0)
-        flips = flips + [f ^ bit for f in flips]
-        bit //= 2
     channels = held * owner_count
-    feats = owned[:, :held].reshape(channels, atoms)
-    par = owned[:, held : held + count + kinds, :held].transpose(0, 2, 1)
-    par = par.reshape(channels, count + kinds)
+    crossing = slab_count == 2 * (reach + 1) == 8 and owner_count == 4
+    if crossing:
+        far = crossed(owned, 2)
+        both = crossed(jnp.concatenate([owned, far], axis=0), 1)
+        size = owned.shape[0]
+        blocks, flips = [owned, both[size:], far, both[:size]], [0, 3, 2, 1]
+    else:
+        blocks, flips, bit = [owned], [0], owner_count // 2
+        while bit:
+            blocks = blocks + [flipped(block, "chan", bit) for block in blocks]
+            flips = flips + [f ^ bit for f in flips]
+            bit //= 2
+    bundle = jnp.concatenate([block[:held] for block in blocks] + [pos], axis=0)
+    par = jnp.concatenate([block[held : held + count + kinds, :held].T for block in blocks], axis=0)
     mine = lax.dynamic_slice_in_dim(mix_weight, owner * held, held, 1)
     mix = jnp.concatenate(
         [lax.dynamic_slice_in_dim(mine, (owner ^ f) * held, held, 2) for f in flips], axis=2
     )
-
-    bundle = jnp.concatenate([feats, pos], axis=0)
-    depth = bundle.shape[0]
 
     def activity(places):
         offset = jnp.stack([lax.rem(p - me + reach + slab_count, slab_count) for p in places])
@@ -307,28 +317,34 @@
     call = lambda act, data, slabs, start, mix=None: accumulate(
         pos, act, data, slabs, 0, box_x, count, start, mix
     )
-    if slab_count == 2 * (reach + 1) == 8:
+    if crossing:
         act = activity([me ^ j for j in range(slab_count)])
+        half = channels // 2
+        mixed = lambda a, b, index: (((a, 0), (b, half)), (a, channels), index)
         three = flipped(bundle, "blk", 3)
-        acc = call(act, [bundle], [(0, 0, 0)], par)
-        three, acc = lax.optimization_barrier((three, acc))
-        pair = jnp.concatenate([bundle, three], axis=0)
+        one = flipped(bundle, "blk", 1)
+        acc = call(act, [bundle, one], [mixed(0, 1, 0)], par)
+        three, one, acc = lax.optimization_barrier((three, one, acc))
+        pair = jnp.concatenate([bundle[:half], one[half:channels], pos, three], axis=0)
         five = flipped(pair, "blk", 5)
-        one = flipped(pair, "blk", 1)
-        acc = call(act, [three], [(0, 0, 3)], acc)
-        acc = call(act, [one], [(0, 0, 1), (0, depth, 2)], acc)
+        two = flipped(three, "blk", 1)
+        acc = call(act, [one, bundle], [mixed(0, 1, 1)], acc)
+        acc = call(act, [three, two], [mixed(0, 1, 3), mixed(1, 0, 2)], acc)
         five, acc = lax.optimization_barrier((five, acc))
-        seven = flipped(five[depth:], "blk", 1)
-        acc = call(act, [five], [(0, 0, 5)], acc)
+        depth = bundle.shape[0]
+        five, six = five[:depth], five[depth:]
+        seven = flipped(six, "blk", 1)
+        acc = call(act, [five], [mixed(0, 0, 5)], acc)
         seven, acc = lax.optimization_barrier((seven, acc))
-        return call(act, [five, seven], [(0, depth, 6), (1, 0, 7)], acc, mix)
+        return call(act, [six, seven], [mixed(0, 1, 6), mixed(1, 0, 7)], acc, mix)
     places = [0] + [k for h in range(1, reach + 1) for k in (h, -h)]
     act = activity([lax.rem(me + k + slab_count, slab_count) for k in places])
     act = jnp.pad(act, ((0, 8 - len(places)), (0, 0)))
     data = [bundle] + [
         moved(bundle, "blk", lambda i, size, k=k: (i - k) % size) for k in places[1:]
     ]
-    return call(act, data, [(j, 0, j) for j in range(len(places))], par, mix)
+    slabs = [(((j, 0),), (j, channels), j) for j in range(len(places))]
+    return call(act, data, slabs, par, mix)
 
 
 def solution(mesh):

time: 22.5 us -> 21.2 us (0.942)
  waiting for transfers between devices: 6.56 us -> 3.44 us
  starting transfers between devices: 8.59 us -> 9.7 us
  local copies, waits for them, and re-layouts: 0.37 us -> 1.04 us
    ppermute x0 -> x2, starting transfers between devices: none -> 5.46 us  [crossed(): return lax.ppermute(value, ('blk', 'chan'), pairs)]
    ppermute x6 -> x5, waiting for transfers between devices: 6.56 us -> 1.38 us  [moved(): lax.ppermute(value, axis, [(i, target(i, size)) for i in range(size)])]
    ppermute x6 -> x5, starting transfers between devices: 8.59 us -> 4.24 us  [moved(): lax.ppermute(value, axis, [(i, target(i, size)) for i in range(size)])]
    ppermute x0 -> x2, waiting for transfers between devices: none -> 2.06 us  [crossed(): return lax.ppermute(value, ('blk', 'chan'), pairs)]
    unnamed x4 -> x10, local copies, waits for them, and re-layouts: 0.01 us -> 0.68 us
  transfers between devices with their start and end apart: 6 -> 7, of which waited for: 5 -> 5; matrix products, arithmetic and copies ran while one was open for 3% -> 3% of each run, Pallas kernels for 15% -> 16%
where the time goes in v5:
time: 21.2 us; the launch traced here: 21 us
  starting transfers between devices  9.7 us (46%)
  Pallas kernels  6.31 us (30%)
  waiting for transfers between devices  3.44 us (16%)
  local copies, waits for them, and re-layouts  1.04 us (5%)
  other arithmetic  0.35 us (2%)
    ppermute x2, starting transfers between devices, crossed(): return lax.ppermute(value, ('blk', 'chan'), pairs)  5.46 us
    pallas_call x5, Pallas kernels, accumulate(): pl.pallas_call(body, out_shape=shapes, in_specs=[whole] * len(operands),...  5.35 us
    ppermute x5, starting transfers between devices, moved(): lax.ppermute(value, axis, [(i, target(i, size)) for i in range(size)])  4.24 us
    ppermute x2, waiting for transfers between devices, crossed(): return lax.ppermute(value, ('blk', 'chan'), pairs)  2.06 us
    ppermute x5, waiting for transfers between devices, moved(): lax.ppermute(value, axis, [(i, target(i, size)) for i in range(size)])  1.38 us
    pallas_call x1, Pallas kernels, pack(): pl.pallas_call(functools.partial(pack_kernel, box_x), out_shape=(jax.Shap...  0.96 us
    unnamed x10, local copies, waits for them, and re-layouts  0.68 us
  transfers between devices with their start and end apart: 7, of which 5 were waited for; matrix products, arithmetic and copies ran while one was open for 3% of the time, Pallas kernels for 16%

profile of v5, /device:TPU:0, one launch (start us, length us, event | category | flops | bytes accessed | tf_op | source)
XLA Modules:
  0.0 21.0 jit_solution(16927983412525224811)
XLA Ops:
  0.0 1.0 %pack.1 = (f32[32,128]{1,0:T(8,128)S(1)}, f32[8,128]{1,0:T(8,128)S(1)}) custom-call(f32[16,128]{1,0:T(8,128)} %refs_0_.1, s32[1,128]{1,0:T(1,128)} %bitcast.21, f32[3,128]{1,0:T(4,128)} %refs_2_.1, f32[2,16]{1,0:T(2,128)} %bitcast.19, f32[8,16]{1,0:T(8,128)} %refs_4_.1, f32[2,16]{1,0:T(2,128)} %bitcast.20), custom_call_target="tpu_custom_call" | custom-call | tf_op jit(solution)/shard_map/pack/pallas_call | solution.py:236
  1.0 3.6 %collective-permute-start = (f32[32,128]{1,0:T(8,128)S(1)}, f32[32,128]{1,0:T(8,128)S(1)}, u32[]{:S(2)}, u32[]{:S(2)}) collective-permute-start(f32[32,128]{1,0:T(8,128)S(1)} %get-tuple-element.24), channel_id=1, source_target_pairs={{0,6},{1,7},{2,4},{3,5},{4,2},{5,3},{6,0},{7,1},{8,14},{9,15},{10,... | collective-permute-start | bytes 49160 | tf_op jit(solution)/shard_map/ppermute | solution.py:265
  4.5 0.1 stack.31
  4.6 0.0 copy-start.1
  4.6 0.7 %copy-done.1 = s32[1,7]{1,0:T(1,128)S(1)} copy-done((s32[1,7]{1,0:T(1,128)S(1)}, s32[1,7]{1,0:T(1,128)}, u32[]{:S(2)}) %copy-start.1) | copy-done | bytes 52
  5.3 0.2 select_reduce_fusion
  5.5 0.5 %collective-permute-done = f32[32,128]{1,0:T(8,128)S(1)} collective-permute-done((f32[32,128]{1,0:T(8,128)S(1)}, f32[32,128]{1,0:T(8,128)S(1)}, u32[]{:S(2)}, u32[]{:S(2)}) %collective-permute-start) | collective-permute-done | bytes 16416 | tf_op jit(solution)/shard_map/ppermute | solution.py:265
  6.0 1.9 %collective-permute-start.1 = (f32[64,128]{1,0:T(8,128)S(1)}, f32[64,128]{1,0:T(8,128)S(1)}, u32[]{:S(2)}, u32[]{:S(2)}) collective-permute-start(f32[64,128]{1,0:T(8,128)S(1)} %pad_maximum_fusion), channel_id=1, source_target_pairs={{0,5},{1,4},{2,7},{3,6},{4,1},{5,0},{6,3},{7,2},{8,13},{9,12},{10,... | collective-permute-start | bytes 98312 | tf_op jit(solution)/shard_map/ppermute | solution.py:265
  7.9 1.6 %collective-permute-done.1 = f32[64,128]{1,0:T(8,128)S(1)} collective-permute-done((f32[64,128]{1,0:T(8,128)S(1)}, f32[64,128]{1,0:T(8,128)S(1)}, u32[]{:S(2)}, u32[]{:S(2)}) %collective-permute-start.1) | collective-permute-done | bytes 32800 | tf_op jit(solution)/shard_map/ppermute | solution.py:265
  9.5 0.6 %collective-permute-start.3 = (f32[72,128]{1,0:T(8,128)S(1)}, f32[72,128]{1,0:T(8,128)S(1)}, u32[]{:S(2)}, u32[]{:S(2)}) collective-permute-start(f32[72,128]{1,0:T(8,128)S(1)} %constant_dynamic-update-slice_fusion.refs_2_.refs_3_), channel_id=1, source_target_pairs={{0,4},{4,0},{8,12},{12,8},{16,20},{20,16},{24,28},{28,24},{1,5},{5... | collective-permute-start | bytes 110600 | tf_op jit(solution)/shard_map/ppermute | solution.py:253
  10.1 1.6 %collective-permute-start.2 = (f32[72,128]{1,0:T(8,128)S(1)}, f32[72,128]{1,0:T(8,128)S(1)}, u32[]{:S(2)}, u32[]{:S(2)}) collective-permute-start(f32[72,128]{1,0:T(8,128)S(1)} %constant_dynamic-update-slice_fusion.refs_2_.refs_3_), channel_id=1, source_target_pairs={{0,12},{4,8},{8,4},{12,0},{16,28},{20,24},{24,20},{28,16},{1,13},{... | collective-permute-start | bytes 110600 | tf_op jit(solution)/shard_map/ppermute | solution.py:253
  11.7 0.1 pad_maximum_fusion.2
  11.7 0.1 copy.10.refs_4_
  11.8 0.0 collective-permute-done.3.refs_3_.refs_2_
  11.8 0.1 broadcast_in_dim.29.refs_1_
  11.9 0.8 %shard_map.82 = (f32[64,1152]{1,0:T(8,128)S(1)}, f32[64,128]{1,0:T(8,128)S(1)}, f32[64,128]{1,0:T(8,128)S(1)}) custom-call(f32[8,128]{1,0:T(8,128)S(1)} %get-tuple-element.23.refs_0_, f32[8,128]{1,0:T(8,128)S(1)} %broadcast_in_dim.29.refs_1_, f32[72,128]{1,0:T(8,128)S(1)} %constant_dynamic-update-slice_fusion.refs_2_.refs_3_, ...), custom_call_target="tpu_custom_call" | custom-call | flops 150994944 | bytes 1048576 | tf_op jit(solution)/shard_map/pallas_call | solution.py:183
  12.7 0.0 copy-start
  12.7 0.9 %collective-permute-done.2.refs_2_ = f32[72,128]{1,0:T(8,128)S(1)} collective-permute-done((f32[72,128]{1,0:T(8,128)S(1)}, f32[72,128]{1,0:T(8,128)S(1)}, u32[]{:S(2)}, u32[]{:S(2)}) %collective-permute-start.2) | collective-permute-done | bytes 36896 | tf_op jit(solution)/shard_map/ppermute | solution.py:253
  13.6 0.1 collective-permute-start.5
  13.7 1.6 %collective-permute-start.4 = (f32[144,128]{1,0:T(8,128)S(1)}, f32[144,128]{1,0:T(8,128)S(1)}, u32[]{:S(2)}, u32[]{:S(2)}) collective-permute-start(f32[144,128]{1,0:T(8,128)S(1)} %constant_dynamic-update-slice_fusion.5), channel_id=1, source_target_pairs={{0,20},{4,16},{8,28},{12,24},{16,4},{20,0},{24,12},{28,8},{1,21},{... | collective-permute-start | bytes 221192 | tf_op jit(solution)/shard_map/ppermute | solution.py:253
  15.3 0.0 copy-done
  15.3 0.1 constant_dynamic-slice_fusion.2
  15.4 0.7 %shard_map.83.refs_4_ = f32[64,1152]{1,0:T(8,128)S(1)} custom-call(f32[8,128]{1,0:T(8,128)S(1)} %get-tuple-element.23.refs_0_, f32[8,128]{1,0:T(8,128)S(1)} %broadcast_in_dim.29.refs_1_, f32[72,128]{1,0:T(8,128)S(1)} %collective-permute-done.3.refs_3_.refs_2_, f32[72,128]{1,0:T(8,128)S(1)} %constant_dynamic-update-slice_fusion.refs_2_.refs_3_, ...), custom_call_target="tpu_custom_call" | custom-call | flops 150994944 | bytes 1048576 | tf_op jit(solution)/shard_map/pallas_call | solution.py:183
  16.1 0.0 collective-permute-done.5.refs_3_
  16.1 1.2 %shard_map.84.refs_3_ = f32[64,1152]{1,0:T(8,128)S(1)} custom-call(f32[8,128]{1,0:T(8,128)S(1)} %get-tuple-element.23.refs_0_, f32[8,128]{1,0:T(8,128)S(1)} %broadcast_in_dim.29.refs_1_, f32[72,128]{1,0:T(8,128)S(1)} %collective-permute-done.2.refs_2_, f32[72,128]{1,0:T(8,128)S(1)} %collective-permute-done.5.refs_3_, f32[64,1152]{1,0:T(8,128)S(1)} %shard_map.83.refs_4_, ...), custom_call_target="tpu_custom_call" | custom-call | flops 301989888 | bytes 1048576 | tf_op jit(solution)/shard_map/pallas_call | solution.py:183
  17.3 0.5 %collective-permute-done.4 = f32[144,128]{1,0:T(8,128)S(1)} collective-permute-done((f32[144,128]{1,0:T(8,128)S(1)}, f32[144,128]{1,0:T(8,128)S(1)}, u32[]{:S(2)}, u32[]{:S(2)}) %collective-permute-start.4) | collective-permute-done | bytes 73760 | tf_op jit(solution)/shard_map/ppermute | solution.py:253
  17.8 0.4 %collective-permute-start.6 = (f32[72,128]{1,0:T(8,128)S(1)}, f32[72,128]{1,0:T(8,128)S(1)}, u32[]{:S(2)}, u32[]{:S(2)}) collective-permute-start(f32[72,128]{1,0:T(8,128)S(1)} %get-tuple-element.46.refs_2_), channel_id=1, source_target_pairs={{0,4},{4,0},{8,12},{12,8},{16,20},{20,16},{24,28},{28,24},{1,5},{5... | collective-permute-start | bytes 110600 | tf_op jit(solution)/shard_map/ppermute | solution.py:253
  18.2 0.1 pad_maximum_fusion.1.refs_7_
  18.3 0.7 %shard_map.85.refs_4_ = f32[64,1152]{1,0:T(8,128)S(1)} custom-call(f32[8,128]{1,0:T(8,128)S(1)} %get-tuple-element.23.refs_0_, f32[8,128]{1,0:T(8,128)S(1)} %broadcast_in_dim.29.refs_1_, f32[72,128]{1,0:T(8,128)S(1)} %get-tuple-element.45.refs_2_, f32[64,1152]{1,0:T(8,128)S(1)} %shard_map.84.refs_3_, f32[64,128]{1,0:T(8,128)S(1)} %get-tuple-element.39.refs_5_.refs_4_, ...), custom_call_target="tpu_custom_call" | custom-call | flops 150994944 | bytes 1048576 | tf_op jit(solution)/shard_map/pallas_call | solution.py:183
  19.0 0.1 collective-permute-done.6.refs_3_
  19.0 1.9 %shard_map.86 = f32[3,16,128]{2,1,0:T(8,128)} custom-call(f32[8,128]{1,0:T(8,128)S(1)} %get-tuple-element.23.refs_0_, f32[8,128]{1,0:T(8,128)S(1)} %broadcast_in_dim.29.refs_1_, f32[72,128]{1,0:T(8,128)S(1)} %get-tuple-element.46.refs_2_, f32[72,128]{1,0:T(8,128)S(1)} %collective-permute-done.6.refs_3_, f32[64,1152]{1,0:T(8,128)S(1)} %shard_map.85.refs_4_, ...), custom_call_target="tpu_custom_call" | custom-call | flops 301989888 | bytes 1048576 | tf_op jit(solution)/shard_map/pallas_call | solution.py:183
  (14 shorter events, 0.0 us)
Async XLA Ops:
  1.0 5.0 %collective-permute-start = (f32[32,128]{1,0:T(8,128)S(1)}, f32[32,128]{1,0:T(8,128)S(1)}, u32[]{:S(2)}, u32[]{:S(2)}) collective-permute-start(f32[32,128]{1,0:T(8,128)S(1)} %get-tuple-element.24), channel_id=1, source_target_pairs={{0,6},{1,7},{2,4},{3,5},{4,2},{5,3},{6,0},{7,1},{8,14},{9,15},{10,... | collective-permute-start | bytes 49160 | tf_op jit(solution)/shard_map/ppermute | solution.py:265
  4.6 0.7 %copy-start.1 = (s32[1,7]{1,0:T(1,128)S(1)}, s32[1,7]{1,0:T(1,128)}, u32[]{:S(2)}) copy-start(s32[1,7]{1,0:T(1,128)} %param.11) | copy-start | bytes 88
  6.0 3.5 %collective-permute-start.1 = (f32[64,128]{1,0:T(8,128)S(1)}, f32[64,128]{1,0:T(8,128)S(1)}, u32[]{:S(2)}, u32[]{:S(2)}) collective-permute-start(f32[64,128]{1,0:T(8,128)S(1)} %pad_maximum_fusion), channel_id=1, source_target_pairs={{0,5},{1,4},{2,7},{3,6},{4,1},{5,0},{6,3},{7,2},{8,13},{9,12},{10,... | collective-permute-start | bytes 98312 | tf_op jit(solution)/shard_map/ppermute | solution.py:265
  9.5 2.4 %collective-permute-start.3 = (f32[72,128]{1,0:T(8,128)S(1)}, f32[72,128]{1,0:T(8,128)S(1)}, u32[]{:S(2)}, u32[]{:S(2)}) collective-permute-start(f32[72,128]{1,0:T(8,128)S(1)} %constant_dynamic-update-slice_fusion.refs_2_.refs_3_), channel_id=1, source_target_pairs={{0,4},{4,0},{8,12},{12,8},{16,20},{20,16},{24,28},{28,24},{1,5},{5... | collective-permute-start | bytes 110600 | tf_op jit(solution)/shard_map/ppermute | solution.py:253
  10.1 3.5 %collective-permute-start.2 = (f32[72,128]{1,0:T(8,128)S(1)}, f32[72,128]{1,0:T(8,128)S(1)}, u32[]{:S(2)}, u32[]{:S(2)}) collective-permute-start(f32[72,128]{1,0:T(8,128)S(1)} %constant_dynamic-update-slice_fusion.refs_2_.refs_3_), channel_id=1, source_target_pairs={{0,12},{4,8},{8,4},{12,0},{16,28},{20,24},{24,20},{28,16},{1,13},{... | collective-permute-start | bytes 110600 | tf_op jit(solution)/shard_map/ppermute | solution.py:253
  12.7 2.6 %copy-start = (f32[3,64,64]{2,1,0:T(8,128)S(1)}, f32[3,64,64]{2,1,0:T(8,128)}, u32[]{:S(2)}) copy-start(f32[3,64,64]{2,1,0:T(8,128)} %param.15) | copy-start | bytes 147460
  13.6 2.5 %collective-permute-start.5 = (f32[72,128]{1,0:T(8,128)S(1)}, f32[72,128]{1,0:T(8,128)S(1)}, u32[]{:S(2)}, u32[]{:S(2)}) collective-permute-start(f32[72,128]{1,0:T(8,128)S(1)} %collective-permute-done.2.refs_2_), channel_id=1, source_target_pairs={{0,4},{4,0},{8,12},{12,8},{16,20},{20,16},{24,28},{28,24},{1,5},{5... | collective-permute-start | bytes 110600 | tf_op jit(solution)/shard_map/ppermute | solution.py:253
  13.7 4.1 %collective-permute-start.4 = (f32[144,128]{1,0:T(8,128)S(1)}, f32[144,128]{1,0:T(8,128)S(1)}, u32[]{:S(2)}, u32[]{:S(2)}) collective-permute-start(f32[144,128]{1,0:T(8,128)S(1)} %constant_dynamic-update-slice_fusion.5), channel_id=1, source_target_pairs={{0,20},{4,16},{8,28},{12,24},{16,4},{20,0},{24,12},{28,8},{1,21},{... | collective-permute-start | bytes 221192 | tf_op jit(solution)/shard_map/ppermute | solution.py:253
  17.8 1.3 %collective-permute-start.6 = (f32[72,128]{1,0:T(8,128)S(1)}, f32[72,128]{1,0:T(8,128)S(1)}, u32[]{:S(2)}, u32[]{:S(2)}) collective-permute-start(f32[72,128]{1,0:T(8,128)S(1)} %get-tuple-element.46.refs_2_), channel_id=1, source_target_pairs={{0,4},{4,0},{8,12},{12,8},{16,20},{20,16},{24,28},{28,24},{1,5},{5... | collective-permute-start | bytes 110600 | tf_op jit(solution)/shard_map/ppermute | solution.py:253

commit v6 on v5

--- a/solution.py
+++ b/solution.py
@@ -87,33 +87,20 @@
     lengths = (box_x, cross_width, cross_width)
     own = [jnp.broadcast_to(pos_ref[axis : axis + 1, :], (tile, lanes)) for axis in range(3)]
     channels = rest[0].shape[0]
-    lane = lax.broadcasted_iota(jnp.int32, (channels, lanes), 1)
-    group, within = lane // tile, lax.rem(lane, tile)
-    if first:
-        par_ref = rest.pop(0)
-        spread = jnp.broadcast_to(par_ref[:, 0:1], (channels, lanes))
-        for n in range(1, count):
-            spread = jnp.where(group == n, par_ref[:, n : n + 1], spread)
-        centre = jnp.zeros((channels, lanes), jnp.float32)
-        for kind in range(par_ref.shape[1] - count):
-            here = pos_ref[3:4, :] == float(kind)
-            centre = jnp.where(here, par_ref[:, count + kind : count + kind + 1], centre)
-    else:
-        acc_ref, spread_ref, centre_ref = rest.pop(0), rest.pop(0), rest.pop(0)
-        spread = spread_ref[...]
+    within = lax.rem(lax.broadcasted_iota(jnp.int32, (channels, lanes), 1), tile)
+    spread_ref, centre_ref = rest.pop(0), rest.pop(0)
+    spread = spread_ref[...]
+    if not first:
+        acc_ref = rest.pop(0)
     if last:
         mix_ref, out_ref, sum_ref = rest
-    elif first:
-        sum_ref, spread_ref, centre_ref = rest
-        spread_ref[...] = spread
-        centre_ref[...] = centre
     else:
         (sum_ref,) = rest
     part = None
     for pieces, (where, base), index in slabs:
         feats = [data[which][at : at + channels // len(pieces), :] for which, at in pieces]
         feats = feats[0] if len(feats) == 1 else jnp.concatenate(feats, axis=0)
-        feats = feats * act_ref[index : index + 1, :]
+        feats = feats * act_ref[index : index + 1, 0:1]
         columns = data[where][base : base + 8, :].T
         for pair in range(lanes // (2 * tile)):
             weights, tables = [], []
@@ -139,8 +126,7 @@
     sum_ref[...] = part if first else acc_ref[...] + part
     if not last:
         return
-    if not first:
-        centre = centre_ref[...]
+    centre = centre_ref[...]
     held = mix_ref.shape[1]
     for order, (start, stop) in enumerate(orders):
         mix = mix_ref[order] * factors[order]
@@ -162,34 +148,59 @@
         out_ref[order] = jnp.log1p(total)
 
 
-def accumulate(pos, act, data, slabs, own_slab, box_x, count, start, mix=None):
-    atoms = pos.shape[1]
-    first, last = not isinstance(start, tuple), mix is not None
-    channels = (start if first else start[1]).shape[0]
-    operands = [pos, act, *data, *((start,) if first else start)]
+def spread_kernel(count, par_ref, pos_ref, spread_ref, centre_ref):
+    group = lax.broadcasted_iota(jnp.int32, spread_ref.shape, 1) // tile
+    spread = jnp.broadcast_to(par_ref[:, 0:1], spread_ref.shape)
+    for n in range(1, count):
+        spread = jnp.where(group == n, par_ref[:, n : n + 1], spread)
+    spread_ref[...] = spread
+    centre = jnp.zeros(centre_ref.shape, jnp.float32)
+    for kind in range(par_ref.shape[1] - count):
+        here = pos_ref[3:4, :] == float(kind)
+        centre = jnp.where(here, par_ref[:, count + kind : count + kind + 1], centre)
+    centre_ref[...] = centre
+
+
+def spread_out(par, pos, count):
+    whole = pl.BlockSpec(memory_space=pltpu.VMEM)
+    narrow = jax.ShapeDtypeStruct((par.shape[0], pos.shape[1]), jnp.float32)
+    return pl.pallas_call(
+        functools.partial(spread_kernel, count),
+        out_shape=[narrow, narrow],
+        in_specs=[whole, whole],
+        out_specs=[whole, whole],
+        compiler_params=pltpu.CompilerParams(vmem_limit_bytes=1 << 20),
+        name="spread",
+    )(par, pos)
+
+
+def accumulate(pos, act, data, slabs, own_slab, box_x, count, spread, acc=None, mix=None):
+    channels, atoms = spread[0].shape
+    first, last = acc is None, mix is not None
+    operands = [pos, act, *data, *spread]
     wide = jax.ShapeDtypeStruct((channels, components * atoms), jnp.float32)
-    narrow = jax.ShapeDtypeStruct((channels, atoms), jnp.float32)
+    shape, scratch = wide, []
+    if not first:
+        operands.append(acc)
     if last:
         operands.append(mix)
-        shapes = jax.ShapeDtypeStruct((len(orders), mix.shape[1], atoms), jnp.float32)
-    else:
-        shapes = [wide, narrow, narrow] if first else [wide]
+        shape = jax.ShapeDtypeStruct((len(orders), mix.shape[1], atoms), jnp.float32)
+        scratch = [pltpu.VMEM(wide.shape, jnp.float32)]
     flops = 2 * channels * count * components * atoms * atoms * len(slabs)
 
     def body(*refs):
         pair_kernel(slabs, len(data), own_slab, first, last, box_x, count, *refs)
 
     whole = pl.BlockSpec(memory_space=pltpu.VMEM)
-    result = pl.pallas_call(
+    return pl.pallas_call(
         body,
-        out_shape=shapes,
+        out_shape=shape,
         in_specs=[whole] * len(operands),
-        out_specs=whole if last else [whole] * len(shapes),
-        scratch_shapes=[pltpu.VMEM(wide.shape, jnp.float32)] if last else [],
+        out_specs=whole,
+        scratch_shapes=scratch,
         cost_estimate=pl.CostEstimate(flops=flops, bytes_accessed=1 << 20, transcendentals=0),
         compiler_params=pltpu.CompilerParams(vmem_limit_bytes=16 << 20),
     )(*operands)
-    return result if last else tuple(result) if first else (result[0], *start[1:])
 
 
 def pack_kernel(box_x, *refs):
@@ -281,7 +292,7 @@
     reach = (block_mask.shape[1] - 1) // 2
     count = radial_weight.shape[0]
     kinds = species_embed.shape[1]
-    held, atoms = node_features.shape
+    held, _ = node_features.shape
     me = lax.axis_index("blk")
     owner = lax.axis_index("chan")
 
@@ -312,10 +323,11 @@
         offset = jnp.stack([lax.rem(p - me + reach + slab_count, slab_count) for p in places])
         at = offset[:, None] == jnp.arange(2 * reach + 1, dtype=jnp.int32)[None, :]
         value = jnp.sum(jnp.where(at, block_mask, 0), axis=1).astype(jnp.float32)
-        return jnp.broadcast_to(value[:, None], (len(places), atoms))
-
-    call = lambda act, data, slabs, start, mix=None: accumulate(
-        pos, act, data, slabs, 0, box_x, count, start, mix
+        return value[:, None]
+
+    spread = spread_out(par, pos, count)
+    call = lambda act, data, slabs, acc=None, mix=None: accumulate(
+        pos, act, data, slabs, 0, box_x, count, spread, acc, mix
     )
     if crossing:
         act = activity([me ^ j for j in range(slab_count)])
@@ -323,7 +335,7 @@
         mixed = lambda a, b, index: (((a, 0), (b, half)), (a, channels), index)
         three = flipped(bundle, "blk", 3)
         one = flipped(bundle, "blk", 1)
-        acc = call(act, [bundle, one], [mixed(0, 1, 0)], par)
+        acc = call(act, [bundle, one], [mixed(0, 1, 0)])
         three, one, acc = lax.optimization_barrier((three, one, acc))
         pair = jnp.concatenate([bundle[:half], one[half:channels], pos, three], axis=0)
         five = flipped(pair, "blk", 5)
@@ -344,7 +356,7 @@
         moved(bundle, "blk", lambda i, size, k=k: (i - k) % size) for k in places[1:]
     ]
     slabs = [(((j, 0),), (j, channels), j) for j in range(len(places))]
-    return call(act, data, slabs, par, mix)
+    return call(act, data, slabs, None, mix)
 
 
 def solution(mesh):

time: 21.2 us -> 21.2 us (level)
    pallas_call x5 -> x6, Pallas kernels: 5.35 us -> 5.45 us  [the longest x5 5.29 us: accumulate(): pl.pallas_call(body, out_shape=shape, in_specs=[whole] * len(operands), o...]
  transfers between devices with their start and end apart: 7 -> 7, of which waited for: 5 -> 4; matrix products, arithmetic and copies ran while one was open for 3% -> 3% of each run, Pallas kernels for 16% -> 17%
where the time goes in v6:
time: 21.2 us; the launch traced here: 21 us
  starting transfers between devices  9.7 us (46%)
  Pallas kernels  6.41 us (30%)
  waiting for transfers between devices  3.35 us (16%)
  local copies, waits for them, and re-layouts  1.05 us (5%)
  other arithmetic  0.35 us (2%)
    ppermute x2, starting transfers between devices, crossed(): return lax.ppermute(value, ('blk', 'chan'), pairs)  5.46 us
    pallas_call x5, Pallas kernels, accumulate(): pl.pallas_call(body, out_shape=shape, in_specs=[whole] * len(operands), o...  5.29 us
    ppermute x5, starting transfers between devices, moved(): lax.ppermute(value, axis, [(i, target(i, size)) for i in range(size)])  4.24 us
    ppermute x2, waiting for transfers between devices, crossed(): return lax.ppermute(value, ('blk', 'chan'), pairs)  2.01 us
    ppermute x5, waiting for transfers between devices, moved(): lax.ppermute(value, axis, [(i, target(i, size)) for i in range(size)])  1.34 us
    pallas_call x1, Pallas kernels, pack(): pl.pallas_call(functools.partial(pack_kernel, box_x), out_shape=(jax.Shap...  0.96 us
    unnamed x10, local copies, waits for them, and re-layouts  0.68 us
  transfers between devices with their start and end apart: 7, of which 4 were waited for; matrix products, arithmetic and copies ran while one was open for 3% of the time, Pallas kernels for 17%

profile of v6, /device:TPU:0, one launch (start us, length us, event | category | flops | bytes accessed | tf_op | source)
XLA Modules:
  0.0 21.0 jit_solution(9555965269959803669)
XLA Ops:
  0.0 1.0 %pack.1 = (f32[32,128]{1,0:T(8,128)S(1)}, f32[8,128]{1,0:T(8,128)S(1)}) custom-call(f32[16,128]{1,0:T(8,128)} %refs_0_.1, s32[1,128]{1,0:T(1,128)} %bitcast.23, f32[3,128]{1,0:T(4,128)} %refs_2_.1, f32[2,16]{1,0:T(2,128)} %bitcast.21, f32[8,16]{1,0:T(8,128)} %refs_4_.1, f32[2,16]{1,0:T(2,128)} %bitcast.22), custom_call_target="tpu_custom_call" | custom-call | tf_op jit(solution)/shard_map/pack/pallas_call | solution.py:247
  1.0 3.6 %collective-permute-start = (f32[32,128]{1,0:T(8,128)S(1)}, f32[32,128]{1,0:T(8,128)S(1)}, u32[]{:S(2)}, u32[]{:S(2)}) collective-permute-start(f32[32,128]{1,0:T(8,128)S(1)} %get-tuple-element.17), channel_id=1, source_target_pairs={{0,6},{1,7},{2,4},{3,5},{4,2},{5,3},{6,0},{7,1},{8,14},{9,15},{10,... | collective-permute-start | bytes 49160 | tf_op jit(solution)/shard_map/ppermute | solution.py:276
  4.5 0.1 stack.31
  4.6 0.0 copy-start.1
  4.6 0.7 %copy-done.1 = s32[1,7]{1,0:T(1,128)S(1)} copy-done((s32[1,7]{1,0:T(1,128)S(1)}, s32[1,7]{1,0:T(1,128)}, u32[]{:S(2)}) %copy-start.1) | copy-done | bytes 52
  5.3 0.2 select_reduce_fusion
  5.5 0.1 copy.20.refs_1_
  5.6 0.4 %collective-permute-done = f32[32,128]{1,0:T(8,128)S(1)} collective-permute-done((f32[32,128]{1,0:T(8,128)S(1)}, f32[32,128]{1,0:T(8,128)S(1)}, u32[]{:S(2)}, u32[]{:S(2)}) %collective-permute-start) | collective-permute-done | bytes 16416 | tf_op jit(solution)/shard_map/ppermute | solution.py:276
  6.0 1.9 %collective-permute-start.1 = (f32[64,128]{1,0:T(8,128)S(1)}, f32[64,128]{1,0:T(8,128)S(1)}, u32[]{:S(2)}, u32[]{:S(2)}) collective-permute-start(f32[64,128]{1,0:T(8,128)S(1)} %pad_maximum_fusion), channel_id=1, source_target_pairs={{0,5},{1,4},{2,7},{3,6},{4,1},{5,0},{6,3},{7,2},{8,13},{9,12},{10,... | collective-permute-start | bytes 98312 | tf_op jit(solution)/shard_map/ppermute | solution.py:276
  7.9 1.6 %collective-permute-done.1 = f32[64,128]{1,0:T(8,128)S(1)} collective-permute-done((f32[64,128]{1,0:T(8,128)S(1)}, f32[64,128]{1,0:T(8,128)S(1)}, u32[]{:S(2)}, u32[]{:S(2)}) %collective-permute-start.1) | collective-permute-done | bytes 32800 | tf_op jit(solution)/shard_map/ppermute | solution.py:276
  9.5 0.6 %collective-permute-start.3 = (f32[72,128]{1,0:T(8,128)S(1)}, f32[72,128]{1,0:T(8,128)S(1)}, u32[]{:S(2)}, u32[]{:S(2)}) collective-permute-start(f32[72,128]{1,0:T(8,128)S(1)} %constant_dynamic-update-slice_fusion.refs_2_.refs_3_), channel_id=1, source_target_pairs={{0,4},{4,0},{8,12},{12,8},{16,20},{20,16},{24,28},{28,24},{1,5},{5... | collective-permute-start | bytes 110600 | tf_op jit(solution)/shard_map/ppermute | solution.py:264
  10.1 1.6 %collective-permute-start.2 = (f32[72,128]{1,0:T(8,128)S(1)}, f32[72,128]{1,0:T(8,128)S(1)}, u32[]{:S(2)}, u32[]{:S(2)}) collective-permute-start(f32[72,128]{1,0:T(8,128)S(1)} %constant_dynamic-update-slice_fusion.refs_2_.refs_3_), channel_id=1, source_target_pairs={{0,12},{4,8},{8,4},{12,0},{16,28},{20,24},{24,20},{28,16},{1,13},{... | collective-permute-start | bytes 110600 | tf_op jit(solution)/shard_map/ppermute | solution.py:264
  11.7 0.1 pad_maximum_fusion.2
  11.7 0.1 copy.15.par_ref
  11.8 0.2 spread.1
  12.0 0.0 collective-permute-done.3.refs_3_.refs_2_
  12.0 0.7 %shard_map.82.refs_6_ = f32[64,1152]{1,0:T(8,128)S(1)} custom-call(f32[8,128]{1,0:T(8,128)S(1)} %get-tuple-element.16.pos_ref.refs_0_, f32[8,1]{1,0:T(8,128)S(1)} %copy.20.refs_1_, f32[72,128]{1,0:T(8,128)S(1)} %constant_dynamic-update-slice_fusion.refs_2_.refs_3_, f32[72,128]{1,0:T(8,128)S(1)} %collective-permute-done.3.refs_3_.refs_2_, ...), custom_call_target="tpu_custom_call" | custom-call | flops 150994944 | bytes 1048576 | tf_op jit(solution)/shard_map/pallas_call | solution.py:195
  12.7 0.0 copy-start
  12.8 0.8 %collective-permute-done.2.refs_2_ = f32[72,128]{1,0:T(8,128)S(1)} collective-permute-done((f32[72,128]{1,0:T(8,128)S(1)}, f32[72,128]{1,0:T(8,128)S(1)}, u32[]{:S(2)}, u32[]{:S(2)}) %collective-permute-start.2) | collective-permute-done | bytes 36896 | tf_op jit(solution)/shard_map/ppermute | solution.py:264
  13.6 0.1 collective-permute-start.5
  13.7 1.6 %collective-permute-start.4 = (f32[144,128]{1,0:T(8,128)S(1)}, f32[144,128]{1,0:T(8,128)S(1)}, u32[]{:S(2)}, u32[]{:S(2)}) collective-permute-start(f32[144,128]{1,0:T(8,128)S(1)} %constant_dynamic-update-slice_fusion.5), channel_id=1, source_target_pairs={{0,20},{4,16},{8,28},{12,24},{16,4},{20,0},{24,12},{28,8},{1,21},{... | collective-permute-start | bytes 221192 | tf_op jit(solution)/shard_map/ppermute | solution.py:264
  15.3 0.0 copy-done
  15.3 0.1 constant_dynamic-slice_fusion.2
  15.4 0.7 %shard_map.83.refs_6_ = f32[64,1152]{1,0:T(8,128)S(1)} custom-call(f32[8,128]{1,0:T(8,128)S(1)} %get-tuple-element.16.pos_ref.refs_0_, f32[8,1]{1,0:T(8,128)S(1)} %copy.20.refs_1_, f32[72,128]{1,0:T(8,128)S(1)} %collective-permute-done.3.refs_3_.refs_2_, f32[72,128]{1,0:T(8,128)S(1)} %constant_dynamic-update-slice_fusion.refs_2_.refs_3_, ...), custom_call_target="tpu_custom_call" | custom-call | flops 150994944 | bytes 1048576 | tf_op jit(solution)/shard_map/pallas_call | solution.py:195
  16.1 0.0 collective-permute-done.5.refs_3_
  16.1 1.2 %shard_map.84.refs_5_ = f32[64,1152]{1,0:T(8,128)S(1)} custom-call(f32[8,128]{1,0:T(8,128)S(1)} %get-tuple-element.16.pos_ref.refs_0_, f32[8,1]{1,0:T(8,128)S(1)} %copy.20.refs_1_, f32[72,128]{1,0:T(8,128)S(1)} %collective-permute-done.2.refs_2_, f32[72,128]{1,0:T(8,128)S(1)} %collective-permute-done.5.refs_3_, ...), custom_call_target="tpu_custom_call" | custom-call | flops 301989888 | bytes 1048576 | tf_op jit(solution)/shard_map/pallas_call | solution.py:195
  17.3 0.5 %collective-permute-done.4 = f32[144,128]{1,0:T(8,128)S(1)} collective-permute-done((f32[144,128]{1,0:T(8,128)S(1)}, f32[144,128]{1,0:T(8,128)S(1)}, u32[]{:S(2)}, u32[]{:S(2)}) %collective-permute-start.4) | collective-permute-done | bytes 73760 | tf_op jit(solution)/shard_map/ppermute | solution.py:264
  17.8 0.4 %collective-permute-start.6 = (f32[72,128]{1,0:T(8,128)S(1)}, f32[72,128]{1,0:T(8,128)S(1)}, u32[]{:S(2)}, u32[]{:S(2)}) collective-permute-start(f32[72,128]{1,0:T(8,128)S(1)} %get-tuple-element.32.refs_2_), channel_id=1, source_target_pairs={{0,4},{4,0},{8,12},{12,8},{16,20},{20,16},{24,28},{28,24},{1,5},{5... | collective-permute-start | bytes 110600 | tf_op jit(solution)/shard_map/ppermute | solution.py:264
  18.2 0.1 pad_maximum_fusion.1.refs_7_
  18.3 0.7 %shard_map.85.refs_6_ = f32[64,1152]{1,0:T(8,128)S(1)} custom-call(f32[8,128]{1,0:T(8,128)S(1)} %get-tuple-element.16.pos_ref.refs_0_, f32[8,1]{1,0:T(8,128)S(1)} %copy.20.refs_1_, f32[72,128]{1,0:T(8,128)S(1)} %get-tuple-element.31.refs_2_, f32[64,128]{1,0:T(8,128)S(1)} %get-tuple-element.18.refs_4_.refs_3_, ...), custom_call_target="tpu_custom_call" | custom-call | flops 150994944 | bytes 1048576 | tf_op jit(solution)/shard_map/pallas_call | solution.py:195
  19.0 0.0 collective-permute-done.6.refs_3_
  19.0 1.9 %shard_map.86 = f32[3,16,128]{2,1,0:T(8,128)} custom-call(f32[8,128]{1,0:T(8,128)S(1)} %get-tuple-element.16.pos_ref.refs_0_, f32[8,1]{1,0:T(8,128)S(1)} %copy.20.refs_1_, f32[72,128]{1,0:T(8,128)S(1)} %get-tuple-element.32.refs_2_, f32[72,128]{1,0:T(8,128)S(1)} %collective-permute-done.6.refs_3_, f32[64,128]{1,0:T(8,128)S(1)} %get-tuple-element.18.refs_4_.refs_3_, ...), custom_call_target="tpu_custom_call" | custom-call | flops 301989888 | bytes 1048576 | tf_op jit(solution)/shard_map/pallas_call | solution.py:195
  (14 shorter events, 0.0 us)
Async XLA Ops:
  1.0 5.0 %collective-permute-start = (f32[32,128]{1,0:T(8,128)S(1)}, f32[32,128]{1,0:T(8,128)S(1)}, u32[]{:S(2)}, u32[]{:S(2)}) collective-permute-start(f32[32,128]{1,0:T(8,128)S(1)} %get-tuple-element.17), channel_id=1, source_target_pairs={{0,6},{1,7},{2,4},{3,5},{4,2},{5,3},{6,0},{7,1},{8,14},{9,15},{10,... | collective-permute-start | bytes 49160 | tf_op jit(solution)/shard_map/ppermute | solution.py:276
  4.6 0.7 %copy-start.1 = (s32[1,7]{1,0:T(1,128)S(1)}, s32[1,7]{1,0:T(1,128)}, u32[]{:S(2)}) copy-start(s32[1,7]{1,0:T(1,128)} %param.11) | copy-start | bytes 88
  6.0 3.5 %collective-permute-start.1 = (f32[64,128]{1,0:T(8,128)S(1)}, f32[64,128]{1,0:T(8,128)S(1)}, u32[]{:S(2)}, u32[]{:S(2)}) collective-permute-start(f32[64,128]{1,0:T(8,128)S(1)} %pad_maximum_fusion), channel_id=1, source_target_pairs={{0,5},{1,4},{2,7},{3,6},{4,1},{5,0},{6,3},{7,2},{8,13},{9,12},{10,... | collective-permute-start | bytes 98312 | tf_op jit(solution)/shard_map/ppermute | solution.py:276
  9.5 2.5 %collective-permute-start.3 = (f32[72,128]{1,0:T(8,128)S(1)}, f32[72,128]{1,0:T(8,128)S(1)}, u32[]{:S(2)}, u32[]{:S(2)}) collective-permute-start(f32[72,128]{1,0:T(8,128)S(1)} %constant_dynamic-update-slice_fusion.refs_2_.refs_3_), channel_id=1, source_target_pairs={{0,4},{4,0},{8,12},{12,8},{16,20},{20,16},{24,28},{28,24},{1,5},{5... | collective-permute-start | bytes 110600 | tf_op jit(solution)/shard_map/ppermute | solution.py:264
  10.1 3.5 %collective-permute-start.2 = (f32[72,128]{1,0:T(8,128)S(1)}, f32[72,128]{1,0:T(8,128)S(1)}, u32[]{:S(2)}, u32[]{:S(2)}) collective-permute-start(f32[72,128]{1,0:T(8,128)S(1)} %constant_dynamic-update-slice_fusion.refs_2_.refs_3_), channel_id=1, source_target_pairs={{0,12},{4,8},{8,4},{12,0},{16,28},{20,24},{24,20},{28,16},{1,13},{... | collective-permute-start | bytes 110600 | tf_op jit(solution)/shard_map/ppermute | solution.py:264
  12.7 2.5 %copy-start = (f32[3,64,64]{2,1,0:T(8,128)S(1)}, f32[3,64,64]{2,1,0:T(8,128)}, u32[]{:S(2)}) copy-start(f32[3,64,64]{2,1,0:T(8,128)} %param.15) | copy-start | bytes 147460
  13.6 2.5 %collective-permute-start.5 = (f32[72,128]{1,0:T(8,128)S(1)}, f32[72,128]{1,0:T(8,128)S(1)}, u32[]{:S(2)}, u32[]{:S(2)}) collective-permute-start(f32[72,128]{1,0:T(8,128)S(1)} %collective-permute-done.2.refs_2_), channel_id=1, source_target_pairs={{0,4},{4,0},{8,12},{12,8},{16,20},{20,16},{24,28},{28,24},{1,5},{5... | collective-permute-start | bytes 110600 | tf_op jit(solution)/shard_map/ppermute | solution.py:264
  13.7 4.1 %collective-permute-start.4 = (f32[144,128]{1,0:T(8,128)S(1)}, f32[144,128]{1,0:T(8,128)S(1)}, u32[]{:S(2)}, u32[]{:S(2)}) collective-permute-start(f32[144,128]{1,0:T(8,128)S(1)} %constant_dynamic-update-slice_fusion.5), channel_id=1, source_target_pairs={{0,20},{4,16},{8,28},{12,24},{16,4},{20,0},{24,12},{28,8},{1,21},{... | collective-permute-start | bytes 221192 | tf_op jit(solution)/shard_map/ppermute | solution.py:264
  17.8 1.3 %collective-permute-start.6 = (f32[72,128]{1,0:T(8,128)S(1)}, f32[72,128]{1,0:T(8,128)S(1)}, u32[]{:S(2)}, u32[]{:S(2)}) collective-permute-start(f32[72,128]{1,0:T(8,128)S(1)} %get-tuple-element.32.refs_2_), channel_id=1, source_target_pairs={{0,4},{4,0},{8,12},{12,8},{16,20},{20,16},{24,28},{28,24},{1,5},{5... | collective-permute-start | bytes 110600 | tf_op jit(solution)/shard_map/ppermute | solution.py:264

commit v7 on v6

--- a/solution.py
+++ b/solution.py
@@ -88,6 +88,7 @@
     own = [jnp.broadcast_to(pos_ref[axis : axis + 1, :], (tile, lanes)) for axis in range(3)]
     channels = rest[0].shape[0]
     within = lax.rem(lax.broadcasted_iota(jnp.int32, (channels, lanes), 1), tile)
+    down = lax.broadcasted_iota(jnp.int32, (tile, lanes), 0)
     spread_ref, centre_ref = rest.pop(0), rest.pop(0)
     spread = spread_ref[...]
     if not first:
@@ -101,21 +102,22 @@
         feats = [data[which][at : at + channels // len(pieces), :] for which, at in pieces]
         feats = feats[0] if len(feats) == 1 else jnp.concatenate(feats, axis=0)
         feats = feats * act_ref[index : index + 1, 0:1]
-        columns = data[where][base : base + 8, :].T
+        across = [
+            jnp.broadcast_to(data[where][base + axis : base + axis + 1, :], (tile, lanes))
+            for axis in range(3)
+        ]
         for pair in range(lanes // (2 * tile)):
             weights, tables = [], []
             for step in (2 * pair, 2 * pair + 1):
                 picked = jnp.take_along_axis(feats, within + step * tile, axis=1)
                 weights.append((spread * picked).astype(jnp.bfloat16))
-                rows = slice(step * tile, (step + 1) * tile)
                 other = [
-                    jnp.broadcast_to(columns[rows, axis : axis + 1], (tile, lanes))
-                    for axis in range(3)
+                    jnp.take_along_axis(axis, down + step * tile, axis=1) for axis in across
                 ]
                 apart = None
                 if index == own_slab:
                     apart = (
-                        lax.broadcasted_iota(jnp.int32, (tile, lanes), 0) + step * tile
+                        down + step * tile
                     ) != lax.broadcasted_iota(jnp.int32, (tile, lanes), 1)
                 tables += pair_rows(own, other, lengths, count, apart)
             stacked = jnp.concatenate([jnp.concatenate(row, axis=1) for row in tables], axis=0)

time: 21.2 us -> 21.1 us (level)
  Pallas kernels: 6.41 us -> 5.91 us
  waiting for transfers between devices: 3.35 us -> 3.71 us
    pallas_call x5, Pallas kernels: 5.29 us -> 4.79 us  [accumulate(): pl.pallas_call(body, out_shape=shape, in_specs=[whole] * len(operands), o...]
    ppermute x5, waiting for transfers between devices: 1.34 us -> 1.7 us  [moved(): lax.ppermute(value, axis, [(i, target(i, size)) for i in range(size)])]
  transfers between devices with their start and end apart: 7 -> 7, of which waited for: 4 -> 5; matrix products, arithmetic and copies ran while one was open for 3% -> 3% of each run, Pallas kernels for 17% -> 15%
where the time goes in v7:
time: 21.1 us; the launch traced here: 20.8 us
  starting transfers between devices  9.7 us (46%)
  Pallas kernels  5.91 us (28%)
  waiting for transfers between devices  3.71 us (18%)
  local copies, waits for them, and re-layouts  1.05 us (5%)
  other arithmetic  0.35 us (2%)
    ppermute x2, starting transfers between devices, crossed(): return lax.ppermute(value, ('blk', 'chan'), pairs)  5.46 us
    pallas_call x5, Pallas kernels, accumulate(): pl.pallas_call(body, out_shape=shape, in_specs=[whole] * len(operands), o...  4.79 us
    ppermute x5, starting transfers between devices, moved(): lax.ppermute(value, axis, [(i, target(i, size)) for i in range(size)])  4.24 us
    ppermute x2, waiting for transfers between devices, crossed(): return lax.ppermute(value, ('blk', 'chan'), pairs)  2.01 us
    ppermute x5, waiting for transfers between devices, moved(): lax.ppermute(value, axis, [(i, target(i, size)) for i in range(size)])  1.7 us
    pallas_call x1, Pallas kernels, pack(): pl.pallas_call(functools.partial(pack_kernel, box_x), out_shape=(jax.Shap...  0.96 us
    unnamed x10, local copies, waits for them, and re-layouts  0.68 us
  transfers between devices with their start and end apart: 7, of which 5 were waited for; matrix products, arithmetic and copies ran while one was open for 3% of the time, Pallas kernels for 15%

profile of v7, /device:TPU:0, one launch (start us, length us, event | category | flops | bytes accessed | tf_op | source)
XLA Modules:
  0.0 20.8 jit_solution(14765386305037348866)
XLA Ops:
  0.0 1.0 %pack.1 = (f32[32,128]{1,0:T(8,128)S(1)}, f32[8,128]{1,0:T(8,128)S(1)}) custom-call(f32[16,128]{1,0:T(8,128)} %refs_0_.1, s32[1,128]{1,0:T(1,128)} %bitcast.23, f32[3,128]{1,0:T(4,128)} %refs_2_.1, f32[2,16]{1,0:T(2,128)} %bitcast.21, f32[8,16]{1,0:T(8,128)} %refs_4_.1, f32[2,16]{1,0:T(2,128)} %bitcast.22), custom_call_target="tpu_custom_call" | custom-call | tf_op jit(solution)/shard_map/pack/pallas_call | solution.py:249
  1.0 3.6 %collective-permute-start = (f32[32,128]{1,0:T(8,128)S(1)}, f32[32,128]{1,0:T(8,128)S(1)}, u32[]{:S(2)}, u32[]{:S(2)}) collective-permute-start(f32[32,128]{1,0:T(8,128)S(1)} %get-tuple-element.17), channel_id=1, source_target_pairs={{0,6},{1,7},{2,4},{3,5},{4,2},{5,3},{6,0},{7,1},{8,14},{9,15},{10,... | collective-permute-start | bytes 49160 | tf_op jit(solution)/shard_map/ppermute | solution.py:278
  4.5 0.1 stack.31
  4.6 0.0 copy-start.1
  4.6 0.7 %copy-done.1 = s32[1,7]{1,0:T(1,128)S(1)} copy-done((s32[1,7]{1,0:T(1,128)S(1)}, s32[1,7]{1,0:T(1,128)}, u32[]{:S(2)}) %copy-start.1) | copy-done | bytes 52
  5.3 0.2 select_reduce_fusion
  5.5 0.1 copy.20.refs_1_
  5.6 0.4 %collective-permute-done = f32[32,128]{1,0:T(8,128)S(1)} collective-permute-done((f32[32,128]{1,0:T(8,128)S(1)}, f32[32,128]{1,0:T(8,128)S(1)}, u32[]{:S(2)}, u32[]{:S(2)}) %collective-permute-start) | collective-permute-done | bytes 16416 | tf_op jit(solution)/shard_map/ppermute | solution.py:278
  6.0 1.9 %collective-permute-start.1 = (f32[64,128]{1,0:T(8,128)S(1)}, f32[64,128]{1,0:T(8,128)S(1)}, u32[]{:S(2)}, u32[]{:S(2)}) collective-permute-start(f32[64,128]{1,0:T(8,128)S(1)} %pad_maximum_fusion), channel_id=1, source_target_pairs={{0,5},{1,4},{2,7},{3,6},{4,1},{5,0},{6,3},{7,2},{8,13},{9,12},{10,... | collective-permute-start | bytes 98312 | tf_op jit(solution)/shard_map/ppermute | solution.py:278
  7.9 1.6 %collective-permute-done.1 = f32[64,128]{1,0:T(8,128)S(1)} collective-permute-done((f32[64,128]{1,0:T(8,128)S(1)}, f32[64,128]{1,0:T(8,128)S(1)}, u32[]{:S(2)}, u32[]{:S(2)}) %collective-permute-start.1) | collective-permute-done | bytes 32800 | tf_op jit(solution)/shard_map/ppermute | solution.py:278
  9.5 0.6 %collective-permute-start.3 = (f32[72,128]{1,0:T(8,128)S(1)}, f32[72,128]{1,0:T(8,128)S(1)}, u32[]{:S(2)}, u32[]{:S(2)}) collective-permute-start(f32[72,128]{1,0:T(8,128)S(1)} %constant_dynamic-update-slice_fusion.refs_2_.refs_3_), channel_id=1, source_target_pairs={{0,4},{4,0},{8,12},{12,8},{16,20},{20,16},{24,28},{28,24},{1,5},{5... | collective-permute-start | bytes 110600 | tf_op jit(solution)/shard_map/ppermute | solution.py:266
  10.1 1.6 %collective-permute-start.2 = (f32[72,128]{1,0:T(8,128)S(1)}, f32[72,128]{1,0:T(8,128)S(1)}, u32[]{:S(2)}, u32[]{:S(2)}) collective-permute-start(f32[72,128]{1,0:T(8,128)S(1)} %constant_dynamic-update-slice_fusion.refs_2_.refs_3_), channel_id=1, source_target_pairs={{0,12},{4,8},{8,4},{12,0},{16,28},{20,24},{24,20},{28,16},{1,13},{... | collective-permute-start | bytes 110600 | tf_op jit(solution)/shard_map/ppermute | solution.py:266
  11.7 0.1 pad_maximum_fusion.2
  11.7 0.1 copy.15.par_ref
  11.8 0.2 spread.1
  12.0 0.0 collective-permute-done.3.refs_3_.refs_2_
  12.0 0.6 %shard_map.82.refs_6_ = f32[64,1152]{1,0:T(8,128)S(1)} custom-call(f32[8,128]{1,0:T(8,128)S(1)} %get-tuple-element.16.pos_ref.refs_0_, f32[8,1]{1,0:T(8,128)S(1)} %copy.20.refs_1_, f32[72,128]{1,0:T(8,128)S(1)} %constant_dynamic-update-slice_fusion.refs_2_.refs_3_, f32[72,128]{1,0:T(8,128)S(1)} %collective-permute-done.3.refs_3_.refs_2_, ...), custom_call_target="tpu_custom_call" | custom-call | flops 150994944 | bytes 1048576 | tf_op jit(solution)/shard_map/pallas_call | solution.py:197
  12.7 0.0 copy-start
  12.7 0.9 %collective-permute-done.2.refs_2_ = f32[72,128]{1,0:T(8,128)S(1)} collective-permute-done((f32[72,128]{1,0:T(8,128)S(1)}, f32[72,128]{1,0:T(8,128)S(1)}, u32[]{:S(2)}, u32[]{:S(2)}) %collective-permute-start.2) | collective-permute-done | bytes 36896 | tf_op jit(solution)/shard_map/ppermute | solution.py:266
  13.6 0.1 collective-permute-start.5
  13.7 1.6 %collective-permute-start.4 = (f32[144,128]{1,0:T(8,128)S(1)}, f32[144,128]{1,0:T(8,128)S(1)}, u32[]{:S(2)}, u32[]{:S(2)}) collective-permute-start(f32[144,128]{1,0:T(8,128)S(1)} %constant_dynamic-update-slice_fusion.5), channel_id=1, source_target_pairs={{0,20},{4,16},{8,28},{12,24},{16,4},{20,0},{24,12},{28,8},{1,21},{... | collective-permute-start | bytes 221192 | tf_op jit(solution)/shard_map/ppermute | solution.py:266
  15.3 0.0 copy-done
  15.3 0.1 constant_dynamic-slice_fusion.2
  15.4 0.7 %shard_map.83.refs_6_ = f32[64,1152]{1,0:T(8,128)S(1)} custom-call(f32[8,128]{1,0:T(8,128)S(1)} %get-tuple-element.16.pos_ref.refs_0_, f32[8,1]{1,0:T(8,128)S(1)} %copy.20.refs_1_, f32[72,128]{1,0:T(8,128)S(1)} %collective-permute-done.3.refs_3_.refs_2_, f32[72,128]{1,0:T(8,128)S(1)} %constant_dynamic-update-slice_fusion.refs_2_.refs_3_, ...), custom_call_target="tpu_custom_call" | custom-call | flops 150994944 | bytes 1048576 | tf_op jit(solution)/shard_map/pallas_call | solution.py:197
  16.0 0.0 collective-permute-done.5.refs_3_
  16.0 1.0 %shard_map.84.refs_5_ = f32[64,1152]{1,0:T(8,128)S(1)} custom-call(f32[8,128]{1,0:T(8,128)S(1)} %get-tuple-element.16.pos_ref.refs_0_, f32[8,1]{1,0:T(8,128)S(1)} %copy.20.refs_1_, f32[72,128]{1,0:T(8,128)S(1)} %collective-permute-done.2.refs_2_, f32[72,128]{1,0:T(8,128)S(1)} %collective-permute-done.5.refs_3_, ...), custom_call_target="tpu_custom_call" | custom-call | flops 301989888 | bytes 1048576 | tf_op jit(solution)/shard_map/pallas_call | solution.py:197
  17.1 0.7 %collective-permute-done.4 = f32[144,128]{1,0:T(8,128)S(1)} collective-permute-done((f32[144,128]{1,0:T(8,128)S(1)}, f32[144,128]{1,0:T(8,128)S(1)}, u32[]{:S(2)}, u32[]{:S(2)}) %collective-permute-start.4) | collective-permute-done | bytes 73760 | tf_op jit(solution)/shard_map/ppermute | solution.py:266
  17.8 0.4 %collective-permute-start.6 = (f32[72,128]{1,0:T(8,128)S(1)}, f32[72,128]{1,0:T(8,128)S(1)}, u32[]{:S(2)}, u32[]{:S(2)}) collective-permute-start(f32[72,128]{1,0:T(8,128)S(1)} %get-tuple-element.32.refs_2_), channel_id=1, source_target_pairs={{0,4},{4,0},{8,12},{12,8},{16,20},{20,16},{24,28},{28,24},{1,5},{5... | collective-permute-start | bytes 110600 | tf_op jit(solution)/shard_map/ppermute | solution.py:266
  18.2 0.1 pad_maximum_fusion.1.refs_7_
  18.3 0.7 %shard_map.85.refs_6_ = f32[64,1152]{1,0:T(8,128)S(1)} custom-call(f32[8,128]{1,0:T(8,128)S(1)} %get-tuple-element.16.pos_ref.refs_0_, f32[8,1]{1,0:T(8,128)S(1)} %copy.20.refs_1_, f32[72,128]{1,0:T(8,128)S(1)} %get-tuple-element.31.refs_2_, f32[64,128]{1,0:T(8,128)S(1)} %get-tuple-element.18.refs_4_.refs_3_, ...), custom_call_target="tpu_custom_call" | custom-call | flops 150994944 | bytes 1048576 | tf_op jit(solution)/shard_map/pallas_call | solution.py:197
  18.9 0.1 collective-permute-done.6.refs_3_
  19.0 1.8 %shard_map.86 = f32[3,16,128]{2,1,0:T(8,128)} custom-call(f32[8,128]{1,0:T(8,128)S(1)} %get-tuple-element.16.pos_ref.refs_0_, f32[8,1]{1,0:T(8,128)S(1)} %copy.20.refs_1_, f32[72,128]{1,0:T(8,128)S(1)} %get-tuple-element.32.refs_2_, f32[72,128]{1,0:T(8,128)S(1)} %collective-permute-done.6.refs_3_, f32[64,128]{1,0:T(8,128)S(1)} %get-tuple-element.18.refs_4_.refs_3_, ...), custom_call_target="tpu_custom_call" | custom-call | flops 301989888 | bytes 1048576 | tf_op jit(solution)/shard_map/pallas_call | solution.py:197
  (14 shorter events, 0.0 us)
Async XLA Ops:
  1.0 5.0 %collective-permute-start = (f32[32,128]{1,0:T(8,128)S(1)}, f32[32,128]{1,0:T(8,128)S(1)}, u32[]{:S(2)}, u32[]{:S(2)}) collective-permute-start(f32[32,128]{1,0:T(8,128)S(1)} %get-tuple-element.17), channel_id=1, source_target_pairs={{0,6},{1,7},{2,4},{3,5},{4,2},{5,3},{6,0},{7,1},{8,14},{9,15},{10,... | collective-permute-start | bytes 49160 | tf_op jit(solution)/shard_map/ppermute | solution.py:278
  4.6 0.7 %copy-start.1 = (s32[1,7]{1,0:T(1,128)S(1)}, s32[1,7]{1,0:T(1,128)}, u32[]{:S(2)}) copy-start(s32[1,7]{1,0:T(1,128)} %param.11) | copy-start | bytes 88
  6.0 3.5 %collective-permute-start.1 = (f32[64,128]{1,0:T(8,128)S(1)}, f32[64,128]{1,0:T(8,128)S(1)}, u32[]{:S(2)}, u32[]{:S(2)}) collective-permute-start(f32[64,128]{1,0:T(8,128)S(1)} %pad_maximum_fusion), channel_id=1, source_target_pairs={{0,5},{1,4},{2,7},{3,6},{4,1},{5,0},{6,3},{7,2},{8,13},{9,12},{10,... | collective-permute-start | bytes 98312 | tf_op jit(solution)/shard_map/ppermute | solution.py:278
  9.5 2.5 %collective-permute-start.3 = (f32[72,128]{1,0:T(8,128)S(1)}, f32[72,128]{1,0:T(8,128)S(1)}, u32[]{:S(2)}, u32[]{:S(2)}) collective-permute-start(f32[72,128]{1,0:T(8,128)S(1)} %constant_dynamic-update-slice_fusion.refs_2_.refs_3_), channel_id=1, source_target_pairs={{0,4},{4,0},{8,12},{12,8},{16,20},{20,16},{24,28},{28,24},{1,5},{5... | collective-permute-start | bytes 110600 | tf_op jit(solution)/shard_map/ppermute | solution.py:266
  10.1 3.5 %collective-permute-start.2 = (f32[72,128]{1,0:T(8,128)S(1)}, f32[72,128]{1,0:T(8,128)S(1)}, u32[]{:S(2)}, u32[]{:S(2)}) collective-permute-start(f32[72,128]{1,0:T(8,128)S(1)} %constant_dynamic-update-slice_fusion.refs_2_.refs_3_), channel_id=1, source_target_pairs={{0,12},{4,8},{8,4},{12,0},{16,28},{20,24},{24,20},{28,16},{1,13},{... | collective-permute-start | bytes 110600 | tf_op jit(solution)/shard_map/ppermute | solution.py:266
  12.7 2.6 %copy-start = (f32[3,64,64]{2,1,0:T(8,128)S(1)}, f32[3,64,64]{2,1,0:T(8,128)}, u32[]{:S(2)}) copy-start(f32[3,64,64]{2,1,0:T(8,128)} %param.15) | copy-start | bytes 147460
  13.6 2.5 %collective-permute-start.5 = (f32[72,128]{1,0:T(8,128)S(1)}, f32[72,128]{1,0:T(8,128)S(1)}, u32[]{:S(2)}, u32[]{:S(2)}) collective-permute-start(f32[72,128]{1,0:T(8,128)S(1)} %collective-permute-done.2.refs_2_), channel_id=1, source_target_pairs={{0,4},{4,0},{8,12},{12,8},{16,20},{20,16},{24,28},{28,24},{1,5},{5... | collective-permute-start | bytes 110600 | tf_op jit(solution)/shard_map/ppermute | solution.py:266
  13.7 4.1 %collective-permute-start.4 = (f32[144,128]{1,0:T(8,128)S(1)}, f32[144,128]{1,0:T(8,128)S(1)}, u32[]{:S(2)}, u32[]{:S(2)}) collective-permute-start(f32[144,128]{1,0:T(8,128)S(1)} %constant_dynamic-update-slice_fusion.5), channel_id=1, source_target_pairs={{0,20},{4,16},{8,28},{12,24},{16,4},{20,0},{24,12},{28,8},{1,21},{... | collective-permute-start | bytes 221192 | tf_op jit(solution)/shard_map/ppermute | solution.py:266
  17.8 1.3 %collective-permute-start.6 = (f32[72,128]{1,0:T(8,128)S(1)}, f32[72,128]{1,0:T(8,128)S(1)}, u32[]{:S(2)}, u32[]{:S(2)}) collective-permute-start(f32[72,128]{1,0:T(8,128)S(1)} %get-tuple-element.32.refs_2_), channel_id=1, source_target_pairs={{0,4},{4,0},{8,12},{12,8},{16,20},{20,16},{24,28},{28,24},{1,5},{5... | collective-permute-start | bytes 110600 | tf_op jit(solution)/shard_map/ppermute | solution.py:266

commit v8 on v7

--- a/solution.py
+++ b/solution.py
@@ -28,6 +28,7 @@
     0.003187821366091919,
 )
 factors = (1.0, math.sqrt(3.0), math.sqrt(15.0))
+own_factors = {6: 0.5 / math.sqrt(3.0), 8: 0.5}
 
 
 def horner(terms, v):
@@ -37,32 +38,30 @@
     return value
 
 
-def pair_rows(own, other, lengths, count, apart):
-    shift = []
-    for axis, length in enumerate(lengths):
-        r = other[axis] - own[axis]
-        shift.append(length * (r - jnp.round(r)))
-    x, y, z = shift
-    s = x * x + y * y + z * z + soften
+def pair_rows(own, other, count, apart):
+    x = other[0] - own[0]
+    y, z = (r - jnp.round(r) for r in (other[1] - own[1], other[2] - own[2]))
+    s = x * x + y * y + z * z + soften / cross_width**2
     inverse = lax.rsqrt(s)
-    square = s * (1.0 / cut_radius**2)
+    square = s * (cross_width / cut_radius) ** 2
     sixth = square * square * square
-    level = 0.5 * math.sqrt(2.0 / cut_radius)
+    level = 0.5 * math.sqrt(2.0 / cut_radius) / cross_width
     envelope = level + sixth * (
-        square * (inverse * (48.0 * cut_radius * level) - 21.0 * level) - 28.0 * level
-    )
-    keep = square < 1.0
+        square * (inverse * (48.0 * cut_radius / cross_width * level) - 21.0 * level)
+        - 28.0 * level
+    )
+    envelope = jnp.maximum(envelope, 0.0)
     if apart is not None:
-        keep = jnp.logical_and(keep, apart)
+        envelope = jnp.where(apart, envelope, 0.0)
     twice = horner(twice_cos_terms, square)
     rest = jnp.maximum(4.0 - twice * twice, 1e-12)
     sine = rest * lax.rsqrt(rest)
-    first = jnp.where(keep, envelope, 0.0) * (sine * inverse)
+    first = envelope * (sine * inverse)
     radial = [first, twice * first]
     while len(radial) < count:
         radial.append(twice * radial[-1] - radial[-2])
     x, y, z = x * inverse, y * inverse, z * inverse
-    xx, yy = x * x, y * y
+    xx, yy, zz = x * x, y * y, z * z
     harmonics = [
         None,
         x,
@@ -70,21 +69,20 @@
         z,
         x * y,
         y * z,
-        z * z * (1.0 / math.sqrt(3.0)) - (xx + yy) * (0.5 / math.sqrt(3.0)),
+        (zz + zz) - (xx + yy),
         x * z,
-        (xx - yy) * 0.5,
+        xx - yy,
     ]
     radial = [r.astype(jnp.bfloat16) for r in radial[:count]]
     harmonics = [None if h is None else h.astype(jnp.bfloat16) for h in harmonics]
     return [[r if h is None else r * h for h in harmonics] for r in radial]
 
 
-def pair_kernel(slabs, data_count, own_slab, first, last, box_x, count, *refs):
+def pair_kernel(slabs, data_count, own_slab, first, last, count, *refs):
     refs = list(refs)
     pos_ref, act_ref = refs[:2]
     data = refs[2 : 2 + data_count]
     rest = refs[2 + data_count :]
-    lengths = (box_x, cross_width, cross_width)
     own = [jnp.broadcast_to(pos_ref[axis : axis + 1, :], (tile, lanes)) for axis in range(3)]
     channels = rest[0].shape[0]
     within = lax.rem(lax.broadcasted_iota(jnp.int32, (channels, lanes), 1), tile)
@@ -106,6 +104,7 @@
             jnp.broadcast_to(data[where][base + axis : base + axis + 1, :], (tile, lanes))
             for axis in range(3)
         ]
+        across[0] = across[0] + act_ref[index : index + 1, 1:2]
         for pair in range(lanes // (2 * tile)):
             weights, tables = [], []
             for step in (2 * pair, 2 * pair + 1):
@@ -119,7 +118,7 @@
                     apart = (
                         down + step * tile
                     ) != lax.broadcasted_iota(jnp.int32, (tile, lanes), 1)
-                tables += pair_rows(own, other, lengths, count, apart)
+                tables += pair_rows(own, other, count, apart)
             stacked = jnp.concatenate([jnp.concatenate(row, axis=1) for row in tables], axis=0)
             product = jnp.dot(
                 jnp.concatenate(weights, axis=1), stacked, preferred_element_type=jnp.float32
@@ -134,7 +133,10 @@
         mix = mix_ref[order] * factors[order]
         mix_high = mix.astype(jnp.bfloat16)
         mix_low = (mix - mix_high.astype(jnp.float32)).astype(jnp.bfloat16)
-        features = [sum_ref[:, m * lanes : (m + 1) * lanes] * centre for m in range(start, stop)]
+        features = [
+            sum_ref[:, m * lanes : (m + 1) * lanes] * (centre * own_factors.get(m, 1.0))
+            for m in range(start, stop)
+        ]
         features = features[0] if len(features) == 1 else jnp.concatenate(features, axis=1)
         high = features.astype(jnp.bfloat16)
         low = (features - high.astype(jnp.float32)).astype(jnp.bfloat16)
@@ -176,7 +178,7 @@
     )(par, pos)
 
 
-def accumulate(pos, act, data, slabs, own_slab, box_x, count, spread, acc=None, mix=None):
+def accumulate(pos, act, data, slabs, own_slab, count, spread, acc=None, mix=None):
     channels, atoms = spread[0].shape
     first, last = acc is None, mix is not None
     operands = [pos, act, *data, *spread]
@@ -191,7 +193,7 @@
     flops = 2 * channels * count * components * atoms * atoms * len(slabs)
 
     def body(*refs):
-        pair_kernel(slabs, len(data), own_slab, first, last, box_x, count, *refs)
+        pair_kernel(slabs, len(data), own_slab, first, last, count, *refs)
 
     whole = pl.BlockSpec(memory_space=pltpu.VMEM)
     return pl.pallas_call(
@@ -205,7 +207,7 @@
     )(*operands)
 
 
-def pack_kernel(box_x, *refs):
+def pack_kernel(*refs):
     sources, (out_ref, own_ref), held_refs = refs[:6], refs[6:8], refs[8:14]
     tile_ref, sems = refs[14:]
     copies = [
@@ -218,24 +220,25 @@
     held = feats_ref.shape[0]
     kinds, count = embed_ref.shape[0], radial_ref.shape[0]
     tile_ref[...] = jnp.zeros_like(tile_ref)
-    out_ref[held:, :] = jnp.zeros((tile, lanes), jnp.float32)
+    out_ref[held:, :] = jnp.zeros((count, lanes), jnp.float32)
     own_ref[...] = jnp.zeros_like(own_ref)
     for copy in copies:
         copy.wait()
     tile_ref[0:kinds, 0:held] = embed_ref[...]
-    columns = tile_ref[...].T
     embedded = jnp.zeros(feats_ref.shape, jnp.float32)
+    down = lax.broadcasted_iota(jnp.int32, feats_ref.shape, 0)
     for kind in range(kinds):
-        embedded = jnp.where(species_ref[...] == kind, columns[:held, kind : kind + 1], embedded)
+        across = jnp.broadcast_to(tile_ref[kind : kind + 1, :], feats_ref.shape)
+        column = jnp.take_along_axis(across, down, axis=1)
+        embedded = jnp.where(species_ref[...] == kind, column, embedded)
     out_ref[0:held, :] = feats_ref[...] * embedded
     out_ref[held : held + count, 0:held] = radial_ref[...]
-    out_ref[held + count : held + count + kinds, 0:held] = center_ref[...]
-    for axis, length in enumerate((box_x, cross_width, cross_width)):
-        own_ref[axis : axis + 1, :] = pos_ref[axis : axis + 1, :] * (1.0 / length)
+    out_ref[held : held + kinds, held : 2 * held] = center_ref[...]
+    own_ref[0:3, :] = pos_ref[...] * (1.0 / cross_width)
     own_ref[3:4, :] = species_ref[...].astype(jnp.float32)
 
 
-def pack(box_x, node_features, species, positions, species_embed, radial_weight, center_embed):
+def pack(node_features, species, positions, species_embed, radial_weight, center_embed):
     held, atoms = node_features.shape
     operands = (
         node_features,
@@ -247,9 +250,9 @@
     )
     operands = [pltpu.with_memory_space_constraint(x, pltpu.HBM) for x in operands]
     return pl.pallas_call(
-        functools.partial(pack_kernel, box_x),
+        pack_kernel,
         out_shape=(
-            jax.ShapeDtypeStruct((held + tile, atoms), jnp.float32),
+            jax.ShapeDtypeStruct((held + radial_weight.shape[0], atoms), jnp.float32),
             jax.ShapeDtypeStruct((8, atoms), jnp.float32),
         ),
         in_specs=[pl.BlockSpec(memory_space=pltpu.HBM)] * len(operands),
@@ -290,7 +293,6 @@
 ):
     slab_count = lax.axis_size("blk")
     owner_count = lax.axis_size("chan")
-    box_x = float(slab_count) * slab_width
     reach = (block_mask.shape[1] - 1) // 2
     count = radial_weight.shape[0]
     kinds = species_embed.shape[1]
@@ -299,7 +301,7 @@
     owner = lax.axis_index("chan")
 
     owned, pos = pack(
-        box_x, node_features, species, positions, species_embed, radial_weight, center_embed
+        node_features, species, positions, species_embed, radial_weight, center_embed
     )
     channels = held * owner_count
     crossing = slab_count == 2 * (reach + 1) == 8 and owner_count == 4
@@ -315,21 +317,27 @@
             flips = flips + [f ^ bit for f in flips]
             bit //= 2
     bundle = jnp.concatenate([block[:held] for block in blocks] + [pos], axis=0)
-    par = jnp.concatenate([block[held : held + count + kinds, :held].T for block in blocks], axis=0)
+    radial = [block[held : held + count, :held] for block in blocks]
+    centres = [block[held : held + kinds, held : 2 * held] for block in blocks]
+    par = jnp.concatenate(
+        [jnp.concatenate(pair, axis=0).T for pair in zip(radial, centres)], axis=0
+    )
     mine = lax.dynamic_slice_in_dim(mix_weight, owner * held, held, 1)
     mix = jnp.concatenate(
         [lax.dynamic_slice_in_dim(mine, (owner ^ f) * held, held, 2) for f in flips], axis=2
     )
 
     def activity(places):
-        offset = jnp.stack([lax.rem(p - me + reach + slab_count, slab_count) for p in places])
+        place = jnp.stack(places)
+        offset = lax.rem(place - me + reach + slab_count, slab_count)
         at = offset[:, None] == jnp.arange(2 * reach + 1, dtype=jnp.int32)[None, :]
         value = jnp.sum(jnp.where(at, block_mask, 0), axis=1).astype(jnp.float32)
-        return value[:, None]
+        moves = (offset - reach - (place - me)).astype(jnp.float32) * (slab_width / cross_width)
+        return jnp.stack([value, moves], axis=1)
 
     spread = spread_out(par, pos, count)
     call = lambda act, data, slabs, acc=None, mix=None: accumulate(
-        pos, act, data, slabs, 0, box_x, count, spread, acc, mix
+        pos, act, data, slabs, 0, count, spread, acc, mix
     )
     if crossing:
         act = activity([me ^ j for j in range(slab_count)])

time: 21.1 us -> 21 us (level)
  waiting for transfers between devices: 3.71 us -> 3.04 us
  local copies, waits for them, and re-layouts: 1.05 us -> 1.37 us
  Pallas kernels: 5.91 us -> 6.19 us
    ppermute x2, waiting for transfers between devices: 2.01 us -> 1.57 us  [crossed(): return lax.ppermute(value, ('blk', 'chan'), pairs)]
    pallas_call x5, Pallas kernels: 4.79 us -> 5.14 us  [accumulate(): pl.pallas_call(body, out_shape=shape, in_specs=[whole] * len(operands), o...]
    ppermute x5, waiting for transfers between devices: 1.7 us -> 1.47 us  [moved(): lax.ppermute(value, axis, [(i, target(i, size)) for i in range(size)])]
    slice x0 -> x6, local copies, waits for them, and re-layouts: none -> 0.22 us  [the longest x3 0.22 us: shards(): centres = [block[held:held + kinds, held:2 * held] for block in blocks]]
  transfers between devices with their start and end apart: 7 -> 7, of which waited for: 5 -> 5; matrix products, arithmetic and copies ran while one was open for 3% -> 5% of each run, Pallas kernels for 15% -> 16%
where the time goes in v8:
time: 21 us; the launch traced here: 20.7 us
  starting transfers between devices  9.57 us (46%)
  Pallas kernels  6.19 us (29%)
  waiting for transfers between devices  3.04 us (14%)
  local copies, waits for them, and re-layouts  1.37 us (7%)
  other arithmetic  0.41 us (2%)
    ppermute x2, starting transfers between devices, crossed(): return lax.ppermute(value, ('blk', 'chan'), pairs)  5.45 us
    pallas_call x5, Pallas kernels, accumulate(): pl.pallas_call(body, out_shape=shape, in_specs=[whole] * len(operands), o...  5.14 us
    ppermute x5, starting transfers between devices, moved(): lax.ppermute(value, axis, [(i, target(i, size)) for i in range(size)])  4.12 us
    ppermute x2, waiting for transfers between devices, crossed(): return lax.ppermute(value, ('blk', 'chan'), pairs)  1.57 us
    ppermute x5, waiting for transfers between devices, moved(): lax.ppermute(value, axis, [(i, target(i, size)) for i in range(size)])  1.47 us
    pallas_call x1, Pallas kernels, pack(): pl.pallas_call(pack_kernel, out_shape=(jax.ShapeDtypeStruct((held + radia...  0.89 us
    unnamed x10, local copies, waits for them, and re-layouts  0.67 us
  transfers between devices with their start and end apart: 7, of which 5 were waited for; matrix products, arithmetic and copies ran while one was open for 5% of the time, Pallas kernels for 16%

profile of v8, /device:TPU:0, one launch (start us, length us, event | category | flops | bytes accessed | tf_op | source)
XLA Modules:
  0.0 20.7 jit_solution(2216525815417348580)
XLA Ops:
  0.0 0.9 %pack.1 = (f32[24,128]{1,0:T(8,128)S(1)}, f32[8,128]{1,0:T(8,128)S(1)}) custom-call(f32[16,128]{1,0:T(8,128)} %refs_0_.1, s32[1,128]{1,0:T(1,128)} %bitcast.32, f32[3,128]{1,0:T(4,128)} %refs_2_.1, f32[2,16]{1,0:T(2,128)} %bitcast.30, f32[8,16]{1,0:T(8,128)} %refs_4_.1, f32[2,16]{1,0:T(2,128)} %bitcast.31), custom_call_target="tpu_custom_call" | custom-call | tf_op jit(solution)/shard_map/pack/pallas_call | solution.py:252
  0.9 3.6 %collective-permute-start = (f32[24,128]{1,0:T(8,128)S(1)}, f32[24,128]{1,0:T(8,128)S(1)}, u32[]{:S(2)}, u32[]{:S(2)}) collective-permute-start(f32[24,128]{1,0:T(8,128)S(1)} %get-tuple-element.17), channel_id=1, source_target_pairs={{0,6},{1,7},{2,4},{3,5},{4,2},{5,3},{6,0},{7,1},{8,14},{9,15},{10,... | collective-permute-start | bytes 36872 | tf_op jit(solution)/shard_map/ppermute | solution.py:281
  4.5 0.1 slice.60
  4.5 0.1 stack.58
  4.6 0.0 copy-start.1
  4.7 0.7 %copy-done.1 = s32[1,7]{1,0:T(1,128)S(1)} copy-done((s32[1,7]{1,0:T(1,128)S(1)}, s32[1,7]{1,0:T(1,128)}, u32[]{:S(2)}) %copy-start.1) | copy-done | bytes 52
  5.3 0.2 select_reduce_fusion
  5.5 0.1 stack.67
  5.7 0.1 copy.22.refs_1_
  5.7 0.1 collective-permute-done
  5.9 1.9 %collective-permute-start.1 = (f32[48,128]{1,0:T(8,128)S(1)}, f32[48,128]{1,0:T(8,128)S(1)}, u32[]{:S(2)}, u32[]{:S(2)}) collective-permute-start(f32[48,128]{1,0:T(8,128)S(1)} %pad_maximum_fusion), channel_id=1, source_target_pairs={{0,5},{1,4},{2,7},{3,6},{4,1},{5,0},{6,3},{7,2},{8,13},{9,12},{10,... | collective-permute-start | bytes 73736 | tf_op jit(solution)/shard_map/ppermute | solution.py:281
  7.8 0.1 slice.76
  7.8 1.4 %collective-permute-done.1 = f32[48,128]{1,0:T(8,128)S(1)} collective-permute-done((f32[48,128]{1,0:T(8,128)S(1)}, f32[48,128]{1,0:T(8,128)S(1)}, u32[]{:S(2)}, u32[]{:S(2)}) %collective-permute-start.1) | collective-permute-done | bytes 24608 | tf_op jit(solution)/shard_map/ppermute | solution.py:281
  9.3 0.6 %collective-permute-start.3 = (f32[72,128]{1,0:T(8,128)S(1)}, f32[72,128]{1,0:T(8,128)S(1)}, u32[]{:S(2)}, u32[]{:S(2)}) collective-permute-start(f32[72,128]{1,0:T(8,128)S(1)} %constant_dynamic-update-slice_fusion.refs_2_.refs_3_), channel_id=1, source_target_pairs={{0,4},{4,0},{8,12},{12,8},{16,20},{20,16},{24,28},{28,24},{1,5},{5... | collective-permute-start | bytes 110600 | tf_op jit(solution)/shard_map/ppermute | solution.py:269
  9.9 1.5 %collective-permute-start.2 = (f32[72,128]{1,0:T(8,128)S(1)}, f32[72,128]{1,0:T(8,128)S(1)}, u32[]{:S(2)}, u32[]{:S(2)}) collective-permute-start(f32[72,128]{1,0:T(8,128)S(1)} %constant_dynamic-update-slice_fusion.refs_2_.refs_3_), channel_id=1, source_target_pairs={{0,12},{4,8},{8,4},{12,0},{16,28},{20,24},{24,20},{28,16},{1,13},{... | collective-permute-start | bytes 110600 | tf_op jit(solution)/shard_map/ppermute | solution.py:269
  11.4 0.1 fusion.6
  11.5 0.1 pad_maximum_fusion.2
  11.6 0.1 copy.17.par_ref
  11.7 0.2 spread.1
  11.8 0.0 collective-permute-done.3.refs_3_.refs_2_
  11.8 0.7 %shard_map.82.refs_6_ = f32[64,1152]{1,0:T(8,128)S(1)} custom-call(f32[8,128]{1,0:T(8,128)S(1)} %get-tuple-element.16.pos_ref.refs_0_, f32[8,2]{1,0:T(8,128)S(1)} %copy.22.refs_1_, f32[72,128]{1,0:T(8,128)S(1)} %constant_dynamic-update-slice_fusion.refs_2_.refs_3_, f32[72,128]{1,0:T(8,128)S(1)} %collective-permute-done.3.refs_3_.refs_2_, ...), custom_call_target="tpu_custom_call" | custom-call | flops 150994944 | bytes 1048576 | tf_op jit(solution)/shard_map/pallas_call | solution.py:199
  12.6 0.0 copy-start
  12.6 0.8 %collective-permute-done.2.refs_2_ = f32[72,128]{1,0:T(8,128)S(1)} collective-permute-done((f32[72,128]{1,0:T(8,128)S(1)}, f32[72,128]{1,0:T(8,128)S(1)}, u32[]{:S(2)}, u32[]{:S(2)}) %collective-permute-start.2) | collective-permute-done | bytes 36896 | tf_op jit(solution)/shard_map/ppermute | solution.py:269
  13.4 0.1 collective-permute-start.5
  13.5 1.5 %collective-permute-start.4 = (f32[144,128]{1,0:T(8,128)S(1)}, f32[144,128]{1,0:T(8,128)S(1)}, u32[]{:S(2)}, u32[]{:S(2)}) collective-permute-start(f32[144,128]{1,0:T(8,128)S(1)} %constant_dynamic-update-slice_fusion.5), channel_id=1, source_target_pairs={{0,20},{4,16},{8,28},{12,24},{16,4},{20,0},{24,12},{28,8},{1,21},{... | collective-permute-start | bytes 221192 | tf_op jit(solution)/shard_map/ppermute | solution.py:269
  15.0 0.0 copy-done
  15.0 0.1 constant_dynamic-slice_fusion.2
  15.1 0.7 %shard_map.83.refs_6_ = f32[64,1152]{1,0:T(8,128)S(1)} custom-call(f32[8,128]{1,0:T(8,128)S(1)} %get-tuple-element.16.pos_ref.refs_0_, f32[8,2]{1,0:T(8,128)S(1)} %copy.22.refs_1_, f32[72,128]{1,0:T(8,128)S(1)} %collective-permute-done.3.refs_3_.refs_2_, f32[72,128]{1,0:T(8,128)S(1)} %constant_dynamic-update-slice_fusion.refs_2_.refs_3_, ...), custom_call_target="tpu_custom_call" | custom-call | flops 150994944 | bytes 1048576 | tf_op jit(solution)/shard_map/pallas_call | solution.py:199
  15.8 0.0 collective-permute-done.5.refs_3_
  15.8 1.1 %shard_map.84.refs_5_ = f32[64,1152]{1,0:T(8,128)S(1)} custom-call(f32[8,128]{1,0:T(8,128)S(1)} %get-tuple-element.16.pos_ref.refs_0_, f32[8,2]{1,0:T(8,128)S(1)} %copy.22.refs_1_, f32[72,128]{1,0:T(8,128)S(1)} %collective-permute-done.2.refs_2_, f32[72,128]{1,0:T(8,128)S(1)} %collective-permute-done.5.refs_3_, ...), custom_call_target="tpu_custom_call" | custom-call | flops 301989888 | bytes 1048576 | tf_op jit(solution)/shard_map/pallas_call | solution.py:199
  16.9 0.6 %collective-permute-done.4 = f32[144,128]{1,0:T(8,128)S(1)} collective-permute-done((f32[144,128]{1,0:T(8,128)S(1)}, f32[144,128]{1,0:T(8,128)S(1)}, u32[]{:S(2)}, u32[]{:S(2)}) %collective-permute-start.4) | collective-permute-done | bytes 73760 | tf_op jit(solution)/shard_map/ppermute | solution.py:269
  17.6 0.4 %collective-permute-start.6 = (f32[72,128]{1,0:T(8,128)S(1)}, f32[72,128]{1,0:T(8,128)S(1)}, u32[]{:S(2)}, u32[]{:S(2)}) collective-permute-start(f32[72,128]{1,0:T(8,128)S(1)} %get-tuple-element.32.refs_2_), channel_id=1, source_target_pairs={{0,4},{4,0},{8,12},{12,8},{16,20},{20,16},{24,28},{28,24},{1,5},{5... | collective-permute-start | bytes 110600 | tf_op jit(solution)/shard_map/ppermute | solution.py:269
  18.0 0.1 pad_maximum_fusion.1.refs_7_
  18.1 0.7 %shard_map.85.refs_6_ = f32[64,1152]{1,0:T(8,128)S(1)} custom-call(f32[8,128]{1,0:T(8,128)S(1)} %get-tuple-element.16.pos_ref.refs_0_, f32[8,2]{1,0:T(8,128)S(1)} %copy.22.refs_1_, f32[72,128]{1,0:T(8,128)S(1)} %get-tuple-element.31.refs_2_, f32[64,128]{1,0:T(8,128)S(1)} %get-tuple-element.18.refs_4_.refs_3_, ...), custom_call_target="tpu_custom_call" | custom-call | flops 150994944 | bytes 1048576 | tf_op jit(solution)/shard_map/pallas_call | solution.py:199
  18.8 0.1 collective-permute-done.6.refs_3_
  18.8 1.9 %shard_map.86 = f32[3,16,128]{2,1,0:T(8,128)} custom-call(f32[8,128]{1,0:T(8,128)S(1)} %get-tuple-element.16.pos_ref.refs_0_, f32[8,2]{1,0:T(8,128)S(1)} %copy.22.refs_1_, f32[72,128]{1,0:T(8,128)S(1)} %get-tuple-element.32.refs_2_, f32[72,128]{1,0:T(8,128)S(1)} %collective-permute-done.6.refs_3_, f32[64,128]{1,0:T(8,128)S(1)} %get-tuple-element.18.refs_4_.refs_3_, ...), custom_call_target="tpu_custom_call" | custom-call | flops 301989888 | bytes 1048576 | tf_op jit(solution)/shard_map/pallas_call | solution.py:199
  (20 shorter events, 0.1 us)
Async XLA Ops:
  0.9 5.0 %collective-permute-start = (f32[24,128]{1,0:T(8,128)S(1)}, f32[24,128]{1,0:T(8,128)S(1)}, u32[]{:S(2)}, u32[]{:S(2)}) collective-permute-start(f32[24,128]{1,0:T(8,128)S(1)} %get-tuple-element.17), channel_id=1, source_target_pairs={{0,6},{1,7},{2,4},{3,5},{4,2},{5,3},{6,0},{7,1},{8,14},{9,15},{10,... | collective-permute-start | bytes 36872 | tf_op jit(solution)/shard_map/ppermute | solution.py:281
  4.6 0.7 %copy-start.1 = (s32[1,7]{1,0:T(1,128)S(1)}, s32[1,7]{1,0:T(1,128)}, u32[]{:S(2)}) copy-start(s32[1,7]{1,0:T(1,128)} %param.11) | copy-start | bytes 88
  5.9 3.4 %collective-permute-start.1 = (f32[48,128]{1,0:T(8,128)S(1)}, f32[48,128]{1,0:T(8,128)S(1)}, u32[]{:S(2)}, u32[]{:S(2)}) collective-permute-start(f32[48,128]{1,0:T(8,128)S(1)} %pad_maximum_fusion), channel_id=1, source_target_pairs={{0,5},{1,4},{2,7},{3,6},{4,1},{5,0},{6,3},{7,2},{8,13},{9,12},{10,... | collective-permute-start | bytes 73736 | tf_op jit(solution)/shard_map/ppermute | solution.py:281
  9.3 2.5 %collective-permute-start.3 = (f32[72,128]{1,0:T(8,128)S(1)}, f32[72,128]{1,0:T(8,128)S(1)}, u32[]{:S(2)}, u32[]{:S(2)}) collective-permute-start(f32[72,128]{1,0:T(8,128)S(1)} %constant_dynamic-update-slice_fusion.refs_2_.refs_3_), channel_id=1, source_target_pairs={{0,4},{4,0},{8,12},{12,8},{16,20},{20,16},{24,28},{28,24},{1,5},{5... | collective-permute-start | bytes 110600 | tf_op jit(solution)/shard_map/ppermute | solution.py:269
  9.9 3.5 %collective-permute-start.2 = (f32[72,128]{1,0:T(8,128)S(1)}, f32[72,128]{1,0:T(8,128)S(1)}, u32[]{:S(2)}, u32[]{:S(2)}) collective-permute-start(f32[72,128]{1,0:T(8,128)S(1)} %constant_dynamic-update-slice_fusion.refs_2_.refs_3_), channel_id=1, source_target_pairs={{0,12},{4,8},{8,4},{12,0},{16,28},{20,24},{24,20},{28,16},{1,13},{... | collective-permute-start | bytes 110600 | tf_op jit(solution)/shard_map/ppermute | solution.py:269
  12.6 2.4 %copy-start = (f32[3,64,64]{2,1,0:T(8,128)S(1)}, f32[3,64,64]{2,1,0:T(8,128)}, u32[]{:S(2)}) copy-start(f32[3,64,64]{2,1,0:T(8,128)} %param.15) | copy-start | bytes 147460
  13.4 2.5 %collective-permute-start.5 = (f32[72,128]{1,0:T(8,128)S(1)}, f32[72,128]{1,0:T(8,128)S(1)}, u32[]{:S(2)}, u32[]{:S(2)}) collective-permute-start(f32[72,128]{1,0:T(8,128)S(1)} %collective-permute-done.2.refs_2_), channel_id=1, source_target_pairs={{0,4},{4,0},{8,12},{12,8},{16,20},{20,16},{24,28},{28,24},{1,5},{5... | collective-permute-start | bytes 110600 | tf_op jit(solution)/shard_map/ppermute | solution.py:269
  13.5 4.1 %collective-permute-start.4 = (f32[144,128]{1,0:T(8,128)S(1)}, f32[144,128]{1,0:T(8,128)S(1)}, u32[]{:S(2)}, u32[]{:S(2)}) collective-permute-start(f32[144,128]{1,0:T(8,128)S(1)} %constant_dynamic-update-slice_fusion.5), channel_id=1, source_target_pairs={{0,20},{4,16},{8,28},{12,24},{16,4},{20,0},{24,12},{28,8},{1,21},{... | collective-permute-start | bytes 221192 | tf_op jit(solution)/shard_map/ppermute | solution.py:269
  17.6 1.3 %collective-permute-start.6 = (f32[72,128]{1,0:T(8,128)S(1)}, f32[72,128]{1,0:T(8,128)S(1)}, u32[]{:S(2)}, u32[]{:S(2)}) collective-permute-start(f32[72,128]{1,0:T(8,128)S(1)} %get-tuple-element.32.refs_2_), channel_id=1, source_target_pairs={{0,4},{4,0},{8,12},{12,8},{16,20},{20,16},{24,28},{28,24},{1,5},{5... | collective-permute-start | bytes 110600 | tf_op jit(solution)/shard_map/ppermute | solution.py:269

commit v9 on v7

--- a/solution.py
+++ b/solution.py
@@ -218,18 +218,20 @@
     held = feats_ref.shape[0]
     kinds, count = embed_ref.shape[0], radial_ref.shape[0]
     tile_ref[...] = jnp.zeros_like(tile_ref)
-    out_ref[held:, :] = jnp.zeros((tile, lanes), jnp.float32)
+    out_ref[held:, :] = jnp.zeros((count, lanes), jnp.float32)
     own_ref[...] = jnp.zeros_like(own_ref)
     for copy in copies:
         copy.wait()
     tile_ref[0:kinds, 0:held] = embed_ref[...]
-    columns = tile_ref[...].T
     embedded = jnp.zeros(feats_ref.shape, jnp.float32)
+    down = lax.broadcasted_iota(jnp.int32, feats_ref.shape, 0)
     for kind in range(kinds):
-        embedded = jnp.where(species_ref[...] == kind, columns[:held, kind : kind + 1], embedded)
+        across = jnp.broadcast_to(tile_ref[kind : kind + 1, :], feats_ref.shape)
+        column = jnp.take_along_axis(across, down, axis=1)
+        embedded = jnp.where(species_ref[...] == kind, column, embedded)
     out_ref[0:held, :] = feats_ref[...] * embedded
     out_ref[held : held + count, 0:held] = radial_ref[...]
-    out_ref[held + count : held + count + kinds, 0:held] = center_ref[...]
+    out_ref[held : held + kinds, held : 2 * held] = center_ref[...]
     for axis, length in enumerate((box_x, cross_width, cross_width)):
         own_ref[axis : axis + 1, :] = pos_ref[axis : axis + 1, :] * (1.0 / length)
     own_ref[3:4, :] = species_ref[...].astype(jnp.float32)
@@ -249,7 +251,7 @@
     return pl.pallas_call(
         functools.partial(pack_kernel, box_x),
         out_shape=(
-            jax.ShapeDtypeStruct((held + tile, atoms), jnp.float32),
+            jax.ShapeDtypeStruct((held + radial_weight.shape[0], atoms), jnp.float32),
             jax.ShapeDtypeStruct((8, atoms), jnp.float32),
         ),
         in_specs=[pl.BlockSpec(memory_space=pltpu.HBM)] * len(operands),
@@ -315,7 +317,11 @@
             flips = flips + [f ^ bit for f in flips]
             bit //= 2
     bundle = jnp.concatenate([block[:held] for block in blocks] + [pos], axis=0)
-    par = jnp.concatenate([block[held : held + count + kinds, :held].T for block in blocks], axis=0)
+    radial = [block[held : held + count, :held] for block in blocks]
+    centres = [block[held : held + kinds, held : 2 * held] for block in blocks]
+    par = jnp.concatenate(
+        [jnp.concatenate(pair, axis=0).T for pair in zip(radial, centres)], axis=0
+    )
     mine = lax.dynamic_slice_in_dim(mix_weight, owner * held, held, 1)
     mix = jnp.concatenate(
         [lax.dynamic_slice_in_dim(mine, (owner ^ f) * held, held, 2) for f in flips], axis=2

time: 21.1 us -> 20.9 us (level)
  waiting for transfers between devices: 3.71 us -> 3.45 us
  local copies, waits for them, and re-layouts: 1.05 us -> 1.27 us
    ppermute x2, waiting for transfers between devices: 2.01 us -> 1.72 us  [crossed(): return lax.ppermute(value, ('blk', 'chan'), pairs)]
    slice x0 -> x6, local copies, waits for them, and re-layouts: none -> 0.22 us  [the longest x3 0.22 us: shards(): centres = [block[held:held + kinds, held:2 * held] for block in blocks]]
  transfers between devices with their start and end apart: 7 -> 7, of which waited for: 5 -> 5; matrix products, arithmetic and copies ran while one was open for 3% -> 5% of each run, Pallas kernels for 15% -> 15%
where the time goes in v9:
time: 20.9 us; the launch traced here: 20.6 us
  starting transfers between devices  9.57 us (46%)
  Pallas kernels  5.85 us (28%)
  waiting for transfers between devices  3.45 us (17%)
  local copies, waits for them, and re-layouts  1.27 us (6%)
  other arithmetic  0.37 us (2%)
    ppermute x2, starting transfers between devices, crossed(): return lax.ppermute(value, ('blk', 'chan'), pairs)  5.45 us
    pallas_call x5, Pallas kernels, accumulate(): pl.pallas_call(body, out_shape=shape, in_specs=[whole] * len(operands), o...  4.79 us
    ppermute x5, starting transfers between devices, moved(): lax.ppermute(value, axis, [(i, target(i, size)) for i in range(size)])  4.12 us
    ppermute x5, waiting for transfers between devices, moved(): lax.ppermute(value, axis, [(i, target(i, size)) for i in range(size)])  1.73 us
    ppermute x2, waiting for transfers between devices, crossed(): return lax.ppermute(value, ('blk', 'chan'), pairs)  1.72 us
    pallas_call x1, Pallas kernels, pack(): pl.pallas_call(functools.partial(pack_kernel, box_x), out_shape=(jax.Shap...  0.89 us
    unnamed x10, local copies, waits for them, and re-layouts  0.68 us
  transfers between devices with their start and end apart: 7, of which 5 were waited for; matrix products, arithmetic and copies ran while one was open for 5% of the time, Pallas kernels for 15%

profile of v9, /device:TPU:0, one launch (start us, length us, event | category | flops | bytes accessed | tf_op | source)
XLA Modules:
  0.0 20.6 jit_solution(1596670844347643263)
XLA Ops:
  0.0 0.9 %pack.1 = (f32[24,128]{1,0:T(8,128)S(1)}, f32[8,128]{1,0:T(8,128)S(1)}) custom-call(f32[16,128]{1,0:T(8,128)} %refs_0_.1, s32[1,128]{1,0:T(1,128)} %bitcast.23, f32[3,128]{1,0:T(4,128)} %refs_2_.1, f32[2,16]{1,0:T(2,128)} %bitcast.21, f32[8,16]{1,0:T(8,128)} %refs_4_.1, f32[2,16]{1,0:T(2,128)} %bitcast.22), custom_call_target="tpu_custom_call" | custom-call | tf_op jit(solution)/shard_map/pack/pallas_call | solution.py:251
  0.9 3.6 %collective-permute-start = (f32[24,128]{1,0:T(8,128)S(1)}, f32[24,128]{1,0:T(8,128)S(1)}, u32[]{:S(2)}, u32[]{:S(2)}) collective-permute-start(f32[24,128]{1,0:T(8,128)S(1)} %get-tuple-element.17), channel_id=1, source_target_pairs={{0,6},{1,7},{2,4},{3,5},{4,2},{5,3},{6,0},{7,1},{8,14},{9,15},{10,... | collective-permute-start | bytes 36872 | tf_op jit(solution)/shard_map/ppermute | solution.py:280
  4.5 0.1 slice.60
  4.5 0.1 stack.31
  4.6 0.0 copy-start.1
  4.6 0.7 %copy-done.1 = s32[1,7]{1,0:T(1,128)S(1)} copy-done((s32[1,7]{1,0:T(1,128)S(1)}, s32[1,7]{1,0:T(1,128)}, u32[]{:S(2)}) %copy-start.1) | copy-done | bytes 52
  5.3 0.2 select_reduce_fusion
  5.5 0.1 copy.20.refs_1_
  5.6 0.3 %collective-permute-done = f32[24,128]{1,0:T(8,128)S(1)} collective-permute-done((f32[24,128]{1,0:T(8,128)S(1)}, f32[24,128]{1,0:T(8,128)S(1)}, u32[]{:S(2)}, u32[]{:S(2)}) %collective-permute-start) | collective-permute-done | bytes 12320 | tf_op jit(solution)/shard_map/ppermute | solution.py:280
  5.9 1.9 %collective-permute-start.1 = (f32[48,128]{1,0:T(8,128)S(1)}, f32[48,128]{1,0:T(8,128)S(1)}, u32[]{:S(2)}, u32[]{:S(2)}) collective-permute-start(f32[48,128]{1,0:T(8,128)S(1)} %pad_maximum_fusion), channel_id=1, source_target_pairs={{0,5},{1,4},{2,7},{3,6},{4,1},{5,0},{6,3},{7,2},{8,13},{9,12},{10,... | collective-permute-start | bytes 73736 | tf_op jit(solution)/shard_map/ppermute | solution.py:280
  7.8 0.1 slice.76
  7.8 1.4 %collective-permute-done.1 = f32[48,128]{1,0:T(8,128)S(1)} collective-permute-done((f32[48,128]{1,0:T(8,128)S(1)}, f32[48,128]{1,0:T(8,128)S(1)}, u32[]{:S(2)}, u32[]{:S(2)}) %collective-permute-start.1) | collective-permute-done | bytes 24608 | tf_op jit(solution)/shard_map/ppermute | solution.py:280
  9.3 0.6 %collective-permute-start.3 = (f32[72,128]{1,0:T(8,128)S(1)}, f32[72,128]{1,0:T(8,128)S(1)}, u32[]{:S(2)}, u32[]{:S(2)}) collective-permute-start(f32[72,128]{1,0:T(8,128)S(1)} %constant_dynamic-update-slice_fusion.refs_2_.refs_3_), channel_id=1, source_target_pairs={{0,4},{4,0},{8,12},{12,8},{16,20},{20,16},{24,28},{28,24},{1,5},{5... | collective-permute-start | bytes 110600 | tf_op jit(solution)/shard_map/ppermute | solution.py:268
  9.9 1.5 %collective-permute-start.2 = (f32[72,128]{1,0:T(8,128)S(1)}, f32[72,128]{1,0:T(8,128)S(1)}, u32[]{:S(2)}, u32[]{:S(2)}) collective-permute-start(f32[72,128]{1,0:T(8,128)S(1)} %constant_dynamic-update-slice_fusion.refs_2_.refs_3_), channel_id=1, source_target_pairs={{0,12},{4,8},{8,4},{12,0},{16,28},{20,24},{24,20},{28,16},{1,13},{... | collective-permute-start | bytes 110600 | tf_op jit(solution)/shard_map/ppermute | solution.py:268
  11.4 0.1 fusion.2
  11.5 0.1 pad_maximum_fusion.2
  11.6 0.1 copy.15.par_ref
  11.7 0.2 spread.1
  11.8 0.0 collective-permute-done.3.refs_3_.refs_2_
  11.8 0.6 %shard_map.82.refs_6_ = f32[64,1152]{1,0:T(8,128)S(1)} custom-call(f32[8,128]{1,0:T(8,128)S(1)} %get-tuple-element.16.pos_ref.refs_0_, f32[8,1]{1,0:T(8,128)S(1)} %copy.20.refs_1_, f32[72,128]{1,0:T(8,128)S(1)} %constant_dynamic-update-slice_fusion.refs_2_.refs_3_, f32[72,128]{1,0:T(8,128)S(1)} %collective-permute-done.3.refs_3_.refs_2_, ...), custom_call_target="tpu_custom_call" | custom-call | flops 150994944 | bytes 1048576 | tf_op jit(solution)/shard_map/pallas_call | solution.py:197
  12.5 0.0 copy-start
  12.5 0.9 %collective-permute-done.2.refs_2_ = f32[72,128]{1,0:T(8,128)S(1)} collective-permute-done((f32[72,128]{1,0:T(8,128)S(1)}, f32[72,128]{1,0:T(8,128)S(1)}, u32[]{:S(2)}, u32[]{:S(2)}) %collective-permute-start.2) | collective-permute-done | bytes 36896 | tf_op jit(solution)/shard_map/ppermute | solution.py:268
  13.4 0.1 collective-permute-start.5
  13.5 1.5 %collective-permute-start.4 = (f32[144,128]{1,0:T(8,128)S(1)}, f32[144,128]{1,0:T(8,128)S(1)}, u32[]{:S(2)}, u32[]{:S(2)}) collective-permute-start(f32[144,128]{1,0:T(8,128)S(1)} %constant_dynamic-update-slice_fusion.5), channel_id=1, source_target_pairs={{0,20},{4,16},{8,28},{12,24},{16,4},{20,0},{24,12},{28,8},{1,21},{... | collective-permute-start | bytes 221192 | tf_op jit(solution)/shard_map/ppermute | solution.py:268
  15.0 0.0 copy-done
  15.0 0.1 constant_dynamic-slice_fusion.2
  15.1 0.7 %shard_map.83.refs_6_ = f32[64,1152]{1,0:T(8,128)S(1)} custom-call(f32[8,128]{1,0:T(8,128)S(1)} %get-tuple-element.16.pos_ref.refs_0_, f32[8,1]{1,0:T(8,128)S(1)} %copy.20.refs_1_, f32[72,128]{1,0:T(8,128)S(1)} %collective-permute-done.3.refs_3_.refs_2_, f32[72,128]{1,0:T(8,128)S(1)} %constant_dynamic-update-slice_fusion.refs_2_.refs_3_, ...), custom_call_target="tpu_custom_call" | custom-call | flops 150994944 | bytes 1048576 | tf_op jit(solution)/shard_map/pallas_call | solution.py:197
  15.8 0.0 collective-permute-done.5.refs_3_
  15.8 1.0 %shard_map.84.refs_5_ = f32[64,1152]{1,0:T(8,128)S(1)} custom-call(f32[8,128]{1,0:T(8,128)S(1)} %get-tuple-element.16.pos_ref.refs_0_, f32[8,1]{1,0:T(8,128)S(1)} %copy.20.refs_1_, f32[72,128]{1,0:T(8,128)S(1)} %collective-permute-done.2.refs_2_, f32[72,128]{1,0:T(8,128)S(1)} %collective-permute-done.5.refs_3_, ...), custom_call_target="tpu_custom_call" | custom-call | flops 301989888 | bytes 1048576 | tf_op jit(solution)/shard_map/pallas_call | solution.py:197
  16.8 0.7 %collective-permute-done.4 = f32[144,128]{1,0:T(8,128)S(1)} collective-permute-done((f32[144,128]{1,0:T(8,128)S(1)}, f32[144,128]{1,0:T(8,128)S(1)}, u32[]{:S(2)}, u32[]{:S(2)}) %collective-permute-start.4) | collective-permute-done | bytes 73760 | tf_op jit(solution)/shard_map/ppermute | solution.py:268
  17.6 0.4 %collective-permute-start.6 = (f32[72,128]{1,0:T(8,128)S(1)}, f32[72,128]{1,0:T(8,128)S(1)}, u32[]{:S(2)}, u32[]{:S(2)}) collective-permute-start(f32[72,128]{1,0:T(8,128)S(1)} %get-tuple-element.32.refs_2_), channel_id=1, source_target_pairs={{0,4},{4,0},{8,12},{12,8},{16,20},{20,16},{24,28},{28,24},{1,5},{5... | collective-permute-start | bytes 110600 | tf_op jit(solution)/shard_map/ppermute | solution.py:268
  18.0 0.1 pad_maximum_fusion.1.refs_7_
  18.1 0.7 %shard_map.85.refs_6_ = f32[64,1152]{1,0:T(8,128)S(1)} custom-call(f32[8,128]{1,0:T(8,128)S(1)} %get-tuple-element.16.pos_ref.refs_0_, f32[8,1]{1,0:T(8,128)S(1)} %copy.20.refs_1_, f32[72,128]{1,0:T(8,128)S(1)} %get-tuple-element.31.refs_2_, f32[64,128]{1,0:T(8,128)S(1)} %get-tuple-element.18.refs_4_.refs_3_, ...), custom_call_target="tpu_custom_call" | custom-call | flops 150994944 | bytes 1048576 | tf_op jit(solution)/shard_map/pallas_call | solution.py:197
  18.7 0.1 collective-permute-done.6.refs_3_
  18.8 1.8 %shard_map.86 = f32[3,16,128]{2,1,0:T(8,128)} custom-call(f32[8,128]{1,0:T(8,128)S(1)} %get-tuple-element.16.pos_ref.refs_0_, f32[8,1]{1,0:T(8,128)S(1)} %copy.20.refs_1_, f32[72,128]{1,0:T(8,128)S(1)} %get-tuple-element.32.refs_2_, f32[72,128]{1,0:T(8,128)S(1)} %collective-permute-done.6.refs_3_, f32[64,128]{1,0:T(8,128)S(1)} %get-tuple-element.18.refs_4_.refs_3_, ...), custom_call_target="tpu_custom_call" | custom-call | flops 301989888 | bytes 1048576 | tf_op jit(solution)/shard_map/pallas_call | solution.py:197
  (17 shorter events, 0.1 us)
Async XLA Ops:
  0.9 5.0 %collective-permute-start = (f32[24,128]{1,0:T(8,128)S(1)}, f32[24,128]{1,0:T(8,128)S(1)}, u32[]{:S(2)}, u32[]{:S(2)}) collective-permute-start(f32[24,128]{1,0:T(8,128)S(1)} %get-tuple-element.17), channel_id=1, source_target_pairs={{0,6},{1,7},{2,4},{3,5},{4,2},{5,3},{6,0},{7,1},{8,14},{9,15},{10,... | collective-permute-start | bytes 36872 | tf_op jit(solution)/shard_map/ppermute | solution.py:280
  4.6 0.7 %copy-start.1 = (s32[1,7]{1,0:T(1,128)S(1)}, s32[1,7]{1,0:T(1,128)}, u32[]{:S(2)}) copy-start(s32[1,7]{1,0:T(1,128)} %param.11) | copy-start | bytes 88
  5.9 3.4 %collective-permute-start.1 = (f32[48,128]{1,0:T(8,128)S(1)}, f32[48,128]{1,0:T(8,128)S(1)}, u32[]{:S(2)}, u32[]{:S(2)}) collective-permute-start(f32[48,128]{1,0:T(8,128)S(1)} %pad_maximum_fusion), channel_id=1, source_target_pairs={{0,5},{1,4},{2,7},{3,6},{4,1},{5,0},{6,3},{7,2},{8,13},{9,12},{10,... | collective-permute-start | bytes 73736 | tf_op jit(solution)/shard_map/ppermute | solution.py:280
  9.3 2.5 %collective-permute-start.3 = (f32[72,128]{1,0:T(8,128)S(1)}, f32[72,128]{1,0:T(8,128)S(1)}, u32[]{:S(2)}, u32[]{:S(2)}) collective-permute-start(f32[72,128]{1,0:T(8,128)S(1)} %constant_dynamic-update-slice_fusion.refs_2_.refs_3_), channel_id=1, source_target_pairs={{0,4},{4,0},{8,12},{12,8},{16,20},{20,16},{24,28},{28,24},{1,5},{5... | collective-permute-start | bytes 110600 | tf_op jit(solution)/shard_map/ppermute | solution.py:268
  9.9 3.5 %collective-permute-start.2 = (f32[72,128]{1,0:T(8,128)S(1)}, f32[72,128]{1,0:T(8,128)S(1)}, u32[]{:S(2)}, u32[]{:S(2)}) collective-permute-start(f32[72,128]{1,0:T(8,128)S(1)} %constant_dynamic-update-slice_fusion.refs_2_.refs_3_), channel_id=1, source_target_pairs={{0,12},{4,8},{8,4},{12,0},{16,28},{20,24},{24,20},{28,16},{1,13},{... | collective-permute-start | bytes 110600 | tf_op jit(solution)/shard_map/ppermute | solution.py:268
  12.5 2.5 %copy-start = (f32[3,64,64]{2,1,0:T(8,128)S(1)}, f32[3,64,64]{2,1,0:T(8,128)}, u32[]{:S(2)}) copy-start(f32[3,64,64]{2,1,0:T(8,128)} %param.15) | copy-start | bytes 147460
  13.4 2.4 %collective-permute-start.5 = (f32[72,128]{1,0:T(8,128)S(1)}, f32[72,128]{1,0:T(8,128)S(1)}, u32[]{:S(2)}, u32[]{:S(2)}) collective-permute-start(f32[72,128]{1,0:T(8,128)S(1)} %collective-permute-done.2.refs_2_), channel_id=1, source_target_pairs={{0,4},{4,0},{8,12},{12,8},{16,20},{20,16},{24,28},{28,24},{1,5},{5... | collective-permute-start | bytes 110600 | tf_op jit(solution)/shard_map/ppermute | solution.py:268
  13.5 4.1 %collective-permute-start.4 = (f32[144,128]{1,0:T(8,128)S(1)}, f32[144,128]{1,0:T(8,128)S(1)}, u32[]{:S(2)}, u32[]{:S(2)}) collective-permute-start(f32[144,128]{1,0:T(8,128)S(1)} %constant_dynamic-update-slice_fusion.5), channel_id=1, source_target_pairs={{0,20},{4,16},{8,28},{12,24},{16,4},{20,0},{24,12},{28,8},{1,21},{... | collective-permute-start | bytes 221192 | tf_op jit(solution)/shard_map/ppermute | solution.py:268
  17.6 1.3 %collective-permute-start.6 = (f32[72,128]{1,0:T(8,128)S(1)}, f32[72,128]{1,0:T(8,128)S(1)}, u32[]{:S(2)}, u32[]{:S(2)}) collective-permute-start(f32[72,128]{1,0:T(8,128)S(1)} %get-tuple-element.32.refs_2_), channel_id=1, source_target_pairs={{0,4},{4,0},{8,12},{12,8},{16,20},{20,16},{24,28},{28,24},{1,5},{5... | collective-permute-start | bytes 110600 | tf_op jit(solution)/shard_map/ppermute | solution.py:268

commit v10 on v9

--- a/solution.py
+++ b/solution.py
@@ -51,13 +51,13 @@
     envelope = level + sixth * (
         square * (inverse * (48.0 * cut_radius * level) - 21.0 * level) - 28.0 * level
     )
-    keep = square < 1.0
+    envelope = jnp.maximum(envelope, 0.0)
     if apart is not None:
-        keep = jnp.logical_and(keep, apart)
+        envelope = jnp.where(apart, envelope, 0.0)
     twice = horner(twice_cos_terms, square)
     rest = jnp.maximum(4.0 - twice * twice, 1e-12)
     sine = rest * lax.rsqrt(rest)
-    first = jnp.where(keep, envelope, 0.0) * (sine * inverse)
+    first = envelope * (sine * inverse)
     radial = [first, twice * first]
     while len(radial) < count:
         radial.append(twice * radial[-1] - radial[-2])

time: 20.9 us -> 20.9 us (level)
  no operation moved by 1% of the time
where the time goes in v10:
time: 20.9 us; the launch traced here: 20.6 us
  starting transfers between devices  9.57 us (46%)
  Pallas kernels  5.83 us (28%)
  waiting for transfers between devices  3.48 us (17%)
  local copies, waits for them, and re-layouts  1.27 us (6%)
  other arithmetic  0.37 us (2%)
    ppermute x2, starting transfers between devices, crossed(): return lax.ppermute(value, ('blk', 'chan'), pairs)  5.45 us
    pallas_call x5, Pallas kernels, accumulate(): pl.pallas_call(body, out_shape=shape, in_specs=[whole] * len(operands), o...  4.77 us
    ppermute x5, starting transfers between devices, moved(): lax.ppermute(value, axis, [(i, target(i, size)) for i in range(size)])  4.12 us
    ppermute x5, waiting for transfers between devices, moved(): lax.ppermute(value, axis, [(i, target(i, size)) for i in range(size)])  1.75 us
    ppermute x2, waiting for transfers between devices, crossed(): return lax.ppermute(value, ('blk', 'chan'), pairs)  1.72 us
    pallas_call x1, Pallas kernels, pack(): pl.pallas_call(functools.partial(pack_kernel, box_x), out_shape=(jax.Shap...  0.89 us
    unnamed x10, local copies, waits for them, and re-layouts  0.68 us
  transfers between devices with their start and end apart: 7, of which 5 were waited for; matrix products, arithmetic and copies ran while one was open for 5% of the time, Pallas kernels for 15%

profile of v10, /device:TPU:0, one launch (start us, length us, event | category | flops | bytes accessed | tf_op | source)
XLA Modules:
  0.0 20.6 jit_solution(2745199361936848644)
XLA Ops:
  0.0 0.9 %pack.1 = (f32[24,128]{1,0:T(8,128)S(1)}, f32[8,128]{1,0:T(8,128)S(1)}) custom-call(f32[16,128]{1,0:T(8,128)} %refs_0_.1, s32[1,128]{1,0:T(1,128)} %bitcast.23, f32[3,128]{1,0:T(4,128)} %refs_2_.1, f32[2,16]{1,0:T(2,128)} %bitcast.21, f32[8,16]{1,0:T(8,128)} %refs_4_.1, f32[2,16]{1,0:T(2,128)} %bitcast.22), custom_call_target="tpu_custom_call" | custom-call | tf_op jit(solution)/shard_map/pack/pallas_call | solution.py:251
  0.9 3.6 %collective-permute-start = (f32[24,128]{1,0:T(8,128)S(1)}, f32[24,128]{1,0:T(8,128)S(1)}, u32[]{:S(2)}, u32[]{:S(2)}) collective-permute-start(f32[24,128]{1,0:T(8,128)S(1)} %get-tuple-element.17), channel_id=1, source_target_pairs={{0,6},{1,7},{2,4},{3,5},{4,2},{5,3},{6,0},{7,1},{8,14},{9,15},{10,... | collective-permute-start | bytes 36872 | tf_op jit(solution)/shard_map/ppermute | solution.py:280
  4.5 0.1 slice.60
  4.5 0.1 stack.31
  4.6 0.0 copy-start.1
  4.6 0.7 %copy-done.1 = s32[1,7]{1,0:T(1,128)S(1)} copy-done((s32[1,7]{1,0:T(1,128)S(1)}, s32[1,7]{1,0:T(1,128)}, u32[]{:S(2)}) %copy-start.1) | copy-done | bytes 52
  5.3 0.2 select_reduce_fusion
  5.5 0.1 copy.20.refs_1_
  5.6 0.3 %collective-permute-done = f32[24,128]{1,0:T(8,128)S(1)} collective-permute-done((f32[24,128]{1,0:T(8,128)S(1)}, f32[24,128]{1,0:T(8,128)S(1)}, u32[]{:S(2)}, u32[]{:S(2)}) %collective-permute-start) | collective-permute-done | bytes 12320 | tf_op jit(solution)/shard_map/ppermute | solution.py:280
  5.9 1.9 %collective-permute-start.1 = (f32[48,128]{1,0:T(8,128)S(1)}, f32[48,128]{1,0:T(8,128)S(1)}, u32[]{:S(2)}, u32[]{:S(2)}) collective-permute-start(f32[48,128]{1,0:T(8,128)S(1)} %pad_maximum_fusion), channel_id=1, source_target_pairs={{0,5},{1,4},{2,7},{3,6},{4,1},{5,0},{6,3},{7,2},{8,13},{9,12},{10,... | collective-permute-start | bytes 73736 | tf_op jit(solution)/shard_map/ppermute | solution.py:280
  7.8 0.1 slice.76
  7.8 1.4 %collective-permute-done.1 = f32[48,128]{1,0:T(8,128)S(1)} collective-permute-done((f32[48,128]{1,0:T(8,128)S(1)}, f32[48,128]{1,0:T(8,128)S(1)}, u32[]{:S(2)}, u32[]{:S(2)}) %collective-permute-start.1) | collective-permute-done | bytes 24608 | tf_op jit(solution)/shard_map/ppermute | solution.py:280
  9.3 0.6 %collective-permute-start.3 = (f32[72,128]{1,0:T(8,128)S(1)}, f32[72,128]{1,0:T(8,128)S(1)}, u32[]{:S(2)}, u32[]{:S(2)}) collective-permute-start(f32[72,128]{1,0:T(8,128)S(1)} %constant_dynamic-update-slice_fusion.refs_2_.refs_3_), channel_id=1, source_target_pairs={{0,4},{4,0},{8,12},{12,8},{16,20},{20,16},{24,28},{28,24},{1,5},{5... | collective-permute-start | bytes 110600 | tf_op jit(solution)/shard_map/ppermute | solution.py:268
  9.9 1.5 %collective-permute-start.2 = (f32[72,128]{1,0:T(8,128)S(1)}, f32[72,128]{1,0:T(8,128)S(1)}, u32[]{:S(2)}, u32[]{:S(2)}) collective-permute-start(f32[72,128]{1,0:T(8,128)S(1)} %constant_dynamic-update-slice_fusion.refs_2_.refs_3_), channel_id=1, source_target_pairs={{0,12},{4,8},{8,4},{12,0},{16,28},{20,24},{24,20},{28,16},{1,13},{... | collective-permute-start | bytes 110600 | tf_op jit(solution)/shard_map/ppermute | solution.py:268
  11.4 0.1 fusion.2
  11.5 0.1 pad_maximum_fusion.2
  11.6 0.1 copy.15.par_ref
  11.7 0.2 spread.1
  11.8 0.0 collective-permute-done.3.refs_3_.refs_2_
  11.8 0.6 %shard_map.82.refs_6_ = f32[64,1152]{1,0:T(8,128)S(1)} custom-call(f32[8,128]{1,0:T(8,128)S(1)} %get-tuple-element.16.pos_ref.refs_0_, f32[8,1]{1,0:T(8,128)S(1)} %copy.20.refs_1_, f32[72,128]{1,0:T(8,128)S(1)} %constant_dynamic-update-slice_fusion.refs_2_.refs_3_, f32[72,128]{1,0:T(8,128)S(1)} %collective-permute-done.3.refs_3_.refs_2_, ...), custom_call_target="tpu_custom_call" | custom-call | flops 150994944 | bytes 1048576 | tf_op jit(solution)/shard_map/pallas_call | solution.py:197
  12.5 0.0 copy-start
  12.5 0.9 %collective-permute-done.2.refs_2_ = f32[72,128]{1,0:T(8,128)S(1)} collective-permute-done((f32[72,128]{1,0:T(8,128)S(1)}, f32[72,128]{1,0:T(8,128)S(1)}, u32[]{:S(2)}, u32[]{:S(2)}) %collective-permute-start.2) | collective-permute-done | bytes 36896 | tf_op jit(solution)/shard_map/ppermute | solution.py:268
  13.4 0.1 collective-permute-start.5
  13.5 1.5 %collective-permute-start.4 = (f32[144,128]{1,0:T(8,128)S(1)}, f32[144,128]{1,0:T(8,128)S(1)}, u32[]{:S(2)}, u32[]{:S(2)}) collective-permute-start(f32[144,128]{1,0:T(8,128)S(1)} %constant_dynamic-update-slice_fusion.5), channel_id=1, source_target_pairs={{0,20},{4,16},{8,28},{12,24},{16,4},{20,0},{24,12},{28,8},{1,21},{... | collective-permute-start | bytes 221192 | tf_op jit(solution)/shard_map/ppermute | solution.py:268
  15.0 0.0 copy-done
  15.0 0.1 constant_dynamic-slice_fusion.2
  15.1 0.6 %shard_map.83.refs_6_ = f32[64,1152]{1,0:T(8,128)S(1)} custom-call(f32[8,128]{1,0:T(8,128)S(1)} %get-tuple-element.16.pos_ref.refs_0_, f32[8,1]{1,0:T(8,128)S(1)} %copy.20.refs_1_, f32[72,128]{1,0:T(8,128)S(1)} %collective-permute-done.3.refs_3_.refs_2_, f32[72,128]{1,0:T(8,128)S(1)} %constant_dynamic-update-slice_fusion.refs_2_.refs_3_, ...), custom_call_target="tpu_custom_call" | custom-call | flops 150994944 | bytes 1048576 | tf_op jit(solution)/shard_map/pallas_call | solution.py:197
  15.8 0.0 collective-permute-done.5.refs_3_
  15.8 1.0 %shard_map.84.refs_5_ = f32[64,1152]{1,0:T(8,128)S(1)} custom-call(f32[8,128]{1,0:T(8,128)S(1)} %get-tuple-element.16.pos_ref.refs_0_, f32[8,1]{1,0:T(8,128)S(1)} %copy.20.refs_1_, f32[72,128]{1,0:T(8,128)S(1)} %collective-permute-done.2.refs_2_, f32[72,128]{1,0:T(8,128)S(1)} %collective-permute-done.5.refs_3_, ...), custom_call_target="tpu_custom_call" | custom-call | flops 301989888 | bytes 1048576 | tf_op jit(solution)/shard_map/pallas_call | solution.py:197
  16.8 0.8 %collective-permute-done.4 = f32[144,128]{1,0:T(8,128)S(1)} collective-permute-done((f32[144,128]{1,0:T(8,128)S(1)}, f32[144,128]{1,0:T(8,128)S(1)}, u32[]{:S(2)}, u32[]{:S(2)}) %collective-permute-start.4) | collective-permute-done | bytes 73760 | tf_op jit(solution)/shard_map/ppermute | solution.py:268
  17.6 0.4 %collective-permute-start.6 = (f32[72,128]{1,0:T(8,128)S(1)}, f32[72,128]{1,0:T(8,128)S(1)}, u32[]{:S(2)}, u32[]{:S(2)}) collective-permute-start(f32[72,128]{1,0:T(8,128)S(1)} %get-tuple-element.32.refs_2_), channel_id=1, source_target_pairs={{0,4},{4,0},{8,12},{12,8},{16,20},{20,16},{24,28},{28,24},{1,5},{5... | collective-permute-start | bytes 110600 | tf_op jit(solution)/shard_map/ppermute | solution.py:268
  18.0 0.1 pad_maximum_fusion.1.refs_7_
  18.1 0.6 %shard_map.85.refs_6_ = f32[64,1152]{1,0:T(8,128)S(1)} custom-call(f32[8,128]{1,0:T(8,128)S(1)} %get-tuple-element.16.pos_ref.refs_0_, f32[8,1]{1,0:T(8,128)S(1)} %copy.20.refs_1_, f32[72,128]{1,0:T(8,128)S(1)} %get-tuple-element.31.refs_2_, f32[64,128]{1,0:T(8,128)S(1)} %get-tuple-element.18.refs_4_.refs_3_, ...), custom_call_target="tpu_custom_call" | custom-call | flops 150994944 | bytes 1048576 | tf_op jit(solution)/shard_map/pallas_call | solution.py:197
  18.7 0.1 collective-permute-done.6.refs_3_
  18.8 1.8 %shard_map.86 = f32[3,16,128]{2,1,0:T(8,128)} custom-call(f32[8,128]{1,0:T(8,128)S(1)} %get-tuple-element.16.pos_ref.refs_0_, f32[8,1]{1,0:T(8,128)S(1)} %copy.20.refs_1_, f32[72,128]{1,0:T(8,128)S(1)} %get-tuple-element.32.refs_2_, f32[72,128]{1,0:T(8,128)S(1)} %collective-permute-done.6.refs_3_, f32[64,128]{1,0:T(8,128)S(1)} %get-tuple-element.18.refs_4_.refs_3_, ...), custom_call_target="tpu_custom_call" | custom-call | flops 301989888 | bytes 1048576 | tf_op jit(solution)/shard_map/pallas_call | solution.py:197
  (17 shorter events, 0.1 us)
Async XLA Ops:
  0.9 5.0 %collective-permute-start = (f32[24,128]{1,0:T(8,128)S(1)}, f32[24,128]{1,0:T(8,128)S(1)}, u32[]{:S(2)}, u32[]{:S(2)}) collective-permute-start(f32[24,128]{1,0:T(8,128)S(1)} %get-tuple-element.17), channel_id=1, source_target_pairs={{0,6},{1,7},{2,4},{3,5},{4,2},{5,3},{6,0},{7,1},{8,14},{9,15},{10,... | collective-permute-start | bytes 36872 | tf_op jit(solution)/shard_map/ppermute | solution.py:280
  4.6 0.7 %copy-start.1 = (s32[1,7]{1,0:T(1,128)S(1)}, s32[1,7]{1,0:T(1,128)}, u32[]{:S(2)}) copy-start(s32[1,7]{1,0:T(1,128)} %param.11) | copy-start | bytes 88
  5.9 3.4 %collective-permute-start.1 = (f32[48,128]{1,0:T(8,128)S(1)}, f32[48,128]{1,0:T(8,128)S(1)}, u32[]{:S(2)}, u32[]{:S(2)}) collective-permute-start(f32[48,128]{1,0:T(8,128)S(1)} %pad_maximum_fusion), channel_id=1, source_target_pairs={{0,5},{1,4},{2,7},{3,6},{4,1},{5,0},{6,3},{7,2},{8,13},{9,12},{10,... | collective-permute-start | bytes 73736 | tf_op jit(solution)/shard_map/ppermute | solution.py:280
  9.3 2.5 %collective-permute-start.3 = (f32[72,128]{1,0:T(8,128)S(1)}, f32[72,128]{1,0:T(8,128)S(1)}, u32[]{:S(2)}, u32[]{:S(2)}) collective-permute-start(f32[72,128]{1,0:T(8,128)S(1)} %constant_dynamic-update-slice_fusion.refs_2_.refs_3_), channel_id=1, source_target_pairs={{0,4},{4,0},{8,12},{12,8},{16,20},{20,16},{24,28},{28,24},{1,5},{5... | collective-permute-start | bytes 110600 | tf_op jit(solution)/shard_map/ppermute | solution.py:268
  9.9 3.5 %collective-permute-start.2 = (f32[72,128]{1,0:T(8,128)S(1)}, f32[72,128]{1,0:T(8,128)S(1)}, u32[]{:S(2)}, u32[]{:S(2)}) collective-permute-start(f32[72,128]{1,0:T(8,128)S(1)} %constant_dynamic-update-slice_fusion.refs_2_.refs_3_), channel_id=1, source_target_pairs={{0,12},{4,8},{8,4},{12,0},{16,28},{20,24},{24,20},{28,16},{1,13},{... | collective-permute-start | bytes 110600 | tf_op jit(solution)/shard_map/ppermute | solution.py:268
  12.5 2.5 %copy-start = (f32[3,64,64]{2,1,0:T(8,128)S(1)}, f32[3,64,64]{2,1,0:T(8,128)}, u32[]{:S(2)}) copy-start(f32[3,64,64]{2,1,0:T(8,128)} %param.15) | copy-start | bytes 147460
  13.4 2.4 %collective-permute-start.5 = (f32[72,128]{1,0:T(8,128)S(1)}, f32[72,128]{1,0:T(8,128)S(1)}, u32[]{:S(2)}, u32[]{:S(2)}) collective-permute-start(f32[72,128]{1,0:T(8,128)S(1)} %collective-permute-done.2.refs_2_), channel_id=1, source_target_pairs={{0,4},{4,0},{8,12},{12,8},{16,20},{20,16},{24,28},{28,24},{1,5},{5... | collective-permute-start | bytes 110600 | tf_op jit(solution)/shard_map/ppermute | solution.py:268
  13.5 4.1 %collective-permute-start.4 = (f32[144,128]{1,0:T(8,128)S(1)}, f32[144,128]{1,0:T(8,128)S(1)}, u32[]{:S(2)}, u32[]{:S(2)}) collective-permute-start(f32[144,128]{1,0:T(8,128)S(1)} %constant_dynamic-update-slice_fusion.5), channel_id=1, source_target_pairs={{0,20},{4,16},{8,28},{12,24},{16,4},{20,0},{24,12},{28,8},{1,21},{... | collective-permute-start | bytes 221192 | tf_op jit(solution)/shard_map/ppermute | solution.py:268
  17.6 1.3 %collective-permute-start.6 = (f32[72,128]{1,0:T(8,128)S(1)}, f32[72,128]{1,0:T(8,128)S(1)}, u32[]{:S(2)}, u32[]{:S(2)}) collective-permute-start(f32[72,128]{1,0:T(8,128)S(1)} %get-tuple-element.32.refs_2_), channel_id=1, source_target_pairs={{0,4},{4,0},{8,12},{12,8},{16,20},{20,16},{24,28},{28,24},{1,5},{5... | collective-permute-start | bytes 110600 | tf_op jit(solution)/shard_map/ppermute | solution.py:268
